TPU v7x, 32 devices: a whole 2x2x4 slice. The times are simulated.
32 devices in a mesh: fsdp: 8 (over z, core), dp: 4 (over y, x).
Axes of the slice: x: 2, y: 2, z: 4, core: 2. Of those that a mesh axis runs over, the one named last changes fastest.
Arguments:
- tokens: bfloat16 [32768, 1152], P(('fsdp', 'dp')), may hold values from -6 to 6
- conditions: bfloat16 [128, 1152], P(('fsdp', 'dp')), may hold values from -6 to 6
- resolution: int32 [32], P(('fsdp', 'dp')), may hold values 0 or 1
- modulate_weight: bfloat16 [1152, 6912], P('fsdp', 'dp'), may hold values from -0.1875 to 0.1875
- modulate_bias: bfloat16 [6912], P(('fsdp', 'dp')), may hold values from -3 to 3
- attend_weight: bfloat16 [1152, 3456], P('fsdp', 'dp'), may hold values from -0.1875 to 0.1875
- forget_weight: bfloat16 [1152, 16], P('fsdp', 'dp'), may hold values from -0.1875 to 0.1875
- forget_bias: float32 [16], replicated, may hold values from 0.5 to 4.5
- conv_taps: float32 [9, 1152], replicated, may hold values from -2 to 2
- output_weight: bfloat16 [1152, 1152], P('fsdp', 'dp'), may hold values from -0.1875 to 0.1875
- expand_weight: bfloat16 [1152, 4608], P('fsdp', 'dp'), may hold values from -0.1875 to 0.1875
- expand_bias: bfloat16 [4608], P(('fsdp', 'dp')), may hold values from -3 to 3
- reduce_weight: bfloat16 [4608, 1152], P('fsdp', 'dp'), may hold values from -0.09375 to 0.09375
- cotangent: bfloat16 [32768, 1152], P(('fsdp', 'dp')), may hold values from -6 to 6
Outputs:
- block_out: bfloat16 [32768, 1152], P(('fsdp', 'dp'))
- tokens_grad: bfloat16 [32768, 1152], P(('fsdp', 'dp'))
- conditions_grad: bfloat16 [128, 1152], P(('fsdp', 'dp'))
- modulate_grad: float32 [1152, 6912], P('fsdp', 'dp')
- modbias_grad: float32 [6912], P(('fsdp', 'dp'))
- attend_grad: float32 [1152, 3456], P('fsdp', 'dp')
- forget_grad: float32 [1152, 16], P('fsdp', 'dp')
- forgetbias_grad: float32 [16], replicated
- taps_grad: float32 [9, 1152], replicated
- output_grad: float32 [1152, 1152], P('fsdp', 'dp')
- expand_grad: float32 [1152, 4608], P('fsdp', 'dp')
- expandbias_grad: float32 [4608], P(('fsdp', 'dp'))
- reduce_grad: float32 [4608, 1152], P('fsdp', 'dp')
Inputs may be any that keep to these rules, and one draw needn't show every extreme that they name: `resolution`: 1 marks a block holding one item of 32 x 32 patches, 0 a block of four items, each a square grid of half that side.
All inputs are finite; a program needn't handle non-finite values.
Results may differ from a plain program's by a relative error of at most 0.019.
The roundings to bfloat16 on the way count: a program that leaves them out, or rounds other values in their place, can miss the bound.
Values may be sent and summed in bfloat16 or wider, within the bound.
No kernel may reach another device: no remote copies, remote signals or barrier semaphores. Data moves between devices by JAX's collectives and lax.ppermute only.
A program may use at most 448 MiB of HBM per device.

v0:
```python
import jax
import jax.numpy as jnp
from jax import lax
from jax.sharding import PartitionSpec as P

GRID = 32
BLOCK_ROWS = 64


highest = lax.Precision.HIGHEST
normalizer = 16.0
ln_eps = 1e-06
rms_floor = 1.0


def forward_dot(former, latter):
    return jnp.dot(former, latter, preferred_element_type=jnp.float32)


def contract_rows(former, latter):
    return lax.dot_general(
        former, latter, (((0,), (0,)), ((), ())), preferred_element_type=jnp.float32
    )


def contract_cols(former, latter):
    return lax.dot_general(
        former, latter, (((1,), (1,)), ((), ())), preferred_element_type=jnp.float32
    )


def layer_norm(values):
    centred = values - jnp.mean(values, axis=-1, keepdims=True)
    return centred * lax.rsqrt(jnp.mean(centred * centred, axis=-1, keepdims=True) + ln_eps)


def slot_pieces(modulation, resolution):
    features = modulation.shape[1] // 6
    grouped = modulation.reshape(resolution.shape[0], 4, 6 * features)
    chosen = jnp.where(
        (resolution == 1)[:, None, None], jnp.broadcast_to(grouped[:, :1], grouped.shape), grouped
    )
    return [
        chosen[:, :, None, index_piece * features : (index_piece + 1) * features]
        for index_piece in range(6)
    ]


def front_piece(token_values, modulation, resolution):
    pieces = slot_pieces(modulation, resolution)
    features = token_values.shape[1]
    grid_tokens = token_values.reshape(resolution.shape[0], 4, -1, features)
    return (layer_norm(grid_tokens) * (1.0 + pieces[1]) + pieces[0]).reshape(-1, features)


def middle_piece(token_values, attended, modulation, resolution):
    pieces = slot_pieces(modulation, resolution)
    features = token_values.shape[1]
    grid_tokens = token_values.reshape(resolution.shape[0], 4, -1, features)
    after_attn = grid_tokens + pieces[2] * attended.reshape(grid_tokens.shape)
    normed_mid = layer_norm(after_attn) * (1.0 + pieces[4]) + pieces[3]
    return (after_attn.reshape(-1, features), normed_mid.reshape(-1, features))


def final_piece(after_attn, reduced, modulation, resolution):
    pieces = slot_pieces(modulation, resolution)
    features = after_attn.shape[1]
    shaped = after_attn.reshape(resolution.shape[0], 4, -1, features)
    return (shaped + pieces[5] * reduced.reshape(shaped.shape)).reshape(-1, features)


def linear_attention(query_rows, key_rows, value_rows, decay_log, starts):
    span_rows = query_rows.shape[1]
    heads_count = query_rows.shape[2]
    head_size = query_rows.shape[3]
    cumul_log = jnp.cumsum(decay_log, axis=1)
    scaling = head_size ** (-0.5)
    scores = jnp.einsum("ntha,nsha->nhts", query_rows, key_rows, precision=highest) * scaling
    causal = jnp.arange(span_rows)[:, None] >= jnp.arange(span_rows)[None, :]
    by_head = jnp.swapaxes(cumul_log, 1, 2)
    spread = by_head[:, :, :, None] - by_head[:, :, None, :]
    weights = jnp.where(causal, jnp.exp(jnp.where(causal, spread, 0.0)), 0.0)
    inside = jnp.einsum("nhts,nshb->nthb", scores * weights, value_rows, precision=highest)
    final_log = cumul_log[:, -1]
    tail_decay = jnp.exp(final_log[:, None, :] - cumul_log)
    contrib = jnp.einsum(
        "ncha,nchb->nhab", key_rows * tail_decay[..., None], value_rows, precision=highest
    )

    def advance(carried, inputs):
        contrib_one, last_log, start_flag = inputs
        before = carried * (1.0 - start_flag)
        updated = before * jnp.exp(last_log)[:, None, None] + contrib_one
        return (updated, before)

    initial = jnp.zeros((heads_count, head_size, head_size), jnp.float32)
    ignored, befores = lax.scan(advance, initial, (contrib, final_log, starts))
    across = (
        jnp.einsum(
            "ntha,nhab->nthb",
            query_rows * jnp.exp(cumul_log)[..., None],
            befores,
            precision=highest,
        )
        * scaling
    )
    return inside + across


def depthwise(normed, resolution, taps):
    length = normed.shape[1]
    position = jnp.arange(length, dtype=jnp.int32)[None, :]
    single = (resolution == 1)[:, None]
    row_width = jnp.where(single, GRID, GRID // 2)
    local_pos = jnp.where(single, position, position % (length // 4))
    grid_row = local_pos // row_width
    grid_col = local_pos % row_width
    total = jnp.zeros(normed.shape, jnp.float32)
    for row_step in (-1, 0, 1):
        moved = jnp.where(
            single[:, :, None],
            jnp.roll(normed, -row_step * GRID, axis=1),
            jnp.roll(normed, -row_step * (GRID // 2), axis=1),
        )
        for col_step in (-1, 0, 1):
            shifted = jnp.roll(moved, -col_step, axis=1)
            valid = (
                (grid_row + row_step >= 0)
                & (grid_row + row_step < row_width)
                & (grid_col + col_step >= 0)
                & (grid_col + col_step < row_width)
            )
            total = (
                total
                + jnp.where(valid[:, :, None], shifted, 0.0)
                * taps[(row_step + 1) * 3 + col_step + 1]
            )
    return total


def attention_piece(projected_values, gate_logit, forget_bias, conv_taps, resolution):
    row_count = projected_values.shape[0]
    features = projected_values.shape[1] // 3
    heads_count = forget_bias.shape[0]
    head_size = features // heads_count
    blocks = resolution.shape[0]
    per_block = row_count // blocks
    span_count = row_count // BLOCK_ROWS
    block_spans = per_block // BLOCK_ROWS

    def split_heads(block_part):
        return block_part.reshape(span_count, BLOCK_ROWS, heads_count, head_size)

    query_rows = split_heads(projected_values[:, :features])
    key_rows = split_heads(projected_values[:, features : 2 * features])
    value_rows = split_heads(projected_values[:, 2 * features :])
    decay_log = (jax.nn.log_sigmoid(gate_logit + forget_bias) / normalizer).reshape(
        span_count, BLOCK_ROWS, heads_count
    )
    span_index = jnp.arange(span_count, dtype=jnp.int32)
    within = span_index % block_spans
    single = jnp.repeat(resolution == 1, block_spans)
    starts = jnp.where(single, within == 0, within % (block_spans // 4) == 0).astype(jnp.float32)
    mixed_heads = linear_attention(query_rows, key_rows, value_rows, decay_log, starts).reshape(
        row_count, heads_count, head_size
    )
    normed = mixed_heads * lax.rsqrt(
        jnp.maximum(jnp.mean(mixed_heads * mixed_heads, axis=-1, keepdims=True), rms_floor)
    )
    return depthwise(normed.reshape(blocks, per_block, features), resolution, conv_taps).reshape(
        row_count, features
    )


def gelu_tanh(values):
    return jax.nn.gelu(values, approximate=True)


def on_device(
    tokens,
    conditions,
    resolution,
    modulate_weight,
    modulate_bias,
    attend_weight,
    forget_weight,
    forget_bias,
    conv_taps,
    output_weight,
    expand_weight,
    expand_bias,
    reduce_weight,
    cotangent,
):
    column_parts = (
        lax.all_gather(modulate_weight, "dp", axis=1, tiled=True),
        lax.all_gather(attend_weight, "dp", axis=1, tiled=True),
        lax.all_gather(forget_weight, "dp", axis=1, tiled=True),
        lax.all_gather(output_weight, "dp", axis=1, tiled=True),
        lax.all_gather(expand_weight, "dp", axis=1, tiled=True),
        lax.all_gather(reduce_weight, "dp", axis=1, tiled=True),
        lax.all_gather(modulate_bias, "dp", axis=0, tiled=True),
        lax.all_gather(expand_bias, "dp", axis=0, tiled=True),
    )
    whole_parts = (
        lax.all_gather(column_parts[0], "fsdp", axis=0, tiled=True),
        lax.all_gather(column_parts[1], "fsdp", axis=0, tiled=True),
        lax.all_gather(column_parts[2], "fsdp", axis=0, tiled=True),
        lax.all_gather(column_parts[3], "fsdp", axis=0, tiled=True),
        lax.all_gather(column_parts[4], "fsdp", axis=0, tiled=True),
        lax.all_gather(column_parts[5], "fsdp", axis=0, tiled=True),
        lax.all_gather(column_parts[6], "fsdp", axis=0, tiled=True),
        lax.all_gather(column_parts[7], "fsdp", axis=0, tiled=True),
    )
    (
        modulate_whole,
        attend_whole,
        forget_whole,
        output_whole,
        expand_whole,
        reduce_whole,
        modbias_whole,
        expandbias_whole,
    ) = whole_parts
    cond_values = conditions.astype(jnp.float32)
    silu_out, silu_back = jax.vjp(jax.nn.silu, cond_values)
    cond_low = silu_out.astype(jnp.bfloat16)
    modulation = forward_dot(cond_low, modulate_whole) + modbias_whole.astype(jnp.float32)
    token_values = tokens.astype(jnp.float32)
    front_out, front_back = jax.vjp(
        lambda former, latter: front_piece(former, latter, resolution), token_values, modulation
    )
    normed_in = front_out.astype(jnp.bfloat16)
    projected = forward_dot(normed_in, attend_whole).astype(jnp.bfloat16)
    gate_logit = forward_dot(normed_in, forget_whole)
    conv_out, attention_back = jax.vjp(
        lambda first_arg, second_arg, third_arg, fourth_arg: attention_piece(
            first_arg, second_arg, third_arg, fourth_arg, resolution
        ),
        projected.astype(jnp.float32),
        gate_logit,
        forget_bias,
        conv_taps,
    )
    conv_low = conv_out.astype(jnp.bfloat16)
    attended = forward_dot(conv_low, output_whole)
    middle_out, middle_back = jax.vjp(
        lambda first_arg, second_arg, third_arg: middle_piece(
            first_arg, second_arg, third_arg, resolution
        ),
        token_values,
        attended,
        modulation,
    )
    after_attn, normed_raw = middle_out
    normed_mid = normed_raw.astype(jnp.bfloat16)
    preact = forward_dot(normed_mid, expand_whole) + expandbias_whole.astype(jnp.float32)
    activated, gelu_back = jax.vjp(gelu_tanh, preact)
    hidden = activated.astype(jnp.bfloat16)
    reduced = forward_dot(hidden, reduce_whole)
    block_values, final_back = jax.vjp(
        lambda first_arg, second_arg, third_arg: final_piece(
            first_arg, second_arg, third_arg, resolution
        ),
        after_attn,
        reduced,
        modulation,
    )
    block_out = block_values.astype(jnp.bfloat16)
    back_columns = (
        lax.all_gather(modulate_weight, "dp", axis=1, tiled=True),
        lax.all_gather(attend_weight, "dp", axis=1, tiled=True),
        lax.all_gather(forget_weight, "dp", axis=1, tiled=True),
        lax.all_gather(output_weight, "dp", axis=1, tiled=True),
        lax.all_gather(expand_weight, "dp", axis=1, tiled=True),
        lax.all_gather(reduce_weight, "dp", axis=1, tiled=True),
        lax.all_gather(modulate_bias, "dp", axis=0, tiled=True),
        lax.all_gather(expand_bias, "dp", axis=0, tiled=True),
    )
    back_whole = (
        lax.all_gather(back_columns[0], "fsdp", axis=0, tiled=True),
        lax.all_gather(back_columns[1], "fsdp", axis=0, tiled=True),
        lax.all_gather(back_columns[2], "fsdp", axis=0, tiled=True),
        lax.all_gather(back_columns[3], "fsdp", axis=0, tiled=True),
        lax.all_gather(back_columns[4], "fsdp", axis=0, tiled=True),
        lax.all_gather(back_columns[5], "fsdp", axis=0, tiled=True),
        lax.all_gather(back_columns[6], "fsdp", axis=0, tiled=True),
        lax.all_gather(back_columns[7], "fsdp", axis=0, tiled=True),
    )
    modulate_again, attend_again, forget_again, output_again, expand_again, reduce_again = (
        back_whole[0],
        back_whole[1],
        back_whole[2],
        back_whole[3],
        back_whole[4],
        back_whole[5],
    )
    cotangent_values = cotangent.astype(jnp.float32)
    grad_after_out, grad_reduced_raw, grad_mod_final = final_back(cotangent_values)
    grad_reduced = grad_reduced_raw.astype(jnp.bfloat16)
    reduce_grad = contract_rows(hidden, grad_reduced)
    grad_activated = contract_cols(grad_reduced, reduce_again)
    grad_preact = gelu_back(grad_activated)[0].astype(jnp.bfloat16)
    expand_grad = contract_rows(normed_mid, grad_preact)
    expandbias_grad = jnp.sum(grad_preact.astype(jnp.float32), axis=0)
    grad_mid = contract_cols(grad_preact, expand_again)
    grad_tokens_mid, grad_attended_raw, grad_mod_mid = middle_back((grad_after_out, grad_mid))
    grad_attended = grad_attended_raw.astype(jnp.bfloat16)
    output_grad = contract_rows(conv_low, grad_attended)
    grad_conv = contract_cols(grad_attended, output_again)
    grad_projected_raw, grad_gate_raw, forgetbias_local, taps_local = attention_back(grad_conv)
    grad_projected = grad_projected_raw.astype(jnp.bfloat16)
    grad_gatelow = grad_gate_raw.astype(jnp.bfloat16)
    attend_grad = contract_rows(normed_in, grad_projected)
    forget_grad = contract_rows(normed_in, grad_gatelow)
    grad_in = contract_cols(grad_projected, attend_again) + contract_cols(
        grad_gatelow, forget_again
    )
    grad_tokens_front, grad_mod_front = front_back(grad_in)
    tokens_grad = (grad_tokens_mid + grad_tokens_front).astype(jnp.bfloat16)
    grad_modulation = (grad_mod_front + grad_mod_mid + grad_mod_final).astype(jnp.bfloat16)
    modulate_grad = contract_rows(cond_low, grad_modulation)
    modbias_grad = jnp.sum(grad_modulation.astype(jnp.float32), axis=0)
    grad_cond_low = contract_cols(grad_modulation, modulate_again)
    conditions_grad = silu_back(grad_cond_low)[0].astype(jnp.bfloat16)
    row_summed = (
        lax.psum_scatter(
            modulate_grad.astype(jnp.bfloat16), "fsdp", scatter_dimension=0, tiled=True
        ).astype(jnp.float32),
        lax.psum_scatter(
            attend_grad.astype(jnp.bfloat16), "fsdp", scatter_dimension=0, tiled=True
        ).astype(jnp.float32),
        lax.psum_scatter(
            forget_grad.astype(jnp.bfloat16), "fsdp", scatter_dimension=0, tiled=True
        ).astype(jnp.float32),
        lax.psum_scatter(
            output_grad.astype(jnp.bfloat16), "fsdp", scatter_dimension=0, tiled=True
        ).astype(jnp.float32),
        lax.psum_scatter(
            expand_grad.astype(jnp.bfloat16), "fsdp", scatter_dimension=0, tiled=True
        ).astype(jnp.float32),
        lax.psum_scatter(
            reduce_grad.astype(jnp.bfloat16), "fsdp", scatter_dimension=0, tiled=True
        ).astype(jnp.float32),
        lax.psum_scatter(
            modbias_grad.astype(jnp.bfloat16), "fsdp", scatter_dimension=0, tiled=True
        ).astype(jnp.float32),
        lax.psum_scatter(
            expandbias_grad.astype(jnp.bfloat16), "fsdp", scatter_dimension=0, tiled=True
        ).astype(jnp.float32),
    )
    owned = (
        lax.psum_scatter(
            row_summed[0].astype(jnp.bfloat16), "dp", scatter_dimension=1, tiled=True
        ).astype(jnp.float32),
        lax.psum_scatter(
            row_summed[1].astype(jnp.bfloat16), "dp", scatter_dimension=1, tiled=True
        ).astype(jnp.float32),
        lax.psum_scatter(
            row_summed[2].astype(jnp.bfloat16), "dp", scatter_dimension=1, tiled=True
        ).astype(jnp.float32),
        lax.psum_scatter(
            row_summed[3].astype(jnp.bfloat16), "dp", scatter_dimension=1, tiled=True
        ).astype(jnp.float32),
        lax.psum_scatter(
            row_summed[4].astype(jnp.bfloat16), "dp", scatter_dimension=1, tiled=True
        ).astype(jnp.float32),
        lax.psum_scatter(
            row_summed[5].astype(jnp.bfloat16), "dp", scatter_dimension=1, tiled=True
        ).astype(jnp.float32),
        lax.psum_scatter(
            row_summed[6].astype(jnp.bfloat16), "dp", scatter_dimension=0, tiled=True
        ).astype(jnp.float32),
        lax.psum_scatter(
            row_summed[7].astype(jnp.bfloat16), "dp", scatter_dimension=0, tiled=True
        ).astype(jnp.float32),
    )
    modbias_owned = owned[6]
    expandbias_owned = owned[7]
    taps_grad, forgetbias_grad = lax.psum((taps_local, forgetbias_local), ("fsdp", "dp"))
    return (
        block_out,
        tokens_grad,
        conditions_grad,
        owned[0],
        modbias_owned,
        owned[1],
        owned[2],
        forgetbias_grad,
        taps_grad,
        owned[3],
        owned[4],
        expandbias_owned,
        owned[5],
    )


def solution(mesh):
    in_specs = (
        P(("fsdp", "dp"), None),
        P(("fsdp", "dp"), None),
        P(("fsdp", "dp")),
        P("fsdp", "dp"),
        P(("fsdp", "dp")),
        P("fsdp", "dp"),
        P("fsdp", "dp"),
        P(),
        P(),
        P("fsdp", "dp"),
        P("fsdp", "dp"),
        P(("fsdp", "dp")),
        P("fsdp", "dp"),
        P(("fsdp", "dp"), None),
    )
    out_specs = (
        P(("fsdp", "dp"), None),
        P(("fsdp", "dp"), None),
        P(("fsdp", "dp"), None),
        P("fsdp", "dp"),
        P(("fsdp", "dp")),
        P("fsdp", "dp"),
        P("fsdp", "dp"),
        P(),
        P(),
        P("fsdp", "dp"),
        P("fsdp", "dp"),
        P(("fsdp", "dp")),
        P("fsdp", "dp"),
    )
    return jax.shard_map(
        on_device, mesh=mesh, in_specs=in_specs, out_specs=out_specs, check_vma=False
    )
```

profile of v0, /device:TPU:0, one launch (start us, length us, event | category | flops | bytes accessed | tf_op | source)
XLA Modules:
  0.0 1908.3 jit_solution(15103723746867306666)
XLA Ops:
  9.5 38.2 %all-gather.28.cloned.1.call-done = bf16[4,1728,144]{1,2,0:T(8,128)(2,1)} async-done(((bf16[1,1728,144]{1,2,0:T(8,128)(2,1)}), bf16[4,1728,144]{1,2,0:T(8,128)(2,1)}) %all-gather.28.cloned.1.call-update) | async-done | bytes 1990672 | tf_op jit(solution)/shard_map/all_gather | solution.py:196
  53.1 15.7 all-gather.1
  71.1 13.6 all-gather.4
  90.5 9.0 all-reduce.55
  100.0 26.0 %all-reduce.53 = (bf16[6912]{0:T(1024)(128)(2,1)S(1)}, bf16[4608]{0:T(1024)(128)(2,1)S(1)}) all-reduce(bf16[6912]{0:T(1024)(128)(2,1)S(1)} %dynamic-update-slice.1, bf16[4608]{0:T(1024)(128)(2,1)S(1)} %dynamic-update-slice.3), channel_id=1, replica_groups=mesh['fsdp'=8,'dp'=4] {'fsdp'}, use_global_device_ids=true, to_apply=%add.43 | all-reduce | flops 11520 | bytes 46080
  133.8 14.2 all-gather.3
  157.4 106.4 %all-gather.14.cloned.1.call-done = bf16[1152,6912]{1,0:T(8,128)(2,1)} async-done(((bf16[144,6912]{1,0:T(8,128)(2,1)}), bf16[1152,6912]{1,0:T(8,128)(2,1)}) %all-gather.14.cloned.1.call-update) | async-done | bytes 15925264 | tf_op jit(solution)/shard_map/all_gather | solution.py:206
  283.9 58.7 %all-gather.16.cloned.1.call-done = bf16[1152,3456]{1,0:T(8,128)(2,1)} async-done(((bf16[144,3456]{1,0:T(8,128)(2,1)}), bf16[1152,3456]{1,0:T(8,128)(2,1)}) %all-gather.16.cloned.1.call-update) | async-done | bytes 7962640 | tf_op jit(solution)/shard_map/all_gather | solution.py:207
  342.6 12.8 convolution_convert_fusion.5
  362.4 9.6 reshape.1366
  372.0 10.2 reshape.1371
  383.8 19.4 %fusion.28 = f32[16,16,72,72]{3,2,1,0:T(8,128)} fusion(f32[16,64,16,72]{3,2,1,0:T(8,128)} %reshape.1371, f32[16,64,16]{1,2,0:T(8,128)S(1)} %get-tuple-element.547, bf16[16,64,16,72]{3,2,1,0:T(8,128)(2,1)} %reshape.1366), kind=kOutput, calls=%fused_computation.66 | convolution fusion | flops 1020395520 | bytes 12451840 | tf_op jit(solution)/shard_map/jvp(ncha,nchb->nhab)/dot_general | solution.py:86
  407.9 72.6 %while.38 = (s32[]{:T(128)}, f32[16,72,72]{2,1,0:T(8,128)S(1)}, f32[16,16,72,72]{3,2,1,0:T(8,128)}, f32[16]{0:T(128)S(1)}, f32[16,16]{1,0:T(8,128)S(1)}, /*index...) while((s32[]{:T(128)}, f32[16,72,72]{2,1,0:T(8,128)S(1)}, ...), condition=%wide.region_4.5_spmd.clone, body=%wide.region_3.4_spmd.clone.sunk | while | flops 497668 | bytes 1920012 | solution.py:97
  480.5 9.6 reshape.1367
  490.1 8.3 reshape.1368
  498.7 10.5 reshape.1372
  515.1 9.4 fusion.31
  524.5 21.0 %multiply_reduce_fusion.1 = (f32[16,64,16]{1,2,0:T(8,128)S(1)}, f32[16,64,16,72]{3,1,2,0:T(8,128)}) fusion(f32[16,16,72,64]{2,3,1,0:T(8,128)} %fusion.31, f32[16,16,72,72]{3,2,1,0:T(8,128)} %get-tuple-element.752, f32[16,64,16,72]{3,2,1,0:T(8,128)} %reshape.1372, f32[16,64,16]{1,2,0:T(8,128)S(1)} %copy-done.26), kind=kOutput, calls=%fused_computation.53 | convolution fusion | flops 1025097728 | bytes 19595264 | tf_op jit(solution)/shard_map/jvp(ntha,nhab->nthb)/dot_general | solution.py:99
  545.5 13.3 copy.290
  558.9 8.5 reshape.1373
  567.3 8.5 reshape.1374
  599.9 10.6 slice_bitcast_fusion.22
  610.4 10.7 slice_bitcast_fusion.24
  646.5 22.6 %add_convert_fusion.2 = bf16[1024,1152]{1,0:T(8,128)(2,1)} fusion(f32[1,1152]{1,0:T(1,128)S(1)} %get-tuple-element.543, f32[1023,1152]{1,0:T(8,128)} %get-tuple-element.545, f32[1023,1152]{1,0:T(8,128)} %get-tuple-element.544, f32[1,1152]{1,0:T(1,128)S(1)} %get-tuple-element.542, f32[1,1152]{1,0:T(1,128)S(1)} %get-tuple-element.539, ...), kind=kLoop, calls=%fused_computation.147 | loop fusion | flops 47185920 | bytes 59033088 | tf_op jit(solution)/shard_map/convert_element_type | solution.py:245
  682.1 23.8 %multiply_convert_fusion = (bf16[1024,4608]{1,0:T(8,128)(2,1)}, f32[1024,4608]{1,0:T(8,128)}) fusion(f32[4608]{0:T(1024)S(1)} %copy-done.103, bf16[1024,1152]{1,0:T(8,128)(2,1)} %fusion.47, bf16[1152,4608]{1,0:T(8,128)(2,1)} %all-gather.22.cloned.1.call-done), kind=kOutput, calls=%fused_computation.29 | convolution fusion | flops 10918821888 | bytes 41306112 | tf_op jit(solution)/shard_map/dot_general | solution.py:17
  705.9 29.3 %fusion.146 = (bf16[4608]{0:T(1024)(128)(2,1)}, bf16[1024,4608]{1,0:T(8,128)(2,1)}) fusion(f32[1024,4608]{1,0:T(8,128)} %get-tuple-element.570, f32[4608]{0:T(1024)S(1)} %copy-done.103, bf16[1024,1152]{1,0:T(8,128)(2,1)S(1)} %copy-done.28, bf16[4608,1152]{1,0:T(8,128)(2,1)} %all-gather.26.cloned.1.call-done), kind=kOutput, calls=%fused_computation.337 | convolution fusion | flops 10975440896 | bytes 41315328 | tf_op jit(solution)/shard_map/dot_general | solution.py:27
  735.2 20.3 %multiply_reduce_fusion.15 = (f32[1024]{0:T(1024)S(1)}, f32[1024,1152]{1,0:T(8,128)}) fusion(f32[1024,1152]{1,0:T(8,128)} %copy-done.6, f32[4,1152]{1,0:T(4,128)S(1)} %copy-done.50, f32[1024]{0:T(1024)S(1)} %broadcast_multiply_fusion, bf16[1024,4608]{1,0:T(8,128)(2,1)} %get-tuple-element.489, bf16[1152,4608]{1,0:T(8,128)(2,1)} %all-gather.22.cloned.1.call-done), kind=kOutput, calls=%fused_computation.145 | convolution fusion | flops 10876353536 | bytes 29517824 | tf_op jit(solution)/shard_map/dot_general | solution.py:27
  756.2 23.6 %fusion.152 = (f32[1024]{0:T(1024)S(1)}, f32[1024,1152]{1,0:T(8,128)}, bf16[1024,1152]{1,0:T(8,128)(2,1)}, f32[1024,1152]{1,0:T(8,128)}) fusion(f32[1024]{0:T(1024)S(1)} %multiply_multiply_fusion.12, f32[1024,1152]{1,0:T(8,128)} %copy-done.6, f32[1024]{0:T(1024)S(1)} %broadcast_multiply_fusion, f32[1024]{0:T(1024)S(1)} %get-tuple-element.557, ...), kind=kOutput, calls=%fused_computation.339 | convolution fusion | flops 10883431424 | bytes 41340928 | tf_op jit(solution)/shard_map/dot_general | solution.py:17
  785.4 16.9 multiply_reduce_fusion.10
  802.5 12.3 multiply_reduce_fusion.9
  823.6 13.0 broadcast_select_fusion.3
  854.6 12.3 add_add_fusion.4
  866.9 10.3 reshape.1375
  877.2 9.7 multiply_reduce_fusion
  887.1 8.4 add_add_fusion
  898.9 23.3 %fusion.21 = f32[16,16,72,72]{3,2,1,0:T(8,128)} fusion(f32[16,64,16,72]{3,1,2,0:T(8,128)S(1)} %add_add_fusion, f32[16,64,16,72]{3,2,1,0:T(8,128)S(1)} %bitcast.349, f32[16,64,16]{1,2,0:T(8,128)S(1)} %copy-done.27), kind=kOutput, calls=%fused_computation.47 | convolution fusion | flops 1021575168 | bytes 14811136 | tf_op jit(solution)/shard_map/transpose(jvp(ntha,nhab->nthb))/dot_general | solution.py:99
  922.2 15.7 fusion.95
  938.0 21.7 %fusion.17 = f32[16,16,72,64]{2,3,1,0:T(8,128)} fusion(f32[16,64,16,72]{3,1,2,0:T(8,128)} %copy-done.4, f32[16,16,64,64]{3,2,1,0:T(8,128)} %copy-done.15, f32[16,16,64]{2,1,0:T(8,128)S(1)} %copy-done.22, pred[64,64]{1,0:T(8,128)(4,1)S(1)} %copy-done.53), kind=kOutput, calls=%fused_computation.43 | convolution fusion | flops 911212544 | bytes 13701120 | tf_op jit(solution)/shard_map/transpose(jvp(nhts,nshb->nthb))/dot_general | solution.py:83
  969.0 79.7 %while.39 = (s32[]{:T(128)}, f32[16,72,72]{2,1,0:T(8,128)S(1)}, f32[16,16,72,72]{3,2,1,0:T(8,128)}, f32[16,16]{1,0:T(8,128)S(1)}, f32[16,16,72,72]{3,2,1,0:T(8,1...) while((s32[]{:T(128)}, f32[16,72,72]{2,1,0:T(8,128)S(1)}, ...), condition=%wide.region_13.14_spmd.clone, body=%wide.region_11.13_spmd.clone.sunk | while | flops 580612 | bytes 2249456 | solution.py:97
  1048.7 17.3 fusion.14
  1066.0 20.0 %add_bitcast_fusion = f32[16,64,16,72]{3,1,2,0:T(8,128)} fusion(f32[16,16,72,64]{2,3,1,0:T(8,128)} %fusion.17, f32[16,16,72,72]{3,2,1,0:T(8,128)} %get-tuple-element.247, f32[16,64,16,72]{3,2,1,0:T(8,128)} %reshape.1371, f32[16,64,16]{1,2,0:T(8,128)S(1)} %copy-done.25), kind=kOutput, calls=%fused_computation.51 | convolution fusion | flops 1021575168 | bytes 19529728 | tf_op jit(solution)/shard_map/transpose(jvp(ncha,nchb->nhab))/dot_general | solution.py:86
  1086.0 13.2 copy.300
  1099.3 8.4 reshape.1376
  1107.8 15.0 bitcast_add_fusion.3
  1122.7 9.9 copy.305
  1132.6 8.5 reshape.1377
  1141.1 24.9 %fusion.13 = (f32[16,64,16]{1,2,0:T(8,128)S(1)}, f32[16,16,64,72]{3,2,1,0:T(8,128)}) fusion(f32[16,64,16,72]{3,2,1,0:T(8,128)} %reshape.1372, f32[16,16,72,72]{3,2,1,0:T(8,128)} %get-tuple-element.800, f32[16,64,16,72]{3,1,2,0:T(8,128)} %copy-done.4), kind=kOutput, calls=%fused_computation.36 | convolution fusion | flops 1022738432 | bytes 19529728 | tf_op jit(solution)/shard_map/transpose(jvp(ntha,nhab->nthb))/dot_general | solution.py:99
  1166.0 10.8 bitcast_add_fusion.2
  1176.8 9.9 copy.307
  1186.7 8.6 reshape.1378
  1195.2 17.1 convolution_convert_fusion.3
  1214.0 17.9 convolution_convert_fusion.2
  1233.6 18.3 convolution_convert_fusion.1
  1260.8 16.9 fusion.141
  1308.7 99.2 %reduce-scatter.30.cloned.1.call-done = bf16[144,4608]{1,0:T(8,128)(2,1)} async-done(((bf16[1152,4608]{1,0:T(8,128)(2,1)}), bf16[144,4608]{1,0:T(8,128)(2,1)}) %reduce-scatter.30.cloned.1.call-update) | async-done | bytes 1327120 | tf_op jit(solution)/shard_map/reduce_scatter | solution.py:339
  1411.7 107.4 %reduce-scatter.32.cloned.1.call-done = bf16[576,1152]{1,0:T(8,128)(2,1)} async-done(((bf16[4608,1152]{1,0:T(8,128)(2,1)}), bf16[576,1152]{1,0:T(8,128)(2,1)}) %reduce-scatter.32.cloned.1.call-update) | async-done | bytes 1327120 | tf_op jit(solution)/shard_map/reduce_scatter | solution.py:342
  1521.9 158.8 %reduce-scatter.24.cloned.1.call-done = bf16[144,6912]{1,0:T(8,128)(2,1)} async-done(((bf16[1152,6912]{1,0:T(8,128)(2,1)}), bf16[144,6912]{1,0:T(8,128)(2,1)}) %reduce-scatter.24.cloned.1.call-update) | async-done | bytes 1990672 | tf_op jit(solution)/shard_map/reduce_scatter | solution.py:327
  1688.7 39.4 %all-reduce.51 = (f32[16]{0:T(128)}, f32[9,1152]{1,0:T(8,128)}) all-reduce(f32[16]{0:T(128)S(1)} %neg.53, f32[9,1152]{1,0:T(8,128)S(1)} %pad_add_fusion.2), channel_id=1, replica_groups=mesh['fsdp'=8,'dp'=4] {'fsdp','dp'}, use_global_device_ids=true, to_apply=%region_41.42 | all-reduce | flops 10384 | bytes 83072 | tf_op jit(solution)/shard_map/psum | solution.py:380
  1737.9 27.0 %all-reduce.52 = (bf16[6912]{0:T(1024)(128)(2,1)S(1)}, bf16[4608]{0:T(1024)(128)(2,1)S(1)}) all-reduce(bf16[6912]{0:T(1024)(128)(2,1)S(1)} %get-tuple-element.490, bf16[4608]{0:T(1024)(128)(2,1)S(1)} %copy-done.120), channel_id=4, replica_groups=mesh['fsdp'=8,'dp'=4] {'fsdp'}, use_global_device_ids=true, to_apply=%region_34.35.clone | all-reduce | flops 11520 | bytes 46080
  1765.1 10.7 fusion.112
  1776.6 15.6 all-reduce.54
  1797.9 17.4 reduce-scatter.42.cloned.1.call-done
  1817.4 31.0 %reduce-scatter.44.cloned.1.call-done = bf16[288,576]{1,0:T(8,128)(2,1)} async-done(((bf16[1152,576]{1,0:T(8,128)(2,1)}), bf16[288,576]{1,0:T(8,128)(2,1)}) %reduce-scatter.44.cloned.1.call-update) | async-done | bytes 331792
  1850.7 48.3 %reduce-scatter.34.cloned.1.call-done = bf16[1728,144]{1,0:T(8,128)(2,1)} async-done(((bf16[6912,144]{1,0:T(8,128)(2,1)}), bf16[1728,144]{1,0:T(8,128)(2,1)}) %reduce-scatter.34.cloned.1.call-update) | async-done | bytes 497680
  (749 shorter events, 406.1 us)
Async XLA Ops:
  7.2 40.5 %all-gather.28.cloned.1.call-start = ((), (), s32[]{:S(2)}) async-start(), calls=%async_computation.23 | async-start | bytes 2580480 | tf_op jit(solution)/shard_map/all_gather | solution.py:196
  7.9 78.1 %all-gather.20.cloned.1.call-start = ((), (), s32[]{:S(2)}) async-start(), calls=%async_computation.14 | async-start | bytes 1658880 | tf_op jit(solution)/shard_map/all_gather | solution.py:200
  8.7 145.6 %all-gather.24.cloned.1.call-start = ((), (), s32[]{:S(2)}) async-start(), calls=%async_computation.16 | async-start | bytes 1843200 | tf_op jit(solution)/shard_map/all_gather | solution.py:201
  9.4 43.7 %copy-start.57 = (bf16[144,864]{1,0:T(8,128)(2,1)S(1)}, bf16[144,864]{1,0:T(8,128)(2,1)}, u32[]{:S(2)}) copy-start(bf16[144,864]{1,0:T(8,128)(2,1)} %param.23) | copy-start | bytes 746500
  9.4 254.4 %all-gather.14.cloned.1.call-start = ((), (), s32[]{:S(2)}) async-start(), calls=%async_computation.11 | async-start | bytes 17915904 | tf_op jit(solution)/shard_map/all_gather | solution.py:206
  53.1 289.5 %all-gather.16.cloned.1.call-start = ((), (), s32[]{:S(2)}) async-start(), calls=%async_computation.12 | async-start | bytes 8957952 | tf_op jit(solution)/shard_map/all_gather | solution.py:207
  68.8 57.8 %copy-start.140 = (bf16[144,4]{0,1:T(4,128)(2,1)S(1)}, bf16[144,4]{0,1:T(4,128)(2,1)}, u32[]{:S(2)}) copy-start(bf16[144,4]{0,1:T(4,128)(2,1)} %param.24) | copy-start | bytes 3460
  68.9 84.2 %copy-start.1 = (bf16[1024,1152]{1,0:T(8,128)(2,1)S(1)}, bf16[1024,1152]{1,0:T(8,128)(2,1)}, u32[]{:S(2)}) copy-start(bf16[1024,1152]{1,0:T(8,128)(2,1)} %param.18) | copy-start | bytes 7077892
  71.0 81.3 %copy-start.102 = (f32[9,1152]{1,0:T(8,128)S(1)}, f32[9,1152]{1,0:T(8,128)}, u32[]{:S(2)}) copy-start(f32[9,1152]{1,0:T(8,128)} %param.26) | copy-start | bytes 124420
  71.0 598.1 %all-gather.18.cloned.1.call-start = ((), (), s32[]{:S(2)}) async-start(), calls=%async_computation.13 | async-start | bytes 2985984 | tf_op jit(solution)/shard_map/all_gather | solution.py:209
  85.9 596.2 %all-gather.22.cloned.1.call-start = ((), (), s32[]{:S(2)}) async-start(), calls=%async_computation.15 | async-start | bytes 11943936 | tf_op jit(solution)/shard_map/all_gather | solution.py:210
  86.7 619.2 %all-gather.26.cloned.1.call-start = ((), (), s32[]{:S(2)}) async-start(), calls=%async_computation.17 | async-start | bytes 11943936 | tf_op jit(solution)/shard_map/all_gather | solution.py:211
  126.0 137.8 %copy-start.64 = (bf16[4,1152]{1,0:T(4,128)(2,1)S(1)}, bf16[4,1152]{1,0:T(4,128)(2,1)}, u32[]{:S(2)}) copy-start(bf16[4,1152]{1,0:T(4,128)(2,1)} %param.19) | copy-start | bytes 27652
  148.1 125.3 %copy-start.45 = (bf16[1152,16]{0,1:T(8,128)(2,1)}, bf16[1152,16]{0,1:T(8,128)(2,1)S(1)}, u32[]{:S(2)}) copy-start(bf16[1152,16]{0,1:T(8,128)(2,1)S(1)} %reshape.1406) | copy-start | bytes 110596
  152.3 362.7 %copy-start.52 = (pred[64,64]{1,0:T(8,128)(4,1)}, pred[64,64]{1,0:T(8,128)(4,1)S(1)}, u32[]{:S(2)}) copy-start(pred[64,64]{1,0:T(8,128)(4,1)S(1)} %iota_compare_fusion) | copy-start | bytes 12292
  153.4 118.8 %copy-start.58 = (f32[1024]{0:T(1024)}, f32[1024]{0:T(1024)S(1)}, u32[]{:S(2)}) copy-start(f32[1024]{0:T(1024)S(1)} %broadcast_multiply_fusion.1) | copy-start | bytes 12292
  154.2 117.3 %copy-start.96 = (f32[1024]{0:T(1024)}, f32[1024]{0:T(1024)S(1)}, u32[]{:S(2)}) copy-start(f32[1024]{0:T(1024)S(1)} %multiply_reduce_fusion.17) | copy-start | bytes 12292
  154.2 118.0 %copy-start.69 = (f32[1024]{0:T(1024)}, f32[1024]{0:T(1024)S(1)}, u32[]{:S(2)}) copy-start(f32[1024]{0:T(1024)S(1)} %fusion.126) | copy-start | bytes 12292
  156.9 1146.9 %reduce-scatter.28.cloned.1.call-start = ((), (), s32[]{:S(2)}) async-start(), calls=%async_computation.20 | async-start | bytes 2985984 | tf_op jit(solution)/shard_map/reduce_scatter | solution.py:336
  272.2 324.0 %copy-start.60 = (f32[4,1152]{1,0:T(4,128)}, f32[4,1152]{1,0:T(4,128)S(1)}, u32[]{:S(2)}) copy-start(f32[4,1152]{1,0:T(4,128)S(1)} %get-tuple-element.548) | copy-start | bytes 55300
  545.5 30.2 %copy-start.34 = (f32[16,64,16]{1,2,0:T(8,128)}, f32[16,64,16]{1,2,0:T(8,128)S(1)}, u32[]{:S(2)}) copy-start(f32[16,64,16]{1,2,0:T(8,128)S(1)} %get-tuple-element.564) | copy-start | bytes 196612
  599.1 47.1 %copy-start.39 = (f32[16,1152]{1,0:T(8,128)}, f32[16,1152]{1,0:T(8,128)S(1)}, u32[]{:S(2)}) copy-start(f32[16,1152]{1,0:T(8,128)S(1)} %get-tuple-element.527) | copy-start | bytes 221188
  599.1 47.1 %copy-start.54 = (f32[16,1152]{1,0:T(8,128)}, f32[16,1152]{1,0:T(8,128)S(1)}, u32[]{:S(2)}) copy-start(f32[16,1152]{1,0:T(8,128)S(1)} %get-tuple-element.526) | copy-start | bytes 221188
  599.9 46.4 %copy-start.32 = (f32[32,1152]{1,0:T(8,128)}, f32[32,1152]{1,0:T(8,128)S(1)}, u32[]{:S(2)}) copy-start(f32[32,1152]{1,0:T(8,128)S(1)} %get-tuple-element.519) | copy-start | bytes 442372
  646.5 22.7 %copy-start.2 = (bf16[1024,1152]{1,0:T(8,128)(2,1)S(1)}, bf16[1024,1152]{1,0:T(8,128)(2,1)}, u32[]{:S(2)}) copy-start(bf16[1024,1152]{1,0:T(8,128)(2,1)} %param.18) | copy-start | bytes 7077892
  646.5 22.7 %copy-start.47 = (f32[4,1152]{1,0:T(4,128)S(1)}, f32[4,1152]{1,0:T(4,128)}, u32[]{:S(2)}) copy-start(f32[4,1152]{1,0:T(4,128)} %get-tuple-element.553) | copy-start | bytes 55300
  677.3 78.7 %copy-start.67 = (f32[1024]{0:T(1024)}, f32[1024]{0:T(1024)S(1)}, u32[]{:S(2)}) copy-start(f32[1024]{0:T(1024)S(1)} %broadcast_multiply_fusion) | copy-start | bytes 12292
  682.1 23.8 %copy-start.28 = (bf16[1024,1152]{1,0:T(8,128)(2,1)S(1)}, bf16[1024,1152]{1,0:T(8,128)(2,1)}, u32[]{:S(2)}) copy-start(bf16[1024,1152]{1,0:T(8,128)(2,1)} %fusion.45) | copy-start | bytes 7077892
  756.1 24.3 %copy-start.11 = (bf16[1024,1152]{1,0:T(8,128)(2,1)S(1)}, bf16[1024,1152]{1,0:T(8,128)(2,1)}, u32[]{:S(2)}) copy-start(bf16[1024,1152]{1,0:T(8,128)(2,1)} %param.31) | copy-start | bytes 7077892
  756.1 24.3 %copy-start.48 = (f32[4,1152]{1,0:T(4,128)S(1)}, f32[4,1152]{1,0:T(4,128)}, u32[]{:S(2)}) copy-start(f32[4,1152]{1,0:T(4,128)} %get-tuple-element.553) | copy-start | bytes 55300
  756.1 29.1 %copy-start.42 = (f32[32,1152]{1,0:T(8,128)S(1)}, f32[32,1152]{1,0:T(8,128)}, u32[]{:S(2)}) copy-start(f32[32,1152]{1,0:T(8,128)} %get-tuple-element.518) | copy-start | bytes 442372
  756.1 29.1 %copy-start.55 = (f32[16,1152]{1,0:T(8,128)S(1)}, f32[16,1152]{1,0:T(8,128)}, u32[]{:S(2)}) copy-start(f32[16,1152]{1,0:T(8,128)} %copy-done.54) | copy-start | bytes 221188
  756.1 29.1 %copy-start.105 = (f32[1,1152]{1,0:T(1,128)S(1)}, f32[1,1152]{1,0:T(1,128)}, u32[]{:S(2)}) copy-start(f32[1,1152]{1,0:T(1,128)} %copy-done.104) | copy-start | bytes 13828
  756.1 29.1 %copy-start.107 = (f32[1,1152]{1,0:T(1,128)S(1)}, f32[1,1152]{1,0:T(1,128)}, u32[]{:S(2)}) copy-start(f32[1,1152]{1,0:T(1,128)} %copy-done.106) | copy-start | bytes 13828
  756.1 29.1 %copy-start.109 = (f32[1,1152]{1,0:T(1,128)S(1)}, f32[1,1152]{1,0:T(1,128)}, u32[]{:S(2)}) copy-start(f32[1,1152]{1,0:T(1,128)} %copy-done.108) | copy-start | bytes 13828
  756.1 29.1 %copy-start.111 = (f32[1,1152]{1,0:T(1,128)S(1)}, f32[1,1152]{1,0:T(1,128)}, u32[]{:S(2)}) copy-start(f32[1,1152]{1,0:T(1,128)} %copy-done.110) | copy-start | bytes 13828
  756.1 29.1 %copy-start.122 = (pred[1024]{0:T(1024)(128)(4,1)S(1)}, pred[1024]{0:T(1024)(128)(4,1)}, u32[]{:S(2)}) copy-start(pred[1024]{0:T(1024)(128)(4,1)} %get-tuple-element.589) | copy-start | bytes 3076
  756.2 29.1 %copy-start.128 = (pred[1024]{0:T(1024)(128)(4,1)S(1)}, pred[1024]{0:T(1024)(128)(4,1)}, u32[]{:S(2)}) copy-start(pred[1024]{0:T(1024)(128)(4,1)} %and_and_fusion.8) | copy-start | bytes 3076
  756.2 29.1 %copy-start.130 = (pred[1024]{0:T(1024)(128)(4,1)S(1)}, pred[1024]{0:T(1024)(128)(4,1)}, u32[]{:S(2)}) copy-start(pred[1024]{0:T(1024)(128)(4,1)} %get-tuple-element.582) | copy-start | bytes 3076
  756.2 29.1 %copy-start.132 = (pred[1024]{0:T(1024)(128)(4,1)S(1)}, pred[1024]{0:T(1024)(128)(4,1)}, u32[]{:S(2)}) copy-start(pred[1024]{0:T(1024)(128)(4,1)} %get-tuple-element.587) | copy-start | bytes 3076
  756.2 29.1 %copy-start.134 = (pred[1024]{0:T(1024)(128)(4,1)S(1)}, pred[1024]{0:T(1024)(128)(4,1)}, u32[]{:S(2)}) copy-start(pred[1024]{0:T(1024)(128)(4,1)} %get-tuple-element.588) | copy-start | bytes 3076
  898.9 23.4 %copy-start.22 = (f32[16,16,64]{2,1,0:T(8,128)S(1)}, f32[16,16,64]{2,1,0:T(8,128)}, u32[]{:S(2)}) copy-start(f32[16,16,64]{2,1,0:T(8,128)} %copy-done.21) | copy-start | bytes 196612
  898.9 23.3 %copy-start.53 = (pred[64,64]{1,0:T(8,128)(4,1)S(1)}, pred[64,64]{1,0:T(8,128)(4,1)}, u32[]{:S(2)}) copy-start(pred[64,64]{1,0:T(8,128)(4,1)} %copy-done.52) | copy-start | bytes 12292
  1107.7 198.3 %reduce-scatter.26.cloned.1.call-start = ((), (), s32[]{:S(2)}) async-start(), calls=%async_computation.19 | async-start | bytes 8957952 | tf_op jit(solution)/shard_map/reduce_scatter | solution.py:330
  1141.1 24.9 %copy-start.7 = (bf16[16,64,16,72]{3,2,1,0:T(8,128)(2,1)S(1)}, bf16[16,64,16,72]{3,2,1,0:T(8,128)(2,1)}, u32[]{:S(2)}) copy-start(bf16[16,64,16,72]{3,2,1,0:T(8,128)(2,1)} %reshape.1368) | copy-start | bytes 7077892
  1212.4 195.5 %reduce-scatter.30.cloned.1.call-start = ((), (), s32[]{:S(2)}) async-start(), calls=%async_computation.21 | async-start | bytes 11943936 | tf_op jit(solution)/shard_map/reduce_scatter | solution.py:339
  1231.9 287.1 %reduce-scatter.32.cloned.1.call-start = ((), (), s32[]{:S(2)}) async-start(), calls=%async_computation.22 | async-start | bytes 11943936 | tf_op jit(solution)/shard_map/reduce_scatter | solution.py:342
  1252.1 428.6 %reduce-scatter.24.cloned.1.call-start = ((), (), s32[]{:S(2)}) async-start(), calls=%async_computation.18 | async-start | bytes 17915904 | tf_op jit(solution)/shard_map/reduce_scatter | solution.py:327
  1300.7 475.1 %reduce-scatter.38.cloned.1.call-start = ((), (), s32[]{:S(2)}) async-start(), calls=%async_computation.26 | async-start | bytes 331776
  1303.8 490.3 %reduce-scatter.40.cloned.1.call-start = ((), (), s32[]{:S(2)}) async-start(), calls=%async_computation.27 | async-start | bytes 737280
  1305.9 489.9 %reduce-scatter.36.cloned.1.call-start = ((), (), s32[]{:S(2)}) async-start(), calls=%async_computation.25 | async-start | bytes 2211840
  1308.6 506.6 %reduce-scatter.42.cloned.1.call-start = ((), (), s32[]{:S(2)}) async-start(), calls=%async_computation.28 | async-start | bytes 2949120
  1411.7 436.8 %reduce-scatter.44.cloned.1.call-start = ((), (), s32[]{:S(2)}) async-start(), calls=%async_computation.29 | async-start | bytes 1843200
  1521.7 166.1 %copy-start.101 = (f32[1152]{0:T(1024)S(1)}, f32[1152]{0:T(1024)}, u32[]{:S(2)}) copy-start(f32[1152]{0:T(1024)} %get-tuple-element.423) | copy-start | bytes 13828
  1521.7 166.1 %copy-start.100 = (f32[1152]{0:T(1024)S(1)}, f32[1152]{0:T(1024)}, u32[]{:S(2)}) copy-start(f32[1152]{0:T(1024)} %get-tuple-element.426) | copy-start | bytes 13828
  1521.7 166.1 %copy-start.99 = (f32[1152]{0:T(1024)S(1)}, f32[1152]{0:T(1024)}, u32[]{:S(2)}) copy-start(f32[1152]{0:T(1024)} %get-tuple-element.425) | copy-start | bytes 13828
  1521.7 166.1 %copy-start.98 = (f32[1152]{0:T(1024)S(1)}, f32[1152]{0:T(1024)}, u32[]{:S(2)}) copy-start(f32[1152]{0:T(1024)} %get-tuple-element.424) | copy-start | bytes 13828
  1521.8 166.1 %copy-start.139 = (f32[1152]{0:T(1024)S(1)}, f32[1152]{0:T(1024)}, u32[]{:S(2)}) copy-start(f32[1152]{0:T(1024)} %get-tuple-element.418) | copy-start | bytes 13828
  1521.8 166.1 %copy-start.138 = (f32[1152]{0:T(1024)S(1)}, f32[1152]{0:T(1024)}, u32[]{:S(2)}) copy-start(f32[1152]{0:T(1024)} %get-tuple-element.422) | copy-start | bytes 13828
  1521.8 166.2 %copy-start.137 = (f32[1152]{0:T(1024)S(1)}, f32[1152]{0:T(1024)}, u32[]{:S(2)}) copy-start(f32[1152]{0:T(1024)} %get-tuple-element.421) | copy-start | bytes 13828
  1521.8 166.2 %copy-start.136 = (f32[1152]{0:T(1024)S(1)}, f32[1152]{0:T(1024)}, u32[]{:S(2)}) copy-start(f32[1152]{0:T(1024)} %get-tuple-element.420) | copy-start | bytes 13828
  1521.8 166.2 %copy-start.135 = (f32[1152]{0:T(1024)S(1)}, f32[1152]{0:T(1024)}, u32[]{:S(2)}) copy-start(f32[1152]{0:T(1024)} %get-tuple-element.419) | copy-start | bytes 13828
  1521.8 206.3 %copy-start.97 = (f32[1024]{0:T(1024)S(1)}, f32[1024]{0:T(1024)}, u32[]{:S(2)}) copy-start(f32[1024]{0:T(1024)} %copy-done.96) | copy-start | bytes 12292
  1521.8 377.3 %reduce-scatter.34.cloned.1.call-start = ((), (), s32[]{:S(2)}) async-start(), calls=%async_computation.24 | async-start | bytes 4423680
  (127 other events, 1113.3 us)
Sparse Core Ops, SparseCore 0:
  9.9 37.7 all-gather.27
  49.5 35.3 all-gather.19
  86.7 30.3 all-gather.23
  119.1 144.5 all-gather.13
  265.8 76.7 all-gather.15
  344.7 32.7 all-gather.17
  379.1 99.4 all-gather.21
  480.2 98.8 all-gather.25
  1107.8 35.9 reduce-scatter.27
  1212.5 83.8 reduce-scatter.25
  1298.8 108.9 reduce-scatter.29
  1410.0 108.9 reduce-scatter.31
  1521.5 159.0 reduce-scatter.23
  1683.4 29.0 reduce-scatter.37
  1716.0 23.5 reduce-scatter.39
  1742.4 32.4 reduce-scatter.35
  1777.8 37.3 reduce-scatter.41
  1818.0 30.3 reduce-scatter.43
  1851.8 47.2 reduce-scatter.33
where the time goes:
time: 1920 us; the launch traced here: 1910 us
  waiting for transfers between devices  668 us (35%)
  matrix products  448 us (23%)
  local copies, waits for them, and re-layouts  323 us (17%)
  other arithmetic  277 us (14%)
  blocking collectives  168 us (9%)
  between operations  23.1 us (1%)
    reduce_scatter x1, waiting for transfers between devices, on_device(): lax.psum_scatter(modulate_grad.astype(jnp.bfloat16), 'fsdp', scatter_dime...  159 us
    reduce_scatter x1, waiting for transfers between devices, on_device(): lax.psum_scatter(reduce_grad.astype(jnp.bfloat16), 'fsdp', scatter_dimens...  107 us
    all_gather x1, waiting for transfers between devices, on_device(): lax.all_gather(column_parts[0], 'fsdp', axis=0, tiled=True)  106 us
    unnamed x25, waiting for transfers between devices  99.7 us
    reduce_scatter x1, waiting for transfers between devices, on_device(): lax.psum_scatter(expand_grad.astype(jnp.bfloat16), 'fsdp', scatter_dimens...  99.2 us
    dot_general x6, matrix products, contract_cols(): lax.dot_general(former, latter, (((1,), (1,)), ((), ())), preferred_eleme...  97.9 us
    unnamed x4, blocking collectives  77.6 us
    dot_general x6, matrix products, forward_dot(): return jnp.dot(former, latter, preferred_element_type=jnp.float32)  77.3 us
  transfers between devices with their start and end apart: 19, of which 9 were waited for; matrix products, arithmetic and copies ran while one was open for 33% of the time, Pallas kernels for 0%

commit v1 on v0

v1 whole, which is shorter than its diff:
```python
import functools
import math

import jax
import jax.numpy as jnp
from jax import lax
from jax.experimental import pallas as pl
from jax.experimental.pallas import tpu as pltpu
from jax.sharding import PartitionSpec as P

GRID = 32
CHUNK = 256
LANES = 128
VMEM_BYTES = 60 * 1024 * 1024
QUARTERS = 4
COST = 0.02
Z_AT, CORE_AT, U_AT, V_AT, FLAG_AT = range(5)
normalizer = 16.0
ln_eps = 1e-06
gelu_scale = math.sqrt(2.0 / math.pi)
rms_floor = 1.0
masked_log = -1e30
highest = lax.Precision.HIGHEST


def dot_nn(former, latter, precision=None):
    return lax.dot_general(
        former, latter, (((1,), (0,)), ((), ())), precision=precision, preferred_element_type=jnp.float32
    )


def dot_nt(former, latter):
    return lax.dot_general(former, latter, (((1,), (1,)), ((), ())), preferred_element_type=jnp.float32)


def dot_tn(former, latter):
    return lax.dot_general(former, latter, (((0,), (0,)), ((), ())), preferred_element_type=jnp.float32)


def head_window(head, head_size):
    first = head * head_size
    start = first // LANES * LANES
    stop = -(-(first + head_size) // LANES) * LANES
    return start, stop - start, first - start


def lane_mask(width, offset, head_size):
    lanes = lax.broadcasted_iota(jnp.int32, (1, width), 1)
    return (lanes >= offset) & (lanes < offset + head_size)


def cell_masks(rows, side):
    position = lax.broadcasted_iota(jnp.int32, (rows, 1), 0)
    grid_col = position & (side - 1)
    grid_row = (position & (side * side - 1)) >> int(math.log2(side))
    return grid_row, grid_col


def conv_forward_tile(values, taps, side):
    rows = values.shape[0]
    grid_row, grid_col = cell_masks(rows, side)
    before = jnp.where(grid_col > 0, pltpu.roll(values, 1, 0), 0.0)
    after = jnp.where(grid_col < side - 1, pltpu.roll(values, rows - 1, 0), 0.0)
    sums = [
        before * taps[3 * step : 3 * step + 1]
        + values * taps[3 * step + 1 : 3 * step + 2]
        + after * taps[3 * step + 2 : 3 * step + 3]
        for step in range(3)
    ]
    upper = jnp.where(grid_row > 0, pltpu.roll(sums[0], side, 0), 0.0)
    lower = jnp.where(grid_row < side - 1, pltpu.roll(sums[2], rows - side, 0), 0.0)
    return sums[1] + upper + lower


def conv_backward_tile(values, grads, taps, side):
    rows = values.shape[0]
    grid_row, grid_col = cell_masks(rows, side)
    before = jnp.where(grid_col > 0, pltpu.roll(values, 1, 0), 0.0)
    after = jnp.where(grid_col < side - 1, pltpu.roll(values, rows - 1, 0), 0.0)
    grad_sums = [
        jnp.where(grid_row < side - 1, pltpu.roll(grads, rows - side, 0), 0.0),
        grads,
        jnp.where(grid_row > 0, pltpu.roll(grads, side, 0), 0.0),
    ]
    tap_rows = []
    for step in range(3):
        for shifted in (before, values, after):
            tap_rows.append(jnp.sum(grad_sums[step] * shifted, axis=0, keepdims=True))
    parts = [
        sum(grad_sums[step] * taps[3 * step + col : 3 * step + col + 1] for step in range(3))
        for col in range(3)
    ]
    result = (
        parts[1]
        + pltpu.roll(jnp.where(grid_col > 0, parts[0], 0.0), rows - 1, 0)
        + pltpu.roll(jnp.where(grid_col < side - 1, parts[2], 0.0), 1, 0)
    )
    return result, tap_rows


def decay_sums(gate, bias, chunk):
    logit = gate + bias
    decay = (jnp.minimum(logit, 0.0) - jnp.log1p(jnp.exp(-jnp.abs(logit)))) / normalizer
    row_at = lax.broadcasted_iota(jnp.int32, (chunk, chunk), 0)
    col_at = lax.broadcasted_iota(jnp.int32, (chunk, chunk), 1)
    lower = jnp.where(row_at >= col_at, 1.0, 0.0)
    return dot_nn(lower, decay, highest)


def attention_forward_kernel(
    heads, head_size, flag_ref, proj_ref, gate_ref, bias_ref, taps_ref, conv_ref, normed_ref, ratio_ref, states_ref, state
):
    chunk_at = pl.program_id(0)
    chunk = proj_ref.shape[0]
    features = heads * head_size
    single = flag_ref[0] == 1

    @pl.when(jnp.logical_or(chunk_at == 0, jnp.logical_not(single)))
    def _():
        state[...] = jnp.zeros_like(state)

    cumul = decay_sums(gate_ref[...], bias_ref[...], chunk)
    cumul_t = jnp.transpose(cumul)
    scaled = cumul + math.log(head_size ** (-0.5))
    from_start = jnp.exp(scaled)
    last = cumul[chunk - 1 : chunk, :]
    to_end = jnp.exp(last - cumul)
    whole = jnp.exp(last)
    row_at = lax.broadcasted_iota(jnp.int32, (chunk, chunk), 0)
    col_at = lax.broadcasted_iota(jnp.int32, (chunk, chunk), 1)
    causal = row_at >= col_at
    lane_at = lax.broadcasted_iota(jnp.int32, (1, LANES), 1)
    rows = pl.ds(pl.multiple_of(chunk_at * chunk, chunk), chunk)
    ratios = jnp.zeros((chunk, LANES), jnp.float32)
    for head in range(heads):
        start, width, offset = head_window(head, head_size)
        inside = lane_mask(width, offset, head_size)
        query = jnp.where(inside, proj_ref[:, start : start + width], 0)
        key = proj_ref[:, features + start : features + start + width]
        value = proj_ref[:, 2 * features + start : 2 * features + start + width]
        spread = scaled[:, head : head + 1] - cumul_t[head : head + 1, :]
        weights = jnp.exp(jnp.where(causal, spread, masked_log))
        scores = (dot_nt(query, key) * weights).astype(jnp.bfloat16)
        held = state[head, :width, :width]
        held_low = held.astype(jnp.bfloat16)
        states_ref[0, head, :width, :width] = held_low
        mixed = dot_nn(scores, value) + from_start[:, head : head + 1] * dot_nn(query, held_low)
        mixed = jnp.where(inside, mixed, 0.0)
        mean_square = jnp.sum(mixed * mixed, axis=1, keepdims=True) / head_size
        ratio = lax.rsqrt(jnp.maximum(mean_square, rms_floor))
        slope = jnp.where(mean_square > rms_floor, 1.0, jnp.where(mean_square == rms_floor, 0.5, 0.0))
        ratios = jnp.where(lane_at == head, ratio, ratios)
        ratios = jnp.where(lane_at == heads + head, slope, ratios)
        window = normed_ref[rows, start : start + width]
        normed_ref[rows, start : start + width] = jnp.where(inside, mixed * ratio, window)
        key_end = (jnp.where(inside, key, 0) * to_end[:, head : head + 1]).astype(jnp.bfloat16)
        state[head, :width, :width] = held * whole[:, head : head + 1] + dot_tn(key_end, value)
    ratio_ref[...] = ratios

    def convolve(side):
        def tile(at, carry):
            lanes = pl.ds(pl.multiple_of(at * LANES, LANES), LANES)
            conv_ref[:, lanes] = conv_forward_tile(normed_ref[:, lanes], taps_ref[:, lanes], side).astype(conv_ref.dtype)
            return carry

        lax.fori_loop(0, features // LANES, tile, 0)

    finished = chunk_at == pl.num_programs(0) - 1

    @pl.when(jnp.logical_and(finished, single))
    def _():
        convolve(GRID)

    @pl.when(jnp.logical_and(finished, jnp.logical_not(single)))
    def _():
        convolve(GRID // 2)


def attention_forward(flag, proj, gate, bias, taps, heads):
    rows = proj.shape[0]
    features = taps.shape[1]
    head_size = features // heads
    chunks = rows // CHUNK
    whole_rows = lambda at: (0, 0)
    return pl.pallas_call(
        functools.partial(attention_forward_kernel, heads, head_size),
        grid=(chunks,),
        in_specs=[
            pl.BlockSpec(memory_space=pltpu.SMEM),
            pl.BlockSpec((CHUNK, 3 * features), lambda at: (at, 0)),
            pl.BlockSpec((CHUNK, LANES), lambda at: (at, 0)),
            pl.BlockSpec((1, LANES), whole_rows),
            pl.BlockSpec((9, features), whole_rows),
        ],
        out_specs=[
            pl.BlockSpec((rows, features), whole_rows),
            pl.BlockSpec((rows, features), whole_rows),
            pl.BlockSpec((CHUNK, LANES), lambda at: (at, 0)),
            pl.BlockSpec((1, heads, 2 * LANES, 2 * LANES), lambda at: (at, 0, 0, 0)),
        ],
        out_shape=[
            jax.ShapeDtypeStruct((rows, features), jnp.bfloat16),
            jax.ShapeDtypeStruct((rows, features), jnp.float32),
            jax.ShapeDtypeStruct((rows, LANES), jnp.float32),
            jax.ShapeDtypeStruct((chunks, heads, 2 * LANES, 2 * LANES), jnp.bfloat16),
        ],
        scratch_shapes=[pltpu.VMEM((heads, 2 * LANES, 2 * LANES), jnp.float32)],
        compiler_params=pltpu.CompilerParams(vmem_limit_bytes=VMEM_BYTES),
        cost_estimate=pl.CostEstimate(flops=int(17 * 10**9 * COST), bytes_accessed=int(20 * 10**6 * COST), transcendentals=0),
        name="attention_forward",
    )(flag, proj, gate, bias, taps)


def attention_backward_kernel(
    heads,
    head_size,
    flag_ref,
    proj_ref,
    gate_ref,
    bias_ref,
    taps_ref,
    normed_ref,
    ratio_ref,
    states_ref,
    grads_ref,
    dproj_ref,
    dgate_ref,
    dbias_ref,
    dtaps_ref,
    dnormed,
    dstate,
):
    step = pl.program_id(0)
    chunks = pl.num_programs(0)
    chunk_at = chunks - 1 - step
    chunk = proj_ref.shape[0]
    features = heads * head_size
    single = flag_ref[0] == 1

    def convolve(side):
        def tile(at, carry):
            lanes = pl.ds(pl.multiple_of(at * LANES, LANES), LANES)
            result, tap_rows = conv_backward_tile(
                normed_ref[:, lanes], grads_ref[:, lanes], taps_ref[:, lanes], side
            )
            dnormed[:, lanes] = result
            for row, tap_row in enumerate(tap_rows):
                dtaps_ref[row : row + 1, lanes] = tap_row
            return carry

        lax.fori_loop(0, features // LANES, tile, 0)

    @pl.when(jnp.logical_and(step == 0, single))
    def _():
        convolve(GRID)

    @pl.when(jnp.logical_and(step == 0, jnp.logical_not(single)))
    def _():
        convolve(GRID // 2)

    @pl.when(step == 0)
    def _():
        dbias_ref[...] = jnp.zeros_like(dbias_ref)

    @pl.when(jnp.logical_or(step == 0, jnp.logical_not(single)))
    def _():
        dstate[...] = jnp.zeros_like(dstate)

    gate = gate_ref[...]
    bias = bias_ref[...]
    cumul = decay_sums(gate, bias, chunk)
    cumul_t = jnp.transpose(cumul)
    scaled = cumul + math.log(head_size ** (-0.5))
    from_start = jnp.exp(scaled)
    last = cumul[chunk - 1 : chunk, :]
    to_end = jnp.exp(last - cumul)
    whole = jnp.exp(last)
    row_at = lax.broadcasted_iota(jnp.int32, (chunk, chunk), 0)
    col_at = lax.broadcasted_iota(jnp.int32, (chunk, chunk), 1)
    causal = row_at >= col_at
    lane_at = lax.broadcasted_iota(jnp.int32, (1, LANES), 1)
    rows = pl.ds(pl.multiple_of(chunk_at * chunk, chunk), chunk)
    balance = jnp.zeros((chunk, LANES), jnp.float32)
    outgoing = jnp.zeros((chunk, LANES), jnp.float32)
    through = jnp.zeros((1, LANES), jnp.float32)
    for head in range(heads):
        start, width, offset = head_window(head, head_size)
        inside = lane_mask(width, offset, head_size)
        query = jnp.where(inside, proj_ref[:, start : start + width], 0)
        key = proj_ref[:, features + start : features + start + width]
        key_in = jnp.where(inside, key, 0)
        value = proj_ref[:, 2 * features + start : 2 * features + start + width]
        value_in = jnp.where(inside, value, 0)
        start_col = from_start[:, head : head + 1]
        end_col = to_end[:, head : head + 1]
        ratio = ratio_ref[:, head : head + 1]
        slope = ratio_ref[:, heads + head : heads + head + 1]
        normed = jnp.where(inside, normed_ref[rows, start : start + width], 0.0)
        dnorm = jnp.where(inside, dnormed[rows, start : start + width], 0.0)
        along = jnp.sum(dnorm * normed, axis=1, keepdims=True) * (slope / head_size)
        dmixed = (dnorm - normed * along) * ratio
        dmixed_start = (dmixed * start_col).astype(jnp.bfloat16)
        dmixed = dmixed.astype(jnp.bfloat16)
        spread = scaled[:, head : head + 1] - cumul_t[head : head + 1, :]
        weights = jnp.exp(jnp.where(causal, spread, masked_log))
        scores = (dot_nt(query, key) * weights).astype(jnp.bfloat16)
        dscores = (dot_nt(dmixed, value) * weights).astype(jnp.bfloat16)
        held = states_ref[0, head, :width, :width]
        dnext = dstate[head, :width, :width]
        dnext_low = dnext.astype(jnp.bfloat16)
        dquery = dot_nn(dscores, key) + dot_nt(dmixed_start, held)
        dkey_inside = dot_tn(dscores, query)
        dkey_after = end_col * dot_nt(value_in, dnext_low)
        dkey = dkey_inside + dkey_after
        dvalue = dot_tn(scores, dmixed) + end_col * dot_nn(key_in, dnext_low)
        dstate[head, :width, :width] = dnext * whole[:, head : head + 1] + dot_tn(query, dmixed_start)
        term = jnp.sum(jnp.sum(dnext * held, axis=1, keepdims=True), axis=0, keepdims=True)
        through = jnp.where(lane_at == head, term, through)
        balance_one = jnp.sum(query * dquery - key_in * dkey_inside, axis=1, keepdims=True)
        balance = jnp.where(lane_at == head, balance_one, balance)
        outgoing_one = jnp.sum(key_in * dkey_after, axis=1, keepdims=True)
        outgoing = jnp.where(lane_at == head, outgoing_one, outgoing)
        for place, grad in ((0, dquery), (1, dkey), (2, dvalue)):
            columns = slice(place * features + start, place * features + start + width)
            dproj_ref[:, columns] = jnp.where(inside, grad.astype(dproj_ref.dtype), dproj_ref[:, columns])
    upper = jnp.where(row_at <= col_at, 1.0, 0.0)
    strict = jnp.where(row_at > col_at, 1.0, 0.0)
    ddecay = dot_nn(upper, balance, highest) + dot_nn(strict, outgoing, highest) + through * whole
    dgate = ddecay / (1.0 + jnp.exp(gate + bias)) / normalizer
    dgate_ref[...] = dgate
    dbias_ref[...] += jnp.sum(dgate, axis=0, keepdims=True)


def attention_backward(flag, proj, gate, bias, taps, normed, ratios, states, grads, heads):
    rows = proj.shape[0]
    features = taps.shape[1]
    head_size = features // heads
    chunks = rows // CHUNK
    whole_rows = lambda at: (0, 0)
    back = lambda at: (chunks - 1 - at, 0)
    return pl.pallas_call(
        functools.partial(attention_backward_kernel, heads, head_size),
        grid=(chunks,),
        in_specs=[
            pl.BlockSpec(memory_space=pltpu.SMEM),
            pl.BlockSpec((CHUNK, 3 * features), back),
            pl.BlockSpec((CHUNK, LANES), back),
            pl.BlockSpec((1, LANES), whole_rows),
            pl.BlockSpec((9, features), whole_rows),
            pl.BlockSpec((rows, features), whole_rows),
            pl.BlockSpec((CHUNK, LANES), back),
            pl.BlockSpec((1, heads, 2 * LANES, 2 * LANES), lambda at: (chunks - 1 - at, 0, 0, 0)),
            pl.BlockSpec((rows, features), whole_rows),
        ],
        out_specs=[
            pl.BlockSpec((CHUNK, 3 * features), back),
            pl.BlockSpec((CHUNK, LANES), back),
            pl.BlockSpec((1, LANES), whole_rows),
            pl.BlockSpec((9, features), whole_rows),
        ],
        out_shape=[
            jax.ShapeDtypeStruct((rows, 3 * features), jnp.bfloat16),
            jax.ShapeDtypeStruct((rows, LANES), jnp.float32),
            jax.ShapeDtypeStruct((1, LANES), jnp.float32),
            jax.ShapeDtypeStruct((9, features), jnp.float32),
        ],
        scratch_shapes=[
            pltpu.VMEM((rows, features), jnp.float32),
            pltpu.VMEM((heads, 2 * LANES, 2 * LANES), jnp.float32),
        ],
        compiler_params=pltpu.CompilerParams(vmem_limit_bytes=VMEM_BYTES),
        cost_estimate=pl.CostEstimate(flops=int(38 * 10**9 * COST), bytes_accessed=int(40 * 10**6 * COST), transcendentals=0),
        name="attention_backward",
    )(flag, proj, gate, bias, taps, normed, ratios, states, grads)


def parts_of(fsdp_size, dp_size):
    return fsdp_size // 2, math.isqrt(dp_size)


def mesh_parts():
    return parts_of(lax.axis_size("fsdp"), lax.axis_size("dp"))


def send(values, move):
    chips, side = mesh_parts()
    pairs = []
    for z in range(chips):
        for core in range(2):
            for u in range(side):
                for v in range(side):
                    to_z, to_core, to_u, to_v = move(z, core, u, v)
                    pairs.append(
                        (
                            ((z * 2 + core) * side + u) * side + v,
                            ((to_z * 2 + to_core) * side + to_u) * side + to_v,
                        )
                    )
    return lax.ppermute(values, ("fsdp", "dp"), pairs)


def along_z(shift):
    chips = mesh_parts()[0]
    return lambda z, core, u, v: ((z + shift) % chips, core, u, v)


def across_core(z, core, u, v):
    return z, 1 - core, u, v


def along_first(shift):
    side = mesh_parts()[1]

    def move(z, core, u, v):
        return (z, core, (u + shift) % side, v) if core == 0 else (z, core, u, (v + shift) % side)

    return move


def along_second(shift):
    side = mesh_parts()[1]

    def move(z, core, u, v):
        return (z, core, u, (v + shift) % side) if core == 0 else (z, core, (u + shift) % side, v)

    return move


def along_dp(shift):
    side = mesh_parts()[1]

    def move(z, core, u, v):
        to = (u * side + v + shift) % (side * side)
        return z, core, to // side, to % side

    return move


def far_pieces(shard):
    chips = mesh_parts()[0]
    return [shard] + [send(shard, along_z(shift)) for shift in range(1, chips)]


def first_pieces(stack):
    side = mesh_parts()[1]
    return [stack] + [send(stack, along_first(shift)) for shift in range(1, side)]


def second_pieces(level):
    side = mesh_parts()[1]
    own = []
    for piece in level:
        own += [piece] + [send(piece, along_second(shift)) for shift in range(1, side)]
    return own


def core_pieces(own):
    return own + [send(piece, across_core) for piece in own]


def gather_shard(shard):
    return core_pieces(second_pieces(first_pieces(jnp.stack(far_pieces(shard)))))


def add_low(*values):
    total = values[0].astype(jnp.float32)
    for value in values[1:]:
        total = total + value.astype(jnp.float32)
    return total


def add_parts(parts, received):
    return [add_low(part, received[first]).astype(jnp.bfloat16) for first, part in enumerate(parts)]


def cross_sum(joint):
    return send(joint, across_core)


def first_sum(parts):
    side = mesh_parts()[1]
    received = [send(parts[shift], along_first(shift)) for shift in range(1, side)]
    return [
        add_low(parts[0][second], *[value[second] for value in received]).astype(jnp.bfloat16)
        for second in range(side)
    ]


def second_sum(level):
    chips, side = mesh_parts()
    received = [send(level[shift], along_second(shift)) for shift in range(1, side)]
    return [
        add_low(level[0][far], *[value[far] for value in received]).astype(jnp.bfloat16)
        for far in range(chips)
    ]


def far_sum(level):
    chips = mesh_parts()[0]
    received = [send(level[shift], along_z(shift)) for shift in range(1, chips)]
    return add_low(level[0], *received)


def tied(*values):
    return lax.optimization_barrier(values)


def fold_of(shape, columns):
    return columns if shape[0] % (16 * columns) == 0 else 1


def folded(values, fold):
    height = values.shape[0] // fold
    return jnp.concatenate([values[at * height : (at + 1) * height] for at in range(fold)], axis=1)


def unfolded(values, fold):
    width = values.shape[1] // fold
    return jnp.concatenate([values[:, at * width : (at + 1) * width] for at in range(fold)], axis=0)


def sum_everywhere(values):
    chips, side = mesh_parts()
    count = chips * 2 * side * side
    bit = 1
    while bit < count:

        def move(z, core, u, v, bit=bit):
            to = (((z * 2 + core) * side + u) * side + v) ^ bit
            return to // (2 * side * side), to // (side * side) % 2, to // side % side, to % side

        values = values + send(values, move)
        bit *= 2
    return values


def source_place(where, sibling, first, second, far, chips, side):
    core = 1 - where[CORE_AT] if sibling else where[CORE_AT]
    from_u = lax.rem(where[U_AT] - jnp.where(core == 0, first, second) + side, side)
    from_v = lax.rem(where[V_AT] - jnp.where(core == 0, second, first) + side, side)
    from_z = lax.rem(where[Z_AT] - far + chips, chips)
    return 2 * from_z + core, from_u * side + from_v


def weight_copies(where, pieces, target, sems, chips, side):
    copies = []
    rows = pieces[0].shape[1]
    for at, piece in enumerate(pieces):
        sibling, first, second = at // (side * side), at // side % side, at % side
        for far in range(chips):
            block, column = source_place(where, sibling, first, second, far, chips, side)
            copies.append(
                pltpu.make_async_copy(
                    piece.at[far],
                    target.at[column, pl.ds(pl.multiple_of(block * rows, 8), rows)],
                    sems.at[at * chips + far],
                )
            )
    return copies


def whole_copies(gathered, target, sems):
    rows = gathered.shape[1]
    columns = target.shape[0]
    return [
        pltpu.make_async_copy(
            gathered.at[at], target.at[at % columns, pl.ds(at // columns * rows, rows)], sems.at[at]
        )
        for at in range(gathered.shape[0])
    ]


def normalize(values):
    centred = values - jnp.mean(values, axis=1, keepdims=True)
    scale = lax.rsqrt(jnp.mean(centred * centred, axis=1, keepdims=True) + ln_eps)
    return centred * scale, scale


def normalize_back(grads, unit, scale):
    return scale * (
        grads - jnp.mean(grads, axis=1, keepdims=True) - unit * jnp.mean(grads * unit, axis=1, keepdims=True)
    )


def front_kernel(chips, side, where, tokens_ref, mod_ref, *rest):
    pieces, rest = rest[: 2 * side * side], rest[2 * side * side :]
    proj_ref, gate_ref, normed_t_ref, weight, sems = rest
    columns = side * side
    wide = proj_ref.shape[1] // columns
    narrow = weight.shape[2] - wide
    copies = weight_copies(where, pieces, weight, sems, chips, side)

    @pl.when(pl.program_id(0) == 0)
    def _():
        for copy in copies:
            copy.start()

    unit, ignored = normalize(tokens_ref[...].astype(jnp.float32))
    normed = (unit * (1.0 + mod_ref[0, 1:2, :]) + mod_ref[0, 0:1, :]).astype(jnp.bfloat16)
    normed_t_ref[...] = jnp.transpose(normed)

    @pl.when(pl.program_id(0) == 0)
    def _():
        for copy in copies:
            copy.wait()

    gate_ref[...] = jnp.zeros_like(gate_ref)
    for column in range(columns):
        product = dot_nn(normed, weight[column])
        proj_ref[:, column * wide : (column + 1) * wide] = product[:, :wide].astype(jnp.bfloat16)
        gate_ref[:, column * narrow : (column + 1) * narrow] = product[:, wide:]


def rows_spec(block, width):
    return pl.BlockSpec((block, width), lambda at, where: (at, 0))


def across_spec(height, block):
    return pl.BlockSpec((height, block), lambda at, where: (0, at))


def mod_spec(features, steps=4):
    share = steps // QUARTERS
    return pl.BlockSpec(
        (1, 8, features), lambda at, where: (jnp.where(where[FLAG_AT] == 1, 0, at // share), 0, 0)
    )


def any_specs(count):
    return [pl.BlockSpec(memory_space=pl.ANY)] * count


def shaped(shape, dtype):
    return jax.ShapeDtypeStruct(shape, dtype)


def call(kernel, where, args, grid, in_specs, out_specs, out_shape, scratch, name, flops, moved):
    return pl.pallas_call(
        kernel,
        grid_spec=pltpu.PrefetchScalarGridSpec(
            num_scalar_prefetch=1, grid=grid, in_specs=in_specs, out_specs=out_specs, scratch_shapes=scratch
        ),
        out_shape=out_shape,
        compiler_params=pltpu.CompilerParams(vmem_limit_bytes=VMEM_BYTES),
        cost_estimate=pl.CostEstimate(flops=int(flops * COST), bytes_accessed=int(moved * COST), transcendentals=0),
        name=name,
    )(where, *args)


def front_forward(where, tokens, mod, pieces, wide):
    chips, side = mesh_parts()
    rows, features = tokens.shape
    block = rows // QUARTERS
    columns = side * side
    depth, width = pieces[0].shape[1:]
    return call(
        functools.partial(front_kernel, chips, side),
        where,
        (tokens, mod, *pieces),
        (QUARTERS,),
        [rows_spec(block, features), mod_spec(features)] + any_specs(len(pieces)),
        [rows_spec(block, columns * wide), rows_spec(block, LANES), across_spec(features, block)],
        [
            shaped((rows, columns * wide), jnp.bfloat16),
            shaped((rows, LANES), jnp.float32),
            shaped((features, rows), jnp.bfloat16),
        ],
        [
            pltpu.VMEM((columns, features, width), jnp.bfloat16),
            pltpu.SemaphoreType.DMA((len(pieces) * chips,)),
        ],
        "front_forward",
        2 * rows * features * columns * width,
        20 * 10**6,
    )


def gelu_parts(values):
    inner = gelu_scale * (values + 0.044715 * values * values * values)
    bent = jnp.tanh(inner)
    half = 0.5 * (1.0 + bent)
    slope = half + 0.5 * values * (1.0 - bent * bent) * (gelu_scale * (1.0 + 3 * 0.044715 * values * values))
    return values * half, slope


def middle_kernel(chips, side, where, conv_ref, tokens_ref, cot_ref, mod_ref, bias_ref, gathered, *rest):
    (
        attended_ref,
        hidden_ref,
        slope_ref,
        hidden_t_ref,
        normed_t_ref,
        conv_t_ref,
        gradred_ref,
        weight,
        sems,
    ) = rest
    columns = side * side
    wide = hidden_ref.shape[1] // columns
    narrow = weight.shape[2] - wide
    copies = whole_copies(gathered, weight, sems)

    @pl.when(pl.program_id(0) == 0)
    def _():
        for copy in copies:
            copy.start()

    conv = conv_ref[...]
    conv_t_ref[...] = jnp.transpose(conv)
    gradred_ref[...] = (cot_ref[...].astype(jnp.float32) * mod_ref[0, 5:6, :]).astype(jnp.bfloat16)

    @pl.when(pl.program_id(0) == 0)
    def _():
        for copy in copies:
            copy.wait()

    for column in range(columns):
        attended_ref[:, column * narrow : (column + 1) * narrow] = dot_nn(conv, weight[column, :, wide:])
    after = tokens_ref[...].astype(jnp.float32) + mod_ref[0, 2:3, :] * attended_ref[...]
    unit, ignored = normalize(after)
    normed = (unit * (1.0 + mod_ref[0, 4:5, :]) + mod_ref[0, 3:4, :]).astype(jnp.bfloat16)
    normed_t_ref[...] = jnp.transpose(normed)
    for column in range(columns):
        span = slice(column * wide, (column + 1) * wide)
        preact = dot_nn(normed, weight[column, :, :wide]) + bias_ref[:, span]
        hidden, slope = gelu_parts(preact)
        low = hidden.astype(jnp.bfloat16)
        hidden_ref[:, span] = low
        slope_ref[:, span] = slope.astype(jnp.bfloat16)
        hidden_t_ref[span, :] = jnp.transpose(low)


def middle_forward(where, conv, tokens, cotangent, mod, bias, gathered, wide):
    chips, side = mesh_parts()
    rows, features = tokens.shape
    block = rows // QUARTERS
    columns = side * side
    width = gathered.shape[2]
    hidden = columns * wide
    return call(
        functools.partial(middle_kernel, chips, side),
        where,
        (conv, tokens, cotangent, mod, bias, gathered),
        (QUARTERS,),
        [
            rows_spec(block, features),
            rows_spec(block, features),
            rows_spec(block, features),
            mod_spec(features),
            pl.BlockSpec((1, hidden), lambda at, where: (0, 0)),
        ]
        + any_specs(1),
        [
            rows_spec(block, features),
            rows_spec(block, hidden),
            rows_spec(block, hidden),
            across_spec(hidden, block),
            across_spec(features, block),
            across_spec(features, block),
            rows_spec(block, features),
        ],
        [
            shaped((rows, features), jnp.float32),
            shaped((rows, hidden), jnp.bfloat16),
            shaped((rows, hidden), jnp.bfloat16),
            shaped((hidden, rows), jnp.bfloat16),
            shaped((features, rows), jnp.bfloat16),
            shaped((features, rows), jnp.bfloat16),
            shaped((rows, features), jnp.bfloat16),
        ],
        [
            pltpu.VMEM((columns, features, width), jnp.bfloat16),
            pltpu.SemaphoreType.DMA((gathered.shape[0],)),
        ],
        "middle_forward",
        2 * rows * features * columns * width,
        60 * 10**6,
    )


def middle_back_kernel(
    chips, side, where, hidden_ref, slope_ref, attended_ref, tokens_ref, cot_ref, mod_ref, *rest
):
    count = 2 * side * side
    gathered, reduce_pieces, rest = rest[0], rest[1 : 1 + count], rest[1 + count :]
    (
        out_ref,
        gradpre_ref,
        gradafter_ref,
        gradatt_ref,
        gradconv_ref,
        sums_ref,
        biassum_ref,
        weight,
        reduce_weight,
        stage,
        sems,
        reduce_sems,
    ) = rest
    columns = side * side
    hidden = hidden_ref.shape[1]
    wide = hidden // columns
    narrow = weight.shape[2] - wide
    height = reduce_pieces[0].shape[1]
    fold = reduce_pieces[0].shape[2] // narrow
    copies = whole_copies(gathered, weight, sems)

    @pl.when(pl.program_id(0) == 0)
    def _():
        biassum_ref[...] = jnp.zeros_like(biassum_ref)

        def staged(turn):
            sibling, far = turn // chips, turn % chips
            slot = turn % 2
            found = []
            for first in range(side):
                for second in range(side):
                    at = first * side + second
                    block, column = source_place(where, sibling, first, second, far, chips, side)
                    found.append(
                        pltpu.make_async_copy(
                            reduce_pieces[sibling * columns + at].at[far],
                            stage.at[slot, column],
                            reduce_sems.at[slot, at],
                        )
                    )
            return block, found

        turns = [staged(turn) for turn in range(2 * chips)]
        for copy in turns[0][1]:
            copy.start()
        for turn, (block, found) in enumerate(turns):
            if turn + 1 < len(turns):
                for copy in turns[turn + 1][1]:
                    copy.start()
            if turn == 0:
                for copy in copies:
                    copy.start()
            for copy in found:
                copy.wait()
            for at in range(fold):
                target = pl.ds(pl.multiple_of((block * fold + at) * height, 8), height)
                for column in range(columns):
                    reduce_weight[target, column * narrow : (column + 1) * narrow] = stage[
                        turn % 2, column, :, at * narrow : (at + 1) * narrow
                    ]

    cot = cot_ref[...].astype(jnp.float32)
    attended = attended_ref[...]
    after = tokens_ref[...].astype(jnp.float32) + mod_ref[0, 2:3, :] * attended
    reduced = dot_nn(hidden_ref[...], reduce_weight[...])
    sums_ref[...] = jnp.zeros_like(sums_ref)
    sums_ref[0, 3:4, :] = jnp.sum(cot * reduced, axis=0, keepdims=True)
    out_ref[...] = (after + mod_ref[0, 5:6, :] * reduced).astype(out_ref.dtype)
    gradred = (cot * mod_ref[0, 5:6, :]).astype(jnp.bfloat16)

    @pl.when(pl.program_id(0) == 0)
    def _():
        for copy in copies:
            copy.wait()

    gradmid = jnp.zeros(after.shape, jnp.float32)
    for column in range(columns):
        span = slice(column * wide, (column + 1) * wide)
        gradact = dot_nt(gradred, reduce_weight[span, :])
        gradpre = (gradact * slope_ref[:, span].astype(jnp.float32)).astype(jnp.bfloat16)
        gradpre_ref[:, span] = gradpre
        biassum_ref[:, span] += jnp.sum(gradpre.astype(jnp.float32), axis=0, keepdims=True)
        gradmid = gradmid + dot_nt(gradpre, weight[column, :, :wide])
    unit, scale = normalize(after)
    sums_ref[0, 1:2, :] = jnp.sum(gradmid, axis=0, keepdims=True)
    sums_ref[0, 2:3, :] = jnp.sum(gradmid * unit, axis=0, keepdims=True)
    gradafter = cot + normalize_back(gradmid * (1.0 + mod_ref[0, 4:5, :]), unit, scale)
    gradafter_ref[...] = gradafter
    sums_ref[0, 0:1, :] = jnp.sum(gradafter * attended, axis=0, keepdims=True)
    gradatt_ref[...] = (gradafter * mod_ref[0, 2:3, :]).astype(jnp.bfloat16)
    gradconv = jnp.zeros(after.shape, jnp.float32)
    for column in range(columns):
        gradconv = gradconv + dot_nt(
            gradatt_ref[:, column * narrow : (column + 1) * narrow], weight[column, :, wide:]
        )
    gradconv_ref[...] = gradconv


def middle_backward(where, hidden, slope, attended, tokens, cotangent, mod, gathered, reduce_pieces):
    chips, side = mesh_parts()
    rows, features = tokens.shape
    steps = QUARTERS if side * side <= 4 else 2 * QUARTERS
    block = rows // steps
    columns = side * side
    inner = hidden.shape[1]
    width = gathered.shape[2]
    depth, narrow = reduce_pieces[0].shape[1:]
    return call(
        functools.partial(middle_back_kernel, chips, side),
        where,
        (hidden, slope, attended, tokens, cotangent, mod, gathered, *reduce_pieces),
        (steps,),
        [
            rows_spec(block, inner),
            rows_spec(block, inner),
            rows_spec(block, features),
            rows_spec(block, features),
            rows_spec(block, features),
            mod_spec(features, steps),
        ]
        + any_specs(1 + len(reduce_pieces)),
        [
            rows_spec(block, features),
            rows_spec(block, inner),
            rows_spec(block, features),
            rows_spec(block, features),
            rows_spec(block, features),
            pl.BlockSpec((1, 8, features), lambda at, where: (at, 0, 0)),
            pl.BlockSpec((1, inner), lambda at, where: (0, 0)),
        ],
        [
            shaped((rows, features), jnp.bfloat16),
            shaped((rows, inner), jnp.bfloat16),
            shaped((rows, features), jnp.float32),
            shaped((rows, features), jnp.bfloat16),
            shaped((rows, features), jnp.float32),
            shaped((steps, 8, features), jnp.float32),
            shaped((1, inner), jnp.float32),
        ],
        [
            pltpu.VMEM((columns, features, width), jnp.bfloat16),
            pltpu.VMEM((inner, features), jnp.bfloat16),
            pltpu.VMEM((2, columns, depth, narrow), jnp.bfloat16),
            pltpu.SemaphoreType.DMA((gathered.shape[0],)),
            pltpu.SemaphoreType.DMA((2, columns)),
        ],
        "middle_backward",
        6 * rows * features * inner,
        80 * 10**6,
    )


def front_back_kernel(
    chips, side, where, gradproj_ref, gradgate_ref, gradafter_ref, tokens_ref, mod_ref, *rest
):
    pieces, rest = rest[: 2 * side * side], rest[2 * side * side :]
    out_ref, sums_ref, weight, both, sems = rest
    columns = side * side
    wide = gradproj_ref.shape[1] // columns
    narrow = weight.shape[2] - wide
    copies = weight_copies(where, pieces, weight, sems, chips, side)

    @pl.when(pl.program_id(0) == 0)
    def _():
        for copy in copies:
            copy.start()

    unit, scale = normalize(tokens_ref[...].astype(jnp.float32))

    @pl.when(pl.program_id(0) == 0)
    def _():
        for copy in copies:
            copy.wait()

    gradin = jnp.zeros(unit.shape, jnp.float32)
    for column in range(columns):
        both[:, :wide] = gradproj_ref[:, column * wide : (column + 1) * wide]
        both[:, wide:] = gradgate_ref[:, column * narrow : (column + 1) * narrow].astype(jnp.bfloat16)
        gradin = gradin + dot_nt(both[...], weight[column])
    sums_ref[...] = jnp.zeros_like(sums_ref)
    sums_ref[0, 0:1, :] = jnp.sum(gradin, axis=0, keepdims=True)
    sums_ref[0, 1:2, :] = jnp.sum(gradin * unit, axis=0, keepdims=True)
    out_ref[...] = (
        gradafter_ref[...] + normalize_back(gradin * (1.0 + mod_ref[0, 1:2, :]), unit, scale)
    ).astype(out_ref.dtype)


def front_backward(where, gradproj, gradgate, gradafter, tokens, mod, pieces):
    chips, side = mesh_parts()
    rows, features = tokens.shape
    block = rows // QUARTERS
    columns = side * side
    width = pieces[0].shape[2]
    return call(
        functools.partial(front_back_kernel, chips, side),
        where,
        (gradproj, gradgate, gradafter, tokens, mod, *pieces),
        (QUARTERS,),
        [
            rows_spec(block, gradproj.shape[1]),
            rows_spec(block, LANES),
            rows_spec(block, features),
            rows_spec(block, features),
            mod_spec(features),
        ]
        + any_specs(len(pieces)),
        [rows_spec(block, features), pl.BlockSpec((1, 8, features), lambda at, where: (at, 0, 0))],
        [shaped((rows, features), jnp.bfloat16), shaped((QUARTERS, 8, features), jnp.float32)],
        [
            pltpu.VMEM((columns, features, width), jnp.bfloat16),
            pltpu.VMEM((block, width), jnp.bfloat16),
            pltpu.SemaphoreType.DMA((len(pieces) * chips,)),
        ],
        "front_backward",
        2 * rows * features * columns * width,
        25 * 10**6,
    )


def target_core(where, sibling):
    return 1 - where[CORE_AT] if sibling else where[CORE_AT]


def target_block(where, sibling, far, chips):
    return 2 * lax.rem(where[Z_AT] + far, chips) + target_core(where, sibling)


def target_column(where, sibling, first, second, side):
    core = target_core(where, sibling)
    to_u = lax.rem(where[U_AT] + jnp.where(core == 0, first, second), side)
    to_v = lax.rem(where[V_AT] + jnp.where(core == 0, second, first), side)
    return to_u * side + to_v


def relative_column(where, sibling, column, side):
    core = target_core(where, sibling)
    by_u = lax.rem(column // side - where[U_AT] + side, side)
    by_v = lax.rem(column % side - where[V_AT] + side, side)
    return jnp.where(core == 0, by_u, by_v), jnp.where(core == 0, by_v, by_u)


def grads_by_column_kernel(side, depth, fars, sibling, added, where, *rest):
    lefts, rest = rest[:fars], rest[fars:]
    right_ref, rest = rest[0], rest[1:]
    received, outs = (rest[0], rest[1:]) if added else (None, rest)
    product = dot_nn(jnp.concatenate([left[...] for left in lefts], axis=0), right_ref[...])

    def store(out):
        for far in range(fars):
            value = product[far * depth : (far + 1) * depth]
            if added:
                value = value + received[0, 0, far].astype(jnp.float32)
            out[far] = value.astype(jnp.bfloat16)

    if sibling:
        store(outs[0].at[0, 0])
        return
    for first in range(side):

        @pl.when(pl.program_id(0) // side == first)
        def _(first=first):
            store(outs[first].at[0])


def grads_by_row_kernel(side, depth, fars, fold, sibling, added, extra, where, *rest):
    lefts, rest = rest[:fars], rest[fars:]
    right_ref, rest = rest[0], rest[1:]
    if extra:
        extra_ref, rest = rest[0], rest[1:]
    received, rest = (rest[0], rest[1:]) if added else (None, rest)
    outs, product, small = rest[:-2], rest[-2], rest[-1]
    if sibling:
        outs = [outs[0].at[first] for first in range(side)]
    columns = side * side
    wide = right_ref.shape[1] // columns
    width = outs[0].shape[-1]
    left = jnp.concatenate([piece[...] for piece in lefts], axis=0)
    product[...] = dot_nn(left, right_ref[...])
    if extra:
        small[...] = dot_nn(left, extra_ref[...].astype(jnp.bfloat16))
    for column in range(columns):
        by_first, by_second = relative_column(where, sibling, column, side)
        for first in range(side):

            @pl.when(by_first == first)
            def _(first=first, column=column, by_second=by_second):
                for far in range(fars):
                    height = depth // fold
                    for at in range(fold):
                        span = slice(far * depth + at * height, far * depth + (at + 1) * height)
                        lanes = slice(at * wide, (at + 1) * wide)
                        value = product[span, column * wide : (column + 1) * wide]
                        if added:
                            value = value + received[first, by_second, far, :, lanes].astype(jnp.float32)
                        outs[first][by_second, far, :, lanes] = value.astype(jnp.bfloat16)
                    if extra:
                        span = slice(far * depth, (far + 1) * depth)
                        narrow = width - wide
                        value = small[span, column * narrow : (column + 1) * narrow]
                        if added:
                            value = value + received[first, by_second, far, :, wide:].astype(jnp.float32)
                        outs[first][by_second, far, :, wide:] = value.astype(jnp.bfloat16)


def weight_grads(where, left_t, right, sibling, received=None, extra=None, narrow=0, fold=1):
    chips, side = mesh_parts()
    columns = side * side
    height, rows = left_t.shape
    depth = height // (2 * chips)
    wide = right.shape[1] // columns
    width = wide * fold + narrow
    added = received is not None
    piece = (depth // fold, width)
    flops = 2 * rows * (height // 2) * columns * width
    moved = 2 * (rows * height // 2 + rows * columns * width + height // 2 * columns * width * (2 if added else 1))

    def left_spec(far, moving):
        return pl.BlockSpec(
            (depth, rows),
            lambda at, where: (target_block(where, sibling, at if moving else far, chips), 0),
        )

    if wide % LANES == 0 and extra is None and fold == 1 and depth < 2 * LANES:
        steps = columns
        specs = [left_spec(far, False) for far in range(chips)]
        specs.append(
            pl.BlockSpec(
                (rows, wide),
                lambda at, where: (0, target_column(where, sibling, at // side, lax.rem(at, side), side)),
            )
        )
        args = [left_t] * chips + [right]
        joint = pl.BlockSpec((1, 1, chips, *piece), lambda at, where: (at // side, lax.rem(at, side), 0, 0, 0))

        def out_spec(first):
            return pl.BlockSpec(
                (1, chips, *piece), lambda at, where: (jnp.clip(at - first * side, 0, side - 1), 0, 0, 0)
            )

        kernel = functools.partial(grads_by_column_kernel, side, depth, chips, sibling, added)
        scratch = []
    else:
        moving = depth >= 2 * LANES
        fars = 1 if moving else chips
        steps = chips if moving else 1
        specs = [left_spec(far, moving) for far in range(fars)]
        specs.append(pl.BlockSpec(right.shape, lambda at, where: (0, 0)))
        args = [left_t] * fars + [right]
        if extra is not None:
            specs.append(pl.BlockSpec(extra.shape, lambda at, where: (0, 0)))
            args.append(extra)
        joint = pl.BlockSpec((side, side, fars, *piece), lambda at, where: (0, 0, at, 0, 0))

        def out_spec(first):
            return pl.BlockSpec((side, fars, *piece), lambda at, where: (0, at, 0, 0))

        kernel = functools.partial(
            grads_by_row_kernel, side, depth, fars, fold, sibling, added, extra is not None
        )
        scratch = [
            pltpu.VMEM((fars * depth, right.shape[1]), jnp.float32),
            pltpu.VMEM((fars * depth, LANES), jnp.float32),
        ]
    if added:
        specs.append(joint)
        args.append(received)
    if sibling:
        outs, arrays = [joint], [shaped((side, side, chips, *piece), jnp.bfloat16)]
    else:
        outs = [out_spec(first) for first in range(side)]
        arrays = [shaped((side, chips, *piece), jnp.bfloat16)] * side
    found = call(kernel, where, args, (steps,), specs, outs, arrays, scratch, "weight_grads", flops, moved)
    return found[0] if sibling else found


def pick(values, at):
    return lax.dynamic_index_in_dim(values, at, 0, keepdims=False)


def on_device(
    tokens,
    conditions,
    resolution,
    modulate_weight,
    modulate_bias,
    attend_weight,
    forget_weight,
    forget_bias,
    conv_taps,
    output_weight,
    expand_weight,
    expand_bias,
    reduce_weight,
    cotangent,
):
    chips, side = mesh_parts()
    columns = side * side
    blocks = 2 * chips
    fsdp_at = lax.axis_index("fsdp")
    dp_at = lax.axis_index("dp")
    z_at, core_at, u_at, v_at = fsdp_at // 2, fsdp_at % 2, dp_at // side, dp_at % side
    where = jnp.stack([z_at, core_at, u_at, v_at, resolution[0]]).astype(jnp.int32)
    slots, features = conditions.shape
    heads = forget_bias.shape[0]
    own_rows, own_columns = modulate_weight.shape
    single = resolution[0] == 1

    attend_pieces = gather_shard(jnp.concatenate([attend_weight, forget_weight], axis=1))

    cond_values = conditions.astype(jnp.float32)
    silu_out, silu_back = jax.vjp(jax.nn.silu, cond_values)
    cond_low = silu_out.astype(jnp.bfloat16)
    small = jnp.concatenate([cond_low.reshape(-1), modulate_bias, expand_bias])
    small_size = small.shape[0]
    small = jnp.stack(gather_shard(small.reshape(1, small_size))).reshape(blocks * columns, small_size)
    order = []
    for block in range(blocks):
        for column in range(columns):
            sibling = jnp.abs(block % 2 - core_at)
            far = (z_at - block // 2) % chips
            by_u, by_v = (u_at - column // side) % side, (v_at - column % side) % side
            first = jnp.where(block % 2 == 0, by_u, by_v)
            second = jnp.where(block % 2 == 0, by_v, by_u)
            order.append(((sibling * side + first) * side + second) * chips + far)
    order = jnp.stack(order)
    chosen = (order[:, None] == jnp.arange(blocks * columns)[None, :]).astype(jnp.bfloat16)
    small = jnp.dot(chosen, small, preferred_element_type=jnp.float32)
    cond_all = small[:, : slots * features].astype(jnp.bfloat16).reshape(-1, features)
    modbias_whole = small[:, slots * features : small_size - expand_bias.shape[0]].reshape(-1)
    expandbias_whole = small[:, small_size - expand_bias.shape[0] :].reshape(1, -1)
    cond_columns = lax.dynamic_slice_in_dim(cond_all, fsdp_at * own_rows, own_rows, axis=1)
    partial = jnp.dot(cond_columns, modulate_weight, preferred_element_type=jnp.float32)
    partial = partial.reshape(chips, 2, columns * slots, own_columns)
    to_sibling = lax.dynamic_index_in_dim(partial, 1 - core_at, 1, keepdims=False)
    partial = lax.dynamic_index_in_dim(partial, core_at, 1, keepdims=False) + send(to_sibling, across_core)
    modulation = pick(partial, z_at)
    for shift in range(1, chips):
        modulation = modulation + send(pick(partial, (z_at + shift) % chips), along_z(shift))
    modulation = modulation.reshape(columns, slots, own_columns)
    pieces = [pick(modulation, dp_at)]
    for shift in range(1, columns):
        pieces.append(send(pick(modulation, (dp_at + shift) % columns), along_dp(shift)))
    pieces = jnp.stack(pieces)
    modulation = jnp.concatenate([pick(pieces, (dp_at - column) % columns) for column in range(columns)], axis=1)
    modulation = (modulation + modbias_whole[None, :]).reshape(slots, 6, features)
    modulation = jnp.pad(modulation, ((0, 0), (0, 2), (0, 0)))

    fold = fold_of(reduce_weight.shape, columns)
    middle_pieces = lax.all_gather(
        jnp.concatenate([expand_weight, output_weight], axis=1), ("fsdp", "dp"), axis=0, tiled=False
    )
    attend_first, reduce_shard = tied(attend_pieces[0], folded(reduce_weight, fold))
    attend_pieces[0] = attend_first
    reduce_far = far_pieces(reduce_shard)

    projected, gate_logit, normed_in_t = front_forward(
        where, tokens, modulation, attend_pieces, attend_weight.shape[1]
    )
    projected, reduce_far = tied(projected, reduce_far)
    reduce_level = first_pieces(jnp.stack(reduce_far))
    bias_wide = jnp.pad(forget_bias[None, :], ((0, 0), (0, LANES - heads)))
    conv_low, normed_heads, ratios, states = attention_forward(
        resolution, projected, gate_logit, bias_wide, conv_taps, heads
    )
    conv_low, reduce_level = tied(conv_low, reduce_level)
    reduce_pieces = second_pieces(reduce_level)
    attended, hidden, slope, hidden_t, normed_mid_t, conv_t, grad_reduced = middle_forward(
        where, conv_low, tokens, cotangent, modulation, expandbias_whole, middle_pieces, expand_weight.shape[1]
    )
    hidden_t, reduce_pieces = tied(hidden_t, reduce_pieces)
    reduce_pieces = core_pieces(reduce_pieces)
    reduce_other = cross_sum(weight_grads(where, hidden_t, grad_reduced, True, fold=fold))
    reduce_parts = weight_grads(where, hidden_t, grad_reduced, False, fold=fold)
    hidden, reduce_parts, reduce_other = tied(hidden, reduce_parts, reduce_other)
    reduce_level = first_sum(add_parts(reduce_parts, reduce_other))
    block_out, grad_preact, grad_after, grad_attended, grad_conv, middle_sums, bias_sums = middle_backward(
        where, hidden, slope, attended, tokens, cotangent, modulation, middle_pieces, reduce_pieces
    )
    grad_preact, reduce_level = tied(grad_preact, reduce_level)
    reduce_level = second_sum(reduce_level)
    expand_other = weight_grads(where, normed_mid_t, grad_preact, True)
    expand_other, conv_t = tied(expand_other, conv_t)
    expand_other = cross_sum(expand_other)
    output_other = cross_sum(weight_grads(where, conv_t, grad_attended, True))
    expand_parts = weight_grads(where, normed_mid_t, grad_preact, False, expand_other)
    output_parts = weight_grads(where, conv_t, grad_attended, False, output_other)
    grad_conv, expand_parts, output_parts, reduce_level = tied(grad_conv, expand_parts, output_parts, reduce_level)
    reduce_grad = far_sum(reduce_level)
    expand_level = first_sum(expand_parts)
    output_level = first_sum(output_parts)
    grad_projected, grad_gate, forgetbias_local, taps_local = attention_backward(
        resolution, projected, gate_logit, bias_wide, conv_taps, normed_heads, ratios, states, grad_conv, heads
    )
    grad_projected, expand_level, output_level, reduce_grad = tied(
        grad_projected, expand_level, output_level, reduce_grad
    )
    reduce_grad = unfolded(reduce_grad, fold)
    expand_level = second_sum(expand_level)
    output_level = second_sum(output_level)
    tokens_grad, front_sums = front_backward(
        where, grad_projected, grad_gate, grad_after, tokens, modulation, attend_pieces
    )
    grad_projected, front_sums, expand_level, output_level = tied(
        grad_projected, front_sums, expand_level, output_level
    )
    narrow = heads // columns
    attend_other = cross_sum(weight_grads(where, normed_in_t, grad_projected, True, None, grad_gate, narrow))
    attend_parts = weight_grads(where, normed_in_t, grad_projected, False, None, grad_gate, narrow)
    attend_level = first_sum(add_parts(attend_parts, attend_other))
    expand_grad = far_sum(expand_level)
    output_grad = far_sum(output_level)
    attend_both = far_sum(second_sum(attend_level))
    attend_grad, forget_grad = attend_both[:, : attend_weight.shape[1]], attend_both[:, attend_weight.shape[1] :]

    middle_sums = jnp.sum(middle_sums.reshape(QUARTERS, -1, 8, features), axis=1)
    grad_modulation = jnp.concatenate([front_sums[:, :2], middle_sums[:, :4]], axis=1)
    first_slot = (jnp.arange(slots) == 0)[:, None, None]
    grad_modulation = jnp.where(
        single, jnp.where(first_slot, jnp.sum(grad_modulation, axis=0, keepdims=True), 0.0), grad_modulation
    )
    grad_modulation = grad_modulation.reshape(slots, columns, own_columns).astype(jnp.bfloat16)
    grad_modulation = jnp.swapaxes(grad_modulation, 0, 1)
    rows_here = [pick(grad_modulation, dp_at)]
    for shift in range(1, columns):
        rows_here.append(send(pick(grad_modulation, (dp_at + shift) % columns), along_dp(shift)))
    rows_here = jnp.concatenate(rows_here, axis=0)
    rows_here = jnp.concatenate(
        [rows_here] + [send(rows_here, along_z(shift)) for shift in range(1, chips)], axis=0
    )
    rows_here = jnp.concatenate([rows_here, send(rows_here, across_core)], axis=0)
    order = []
    for sibling in range(2):
        for far in range(chips):
            for shift in range(columns):
                block = 2 * ((z_at - far) % chips) + jnp.abs(core_at - sibling)
                order.append(block * columns + (dp_at - shift) % columns)
    order = (jnp.stack(order)[:, None] * slots + jnp.arange(slots)[None, :]).reshape(-1)
    chosen = (order[:, None] == jnp.arange(order.shape[0])[None, :]).astype(jnp.bfloat16)
    cond_here = jnp.dot(chosen, cond_columns, preferred_element_type=jnp.float32).astype(jnp.bfloat16)
    modulate_grad = lax.dot_general(
        cond_here, rows_here, (((0,), (0,)), ((), ())), preferred_element_type=jnp.float32
    )
    modbias_here = jnp.sum(rows_here.astype(jnp.float32), axis=0, keepdims=True)
    modbias_all = jnp.stack(
        [modbias_here] + [send(modbias_here, along_dp(shift)) for shift in range(1, columns)]
    )
    modbias_all = jnp.concatenate([pick(modbias_all, (dp_at - column) % columns) for column in range(columns)], axis=1)
    own_bias = modulate_bias.shape[0]
    linear_at = fsdp_at * columns + dp_at
    modbias_grad = lax.dynamic_slice_in_dim(modbias_all, linear_at * own_bias, own_bias, axis=1).reshape(-1)
    grad_cond = lax.dot_general(
        rows_here, modulate_weight, (((1,), (1,)), ((), ())), preferred_element_type=jnp.float32
    )
    grad_cond = jnp.moveaxis(grad_cond.reshape(blocks, columns, slots, own_rows), 1, 0)
    cond_sum = grad_cond[0]
    for shift in range(1, columns):
        cond_sum = cond_sum + send(grad_cond[shift], along_dp(-shift))
    cond_sum = cond_sum.reshape(2, chips, slots, own_rows)
    cond_parts = []
    for sibling in range(2):
        for far in range(chips):
            def move(z, core, u, v, sibling=sibling, far=far):
                return (z - far) % chips, core ^ sibling, u, v
            part = cond_sum[sibling, far]
            cond_parts.append(part if sibling + far == 0 else send(part, move))
    cond_parts = jnp.stack(cond_parts)
    cond_columns_all = []
    for block in range(blocks):
        sibling = jnp.abs(block % 2 - core_at)
        cond_columns_all.append(pick(cond_parts, sibling * chips + (block // 2 - z_at) % chips))
    grad_cond_low = jnp.concatenate(cond_columns_all, axis=1)
    conditions_grad = silu_back(grad_cond_low)[0].astype(jnp.bfloat16)

    sums = jnp.concatenate(
        [
            taps_local,
            jnp.pad(forgetbias_local, ((0, 0), (0, features - LANES))),
            bias_sums.reshape(-1, features),
        ],
        axis=0,
    )
    sums, front_sums = tied(sums, front_sums)
    sums = sum_everywhere(sums)
    taps_count = conv_taps.shape[0]
    taps_grad = sums[:taps_count]
    forgetbias_grad = sums[taps_count, :heads]
    own_bias = expand_bias.shape[0]
    expandbias_grad = lax.dynamic_slice_in_dim(
        sums[taps_count + 1 :].reshape(-1), linear_at * own_bias, own_bias, axis=0
    )
    return (
        block_out,
        tokens_grad,
        conditions_grad,
        modulate_grad,
        modbias_grad,
        attend_grad,
        forget_grad,
        forgetbias_grad,
        taps_grad,
        output_grad,
        expand_grad,
        expandbias_grad,
        reduce_grad,
    )


def solution(mesh):
    in_specs = (
        P(("fsdp", "dp"), None),
        P(("fsdp", "dp"), None),
        P(("fsdp", "dp")),
        P("fsdp", "dp"),
        P(("fsdp", "dp")),
        P("fsdp", "dp"),
        P("fsdp", "dp"),
        P(),
        P(),
        P("fsdp", "dp"),
        P("fsdp", "dp"),
        P(("fsdp", "dp")),
        P("fsdp", "dp"),
        P(("fsdp", "dp"), None),
    )
    out_specs = (
        P(("fsdp", "dp"), None),
        P(("fsdp", "dp"), None),
        P(("fsdp", "dp"), None),
        P("fsdp", "dp"),
        P(("fsdp", "dp")),
        P("fsdp", "dp"),
        P("fsdp", "dp"),
        P(),
        P(),
        P("fsdp", "dp"),
        P("fsdp", "dp"),
        P(("fsdp", "dp")),
        P("fsdp", "dp"),
    )
    return jax.shard_map(
        on_device, mesh=mesh, in_specs=in_specs, out_specs=out_specs, check_vma=False
    )
```

time: 1920 us -> 716 us (0.37)
  waiting for transfers between devices: 668 us -> 154 us
  matrix products: 448 us -> 3.34 us
  Pallas kernels: 0 us -> 358 us
  local copies, waits for them, and re-layouts: 323 us -> 29.2 us
  other arithmetic: 277 us -> 45.5 us
  blocking collectives: 168 us -> 0 us
  starting transfers between devices: 1.24 us -> 101 us
    dot_general x30 -> x4, matrix products: 448 us -> 3.34 us  [the longest x1 2.41 us: on_device(): lax.dot_general(cond_here, rows_here, (((0,), (0,)), ((), ())), preferred...]
    reduce_scatter x5 -> x0, waiting for transfers between devices: 365 us -> none  [the longest x1 159 us: on_device(): lax.psum_scatter(modulate_grad.astype(jnp.bfloat16), 'fsdp', scatter_dime...]
    pallas_call x0 -> x14, Pallas kernels: none -> 358 us  [the longest x12 243 us: call(): pl.pallas_call(kernel, grid_spec=pltpu.PrefetchScalarGridSpec(num_scalar_...]
    all_gather x8 -> x1, waiting for transfers between devices: 203 us -> 0.01 us  [on_device(): lax.all_gather(jnp.concatenate([expand_weight, output_weight], axis=1), (...]
    ppermute x0 -> x86, waiting for transfers between devices: none -> 154 us  [send(): return lax.ppermute(values, ('fsdp', 'dp'), pairs)]
    ppermute x0 -> x86, starting transfers between devices: none -> 101 us  [send(): return lax.ppermute(values, ('fsdp', 'dp'), pairs)]
    unnamed x25 -> x1, waiting for transfers between devices: 99.7 us -> 0.02 us
    reshape x13 -> x9, local copies, waits for them, and re-layouts: 101 us -> 1.83 us  [the longest x1 0.71 us: on_device(): small[:, small_size - expand_bias.shape[0]:].reshape(1, -1)]
  transfers between devices with their start and end apart: 19 -> 87, of which waited for: 9 -> 33; matrix products, arithmetic and copies ran while one was open for 33% -> 7% of each run, Pallas kernels for 0% -> 43%
where the time goes in v1:
time: 716 us; the launch traced here: 708 us
  Pallas kernels  358 us (50%)
  waiting for transfers between devices  154 us (22%)
  starting transfers between devices  101 us (14%)
  other arithmetic  45.5 us (6%)
  local copies, waits for them, and re-layouts  29.2 us (4%)
  between operations  16.1 us (2%)
    pallas_call x12, Pallas kernels, call(): pl.pallas_call(kernel, grid_spec=pltpu.PrefetchScalarGridSpec(num_scalar_...  243 us
    ppermute x86, waiting for transfers between devices, send(): return lax.ppermute(values, ('fsdp', 'dp'), pairs)  154 us
    ppermute x86, starting transfers between devices, send(): return lax.ppermute(values, ('fsdp', 'dp'), pairs)  101 us
    pallas_call x1, Pallas kernels, attention_backward(): pl.pallas_call(functools.partial(attention_backward_kernel, heads, head_s...  71.6 us
    pallas_call x1, Pallas kernels, attention_forward(): pl.pallas_call(functools.partial(attention_forward_kernel, heads, head_si...  43.3 us
  transfers between devices with their start and end apart: 87, of which 33 were waited for; matrix products, arithmetic and copies ran while one was open for 7% of the time, Pallas kernels for 43%

profile of v1, /device:TPU:0, one launch (start us, length us, event | category | flops | bytes accessed | tf_op | source)
XLA Modules:
  0.0 707.7 jit_solution(1932247690175789283)
XLA Ops:
  7.3 1.9 pad_maximum_fusion.3
  11.4 3.1 collective-permute-start
  14.5 2.6 collective-permute-start.1
  21.4 2.9 collective-permute-start.19
  31.0 2.9 collective-permute-done.5
  38.2 11.4 %collective-permute-done.18 = bf16[144,868]{1,0:T(8,128)(2,1)S(1)} collective-permute-done((bf16[144,868]{1,0:T(8,128)(2,1)S(1)}, bf16[144,868]{1,0:T(8,128)(2,1)S(1)}, u32[]{:S(2)}, u32[]{:S(2)}) %collective-permute-start.18) | collective-permute-done | bytes 250016 | tf_op jit(solution)/shard_map/ppermute | solution.py:399
  57.6 24.5 %collective-permute-done.21.rest_2_ = bf16[4,144,868]{2,1,0:T(8,128)(2,1)S(1)} collective-permute-done((bf16[4,144,868]{2,1,0:T(8,128)(2,1)S(1)}, bf16[4,144,868]{2,1,0:T(8,128)(2,1)S(1)}, u32[]{:S(2)}, u32[]{:S(2)}) %collective-permute-start.21) | collective-permute-done | bytes 999968 | tf_op jit(solution)/shard_map/ppermute | solution.py:399
  83.6 6.2 collective-permute-start.11
  90.1 2.1 collective-permute-start.13
  92.2 3.5 collective-permute-done.11
  96.7 4.6 collective-permute-done.12
  104.5 4.3 collective-permute-done.14
  110.4 2.8 collective-permute-done.15
  119.1 2.2 collective-permute-start.27
  122.8 1.9 collective-permute-start.29
  126.2 20.8 %front_forward.1 = (bf16[1024,3456]{1,0:T(8,128)(2,1)}, f32[1024,128]{1,0:T(8,128)}, bf16[1152,1024]{1,0:T(8,128)(2,1)}) custom-call(s32[5]{0:T(128)} %stack.335.where, bf16[1024,1152]{1,0:T(8,128)(2,1)} %tokens_ref.7, f32[4,8,1152]{2,1,0:T(8,128)} %pad.12.mod_ref, bf16[4,144,868]{2,1,0:T(8,128)(2,1)} %copy-done.1, ...), custom_call_target="tpu_custom_call" | custom-call | flops 163829520 | bytes 400000 | tf_op jit(solution)/shard_map/front_forward/pallas_call | solution.py:638
  147.0 15.1 %collective-permute-done.28 = bf16[144,1152]{1,0:T(8,128)(2,1)S(1)} collective-permute-done((bf16[144,1152]{1,0:T(8,128)(2,1)S(1)}, bf16[144,1152]{1,0:T(8,128)(2,1)S(1)}, u32[]{:S(2)}, u32[]{:S(2)}) %collective-permute-start.28) | collective-permute-done | bytes 331808 | tf_op jit(solution)/shard_map/ppermute | solution.py:399
  163.1 1.8 collective-permute-start.30
  165.4 43.3 %attention_forward.1 = (bf16[1024,1152]{1,0:T(8,128)(2,1)}, f32[1024,1152]{1,0:T(8,128)}, f32[1024,128]{1,0:T(8,128)}, bf16[4,16,256,256]{3,2,1,0:T(8,128)(2,1)}) custom-call(s32[1]{0:T(128)S(6)} %copy.94.flag_ref, bf16[1024,3456]{1,0:T(8,128)(2,1)} %get-tuple-element.101.proj_ref, f32[1024,128]{1,0:T(8,128)} %get-tuple-element.102.gate_ref, ...), custom_call_target="tpu_custom_call" | custom-call | flops 340000000 | bytes 400000 | tf_op jit(solution)/shard_map/attention_forward/pallas_call | solution.py:185
  211.6 41.4 %middle_forward.1 = (f32[1024,1152]{1,0:T(8,128)}, bf16[1024,4608]{1,0:T(8,128)(2,1)}, bf16[1024,4608]{1,0:T(8,128)(2,1)}, bf16[4608,1024]{1,0:T(8,128)(2,1)}, b...) custom-call(s32[5]{0:T(128)} %stack.335.where, ...), custom_call_target="tpu_custom_call" | custom-call | flops 271790912 | bytes 1200000 | tf_op jit(solution)/shard_map/middle_forward/pallas_call | solution.py:638
  253.1 13.7 %weight_grads.9 = bf16[2,2,4,144,1152]{4,3,2,1,0:T(8,128)(2,1)} custom-call(s32[5]{0:T(128)} %stack.335.where, bf16[4608,1024]{1,0:T(8,128)(2,1)} %get-tuple-element.113.rest_0_, bf16[1024,1152]{1,0:T(8,128)(2,1)} %get-tuple-element.114.rest_1_), custom_call_target="tpu_custom_call" | custom-call | flops 434865440 | bytes 707788 | tf_op jit(solution)/shard_map/weight_grads/pallas_call | solution.py:638
  266.8 13.7 %weight_grads.8 = (bf16[2,4,144,1152]{3,2,1,0:T(8,128)(2,1)}, bf16[2,4,144,1152]{3,2,1,0:T(8,128)(2,1)}) custom-call(s32[5]{0:T(128)} %stack.335.where, bf16[4608,1024]{1,0:T(8,128)(2,1)} %get-tuple-element.113.rest_0_, bf16[1024,1152]{1,0:T(8,128)(2,1)} %get-tuple-element.114.rest_1_), custom_call_target="tpu_custom_call" | custom-call | flops 434865440 | bytes 707788 | tf_op jit(solution)/shard_map/weight_grads/pallas_call | solution.py:638
  280.5 6.9 fusion.1
  289.7 4.0 collective-permute-done.34.rest_5_
  298.9 68.4 %middle_backward.1 = (bf16[1024,1152]{1,0:T(8,128)(2,1)}, bf16[1024,4608]{1,0:T(8,128)(2,1)}, f32[1024,1152]{1,0:T(8,128)}, bf16[1024,1152]{1,0:T(8,128)(2,1)}, ...) custom-call(s32[5]{0:T(128)} %stack.335.where, bf16[1024,4608]{1,0:T(8,128)(2,1)} %get-tuple-element.117.hidden_ref, ...), custom_call_target="tpu_custom_call" | custom-call | flops 652298176 | bytes 1600000 | tf_op jit(solution)/shard_map/middle_backward/pallas_call | solution.py:638
  367.3 4.0 fusion.5
  371.3 11.2 %weight_grads.10 = bf16[2,2,4,144,1152]{4,3,2,1,0:T(8,128)(2,1)} custom-call(s32[5]{0:T(128)} %stack.335.where, bf16[1152,1024]{1,0:T(8,128)(2,1)} %get-tuple-element.129.rest_0_.rest_1_.rest_2_.rest_3_, bf16[1152,1024]{1,0:T(8,128)(2,1)} %get-tuple-element.129.rest_0_.rest_1_.rest_2_.rest_3_, ...), custom_call_target="tpu_custom_call" | custom-call | flops 108716360 | bytes 318504 | tf_op jit(solution)/shard_map/weight_grads/pallas_call | solution.py:638
  382.9 6.3 weight_grads.12
  390.0 4.0 collective-permute-done.40.rest_5_
  395.2 7.8 %weight_grads.13 = (bf16[2,4,144,288]{3,2,1,0:T(8,128)(2,1)}, bf16[2,4,144,288]{3,2,1,0:T(8,128)(2,1)}) custom-call(s32[5]{0:T(128)} %stack.335.where, bf16[1152,1024]{1,0:T(8,128)(2,1)} %get-tuple-element.139.rest_0_.rest_1_.rest_2_.rest_3_, bf16[1152,1024]{1,0:T(8,128)(2,1)} %get-tuple-element.139.rest_0_.rest_1_.rest_2_.rest_3_, ...), custom_call_target="tpu_custom_call" | custom-call | flops 27179088 | bytes 123863 | tf_op jit(solution)/shard_map/weight_grads/pallas_call | solution.py:638
  403.0 4.4 collective-permute-done.41
  409.0 13.0 %weight_grads.11 = (bf16[2,4,144,1152]{3,2,1,0:T(8,128)(2,1)}, bf16[2,4,144,1152]{3,2,1,0:T(8,128)(2,1)}) custom-call(s32[5]{0:T(128)} %stack.335.where, bf16[1152,1024]{1,0:T(8,128)(2,1)} %get-tuple-element.129.rest_0_.rest_1_.rest_2_.rest_3_, bf16[1152,1024]{1,0:T(8,128)(2,1)} %get-tuple-element.129.rest_0_.rest_1_.rest_2_.rest_3_, ...), custom_call_target="tpu_custom_call" | custom-call | flops 108716360 | bytes 424673 | tf_op jit(solution)/shard_map/weight_grads/pallas_call | solution.py:638
  422.6 10.8 %collective-permute-start.44 = (bf16[144,1152]{1,0:T(8,128)(2,1)S(1)}, bf16[144,1152]{1,0:T(8,128)(2,1)S(1)}, u32[]{:S(2)}, u32[]{:S(2)}) collective-permute-start(bf16[144,1152]{1,0:T(8,128)(2,1)S(1)} %get-tuple-element.152), channel_id=1, source_target_pairs={{0,8},{1,9},{2,10},{3,11},{4,12},{5,13},{6,14},{7,15},{8,16},{9,17... | collective-permute-start | bytes 995336 | tf_op jit(solution)/shard_map/ppermute | solution.py:399
  435.7 1.9 collective-permute-start.43
  437.6 71.6 %attention_backward.1 = (bf16[1024,3456]{1,0:T(8,128)(2,1)}, f32[1024,128]{1,0:T(8,128)}, f32[1,128]{1,0:T(1,128)}, f32[9,1152]{1,0:T(8,128)}) custom-call(s32[1]{0:T(128)S(6)} %copy.94.flag_ref, bf16[1024,3456]{1,0:T(8,128)(2,1)} %get-tuple-element.101.proj_ref, f32[1024,128]{1,0:T(8,128)} %get-tuple-element.102.gate_ref, f32[1,128]{1,0:T(1,128)} %pad.13.bias_ref, ...), custom_call_target="tpu_custom_call" | custom-call | flops 760000000 | bytes 800000 | tf_op jit(solution)/shard_map/attention_backward/pallas_call | solution.py:341
  511.5 2.2 fusion.17
  513.6 3.6 fusion.7
  517.5 1.7 collective-permute-start.48
  519.4 22.2 %front_backward.1 = (bf16[1024,1152]{1,0:T(8,128)(2,1)}, f32[4,8,1152]{2,1,0:T(8,128)}) custom-call(s32[5]{0:T(128)} %stack.335.where, bf16[1024,3456]{1,0:T(8,128)(2,1)} %get-tuple-element.167.gradproj_ref.rest_4_, f32[1024,128]{1,0:T(8,128)} %get-tuple-element.156.gradgate_ref.rest_5_, f32[1024,1152]{1,0:T(8,128)} %get-tuple-element.157.gradafter_ref, ...), custom_call_target="tpu_custom_call" | custom-call | flops 163829520 | bytes 500000 | tf_op jit(solution)/shard_map/front_backward/pallas_call | solution.py:638
  542.4 2.5 fusion.25
  544.9 12.6 %weight_grads.15 = bf16[2,2,4,144,868]{4,3,2,1,0:T(8,128)(2,1)} custom-call(s32[5]{0:T(128)} %stack.335.where, bf16[1152,1024]{1,0:T(8,128)(2,1)} %get-tuple-element.166.rest_0_.rest_1_.rest_2_.rest_3_, bf16[1152,1024]{1,0:T(8,128)(2,1)} %get-tuple-element.166.rest_0_.rest_1_.rest_2_.rest_3_, ...), custom_call_target="tpu_custom_call" | custom-call | flops 81914760 | bytes 245800 | tf_op jit(solution)/shard_map/weight_grads/pallas_call | solution.py:638
  559.8 1.9 collective-permute-start.50
  570.7 3.3 collective-permute-done.76
  576.1 3.0 collective-permute-start.82
  580.3 12.4 %weight_grads.14 = (bf16[2,4,144,868]{3,2,1,0:T(8,128)(2,1)}, bf16[2,4,144,868]{3,2,1,0:T(8,128)(2,1)}) custom-call(s32[5]{0:T(128)} %stack.335.where, bf16[1152,1024]{1,0:T(8,128)(2,1)} %get-tuple-element.166.rest_0_.rest_1_.rest_2_.rest_3_, bf16[1152,1024]{1,0:T(8,128)(2,1)} %get-tuple-element.166.rest_0_.rest_1_.rest_2_.rest_3_, ...), custom_call_target="tpu_custom_call" | custom-call | flops 81914760 | bytes 245800 | tf_op jit(solution)/shard_map/weight_grads/pallas_call | solution.py:638
  597.2 8.6 %collective-permute-done.78 = f32[14,1152]{1,0:T(8,128)S(1)} collective-permute-done((f32[14,1152]{1,0:T(8,128)S(1)}, f32[14,1152]{1,0:T(8,128)S(1)}, u32[]{:S(2)}, u32[]{:S(2)}) %collective-permute-start.78) | collective-permute-done | bytes 64544 | tf_op jit(solution)/shard_map/ppermute | solution.py:399
  606.4 3.6 concatenate.59
  610.1 2.2 collective-permute-start.66
  614.9 2.4 fusion.8
  619.6 1.9 collective-permute-start.56
  623.7 4.0 fusion.3
  629.9 2.5 collective-permute-start.59
  632.4 8.8 %collective-permute-done.59 = f32[4,144]{1,0:T(4,128)S(1)} collective-permute-done((f32[4,144]{1,0:T(4,128)S(1)}, f32[4,144]{1,0:T(4,128)S(1)}, u32[]{:S(2)}, u32[]{:S(2)}) %collective-permute-start.59) | collective-permute-done | bytes 2336 | tf_op jit(solution)/shard_map/ppermute | solution.py:399
  641.2 4.5 collective-permute-done.60
  646.3 4.8 collective-permute-done.61
  652.3 3.0 collective-permute-done.63
  655.3 3.9 collective-permute-done.64
  659.4 2.0 collective-permute-start.65
  667.0 12.1 %collective-permute-done.71 = bf16[4,144,868]{2,1,0:T(8,128)(2,1)S(1)} collective-permute-done((bf16[4,144,868]{2,1,0:T(8,128)(2,1)}, bf16[4,144,868]{2,1,0:T(8,128)(2,1)S(1)}, u32[]{:S(2)}, u32[]{:S(2)}) %collective-permute-start.71) | collective-permute-done | bytes 999968 | tf_op jit(solution)/shard_map/ppermute | solution.py:399
  679.8 1.7 collective-permute-start.73
  681.5 2.8 collective-permute-start.74
  684.4 2.1 convert_add_fusion.4
  686.5 3.8 collective-permute-done.72
  690.3 9.4 %collective-permute-done.73 = bf16[144,868]{1,0:T(8,128)(2,1)S(1)} collective-permute-done((bf16[144,868]{1,0:T(8,128)(2,1)S(1)}, bf16[144,868]{1,0:T(8,128)(2,1)S(1)}, u32[]{:S(2)}, u32[]{:S(2)}) %collective-permute-start.73) | collective-permute-done | bytes 250016 | tf_op jit(solution)/shard_map/ppermute | solution.py:399
  (330 shorter events, 101.3 us)
Async XLA Ops:
  7.2 204.4 %all-gather.3.cloned.1.call-start = ((), (), s32[]{:S(2)}) async-start(), calls=%async_computation | async-start | bytes 14598144 | tf_op jit(solution)/shard_map/all_gather | solution.py:1235
  11.4 10.0 %collective-permute-start = (bf16[1,4968]{1,0:T(2,128)(2,1)S(1)}, bf16[1,4968]{1,0:T(2,128)(2,1)S(1)}, u32[]{:S(2)}, u32[]{:S(2)}) collective-permute-start(bf16[1,4968]{1,0:T(2,128)(2,1)S(1)} %reshape.484), channel_id=1, source_target_pairs={{0,8},{1,9},{2,10},{3,11},{4,12},{5,13},{6,14},{7,15},{8,16},{9,17... | collective-permute-start | bytes 29816 | tf_op jit(solution)/shard_map/ppermute | solution.py:399
  14.5 9.8 %collective-permute-start.1 = (bf16[1,4968]{1,0:T(2,128)(2,1)S(1)}, bf16[1,4968]{1,0:T(2,128)(2,1)S(1)}, u32[]{:S(2)}, u32[]{:S(2)}) collective-permute-start(bf16[1,4968]{1,0:T(2,128)(2,1)S(1)} %reshape.484), channel_id=1, source_target_pairs={{0,16},{1,17},{2,18},{3,19},{4,20},{5,21},{6,22},{7,23},{8,24},{9,... | collective-permute-start | bytes 29816 | tf_op jit(solution)/shard_map/ppermute | solution.py:399
  17.1 7.2 %collective-permute-start.2 = (bf16[1,4968]{1,0:T(2,128)(2,1)S(1)}, bf16[1,4968]{1,0:T(2,128)(2,1)S(1)}, u32[]{:S(2)}, u32[]{:S(2)}) collective-permute-start(bf16[1,4968]{1,0:T(2,128)(2,1)S(1)} %reshape.484), channel_id=1, source_target_pairs={{0,24},{1,25},{2,26},{3,27},{4,28},{5,29},{6,30},{7,31},{8,0},{9,1... | collective-permute-start | bytes 29816 | tf_op jit(solution)/shard_map/ppermute | solution.py:399
  20.3 17.9 %collective-permute-start.17 = (bf16[144,868]{1,0:T(8,128)(2,1)S(1)}, bf16[144,868]{1,0:T(8,128)(2,1)S(1)}, u32[]{:S(2)}, u32[]{:S(2)}) collective-permute-start(bf16[144,868]{1,0:T(8,128)(2,1)S(1)} %pad_maximum_fusion.4), channel_id=1, source_target_pairs={{0,8},{1,9},{2,10},{3,11},{4,12},{5,13},{6,14},{7,15},{8,16},{9,17... | collective-permute-start | bytes 749960 | tf_op jit(solution)/shard_map/ppermute | solution.py:399
  21.0 28.6 %collective-permute-start.18 = (bf16[144,868]{1,0:T(8,128)(2,1)S(1)}, bf16[144,868]{1,0:T(8,128)(2,1)S(1)}, u32[]{:S(2)}, u32[]{:S(2)}) collective-permute-start(bf16[144,868]{1,0:T(8,128)(2,1)S(1)} %pad_maximum_fusion.4), channel_id=1, source_target_pairs={{0,16},{1,17},{2,18},{3,19},{4,20},{5,21},{6,22},{7,23},{8,24},{9,... | collective-permute-start | bytes 749960 | tf_op jit(solution)/shard_map/ppermute | solution.py:399
  21.4 28.2 %collective-permute-start.19 = (bf16[144,868]{1,0:T(8,128)(2,1)S(1)}, bf16[144,868]{1,0:T(8,128)(2,1)S(1)}, u32[]{:S(2)}, u32[]{:S(2)}) collective-permute-start(bf16[144,868]{1,0:T(8,128)(2,1)S(1)} %pad_maximum_fusion.4), channel_id=1, source_target_pairs={{0,24},{1,25},{2,26},{3,27},{4,28},{5,29},{6,30},{7,31},{8,0},{9,1... | collective-permute-start | bytes 749960 | tf_op jit(solution)/shard_map/ppermute | solution.py:399
  51.8 30.3 %collective-permute-start.21 = (bf16[4,144,868]{2,1,0:T(8,128)(2,1)S(1)}, bf16[4,144,868]{2,1,0:T(8,128)(2,1)S(1)}, u32[]{:S(2)}, u32[]{:S(2)}) collective-permute-start(bf16[4,144,868]{2,1,0:T(8,128)(2,1)S(1)} %pad_maximum_fusion.1.rest_0_), channel_id=1, source_target_pairs={{0,2},{1,3},{2,0},{3,1},{4,5},{5,4},{6,7},{7,6},{8,10},{9,11},{10,... | collective-permute-start | bytes 2999816 | tf_op jit(solution)/shard_map/ppermute | solution.py:399
  54.2 60.1 %collective-permute-start.20 = (bf16[4,144,868]{2,1,0:T(8,128)(2,1)S(1)}, bf16[4,144,868]{2,1,0:T(8,128)(2,1)}, u32[]{:S(2)}, u32[]{:S(2)}) collective-permute-start(bf16[4,144,868]{2,1,0:T(8,128)(2,1)S(1)} %pad_maximum_fusion.1.rest_0_), channel_id=1, source_target_pairs={{0,1},{1,0},{2,3},{3,2},{4,6},{5,7},{6,4},{7,5},{8,9},{9,8},{10,11... | collective-permute-start | bytes 2999816 | tf_op jit(solution)/shard_map/ppermute | solution.py:399
  82.1 32.2 %collective-permute-start.22 = (bf16[4,144,868]{2,1,0:T(8,128)(2,1)S(1)}, bf16[4,144,868]{2,1,0:T(8,128)(2,1)}, u32[]{:S(2)}, u32[]{:S(2)}) collective-permute-start(bf16[4,144,868]{2,1,0:T(8,128)(2,1)S(1)} %collective-permute-done.21.rest_2_), channel_id=1, source_target_pairs={{0,1},{1,0},{2,3},{3,2},{4,6},{5,7},{6,4},{7,5},{8,9},{9,8},{10,11... | collective-permute-start | bytes 2999816 | tf_op jit(solution)/shard_map/ppermute | solution.py:399
  83.6 12.1 %collective-permute-start.11 = (f32[16,1728]{1,0:T(8,128)S(1)}, f32[16,1728]{1,0:T(8,128)S(1)}, u32[]{:S(2)}, u32[]{:S(2)}) collective-permute-start(f32[16,1728]{1,0:T(8,128)S(1)} %get-tuple-element.242), channel_id=1, source_target_pairs={{0,8},{1,9},{2,10},{3,11},{4,12},{5,13},{6,14},{7,15},{8,16},{9,17... | collective-permute-start | bytes 331784 | tf_op jit(solution)/shard_map/ppermute | solution.py:399
  89.8 11.6 %collective-permute-start.12 = (f32[16,1728]{1,0:T(8,128)S(1)}, f32[16,1728]{1,0:T(8,128)S(1)}, u32[]{:S(2)}, u32[]{:S(2)}) collective-permute-start(f32[16,1728]{1,0:T(8,128)S(1)} %get-tuple-element.244), channel_id=1, source_target_pairs={{0,16},{1,17},{2,18},{3,19},{4,20},{5,21},{6,22},{7,23},{8,24},{9,... | collective-permute-start | bytes 331784 | tf_op jit(solution)/shard_map/ppermute | solution.py:399
  90.1 11.9 %collective-permute-start.13 = (f32[16,1728]{1,0:T(8,128)S(1)}, f32[16,1728]{1,0:T(8,128)S(1)}, u32[]{:S(2)}, u32[]{:S(2)}) collective-permute-start(f32[16,1728]{1,0:T(8,128)S(1)} %get-tuple-element.243), channel_id=1, source_target_pairs={{0,24},{1,25},{2,26},{3,27},{4,28},{5,29},{6,30},{7,31},{8,0},{9,1... | collective-permute-start | bytes 331784 | tf_op jit(solution)/shard_map/ppermute | solution.py:399
  95.7 26.6 %collective-permute-start.23 = (bf16[4,144,868]{2,1,0:T(8,128)(2,1)S(1)}, bf16[4,144,868]{2,1,0:T(8,128)(2,1)}, u32[]{:S(2)}, u32[]{:S(2)}) collective-permute-start(bf16[4,144,868]{2,1,0:T(8,128)(2,1)S(1)} %pad_maximum_fusion.1.rest_0_), channel_id=1, source_target_pairs={{0,4},{1,5},{2,6},{3,7},{4,0},{5,1},{6,2},{7,3},{8,12},{9,13},{10,... | collective-permute-start | bytes 2999816 | tf_op jit(solution)/shard_map/ppermute | solution.py:399
  101.4 21.5 %collective-permute-start.25 = (bf16[4,144,868]{2,1,0:T(8,128)(2,1)S(1)}, bf16[4,144,868]{2,1,0:T(8,128)(2,1)}, u32[]{:S(2)}, u32[]{:S(2)}) collective-permute-start(bf16[4,144,868]{2,1,0:T(8,128)(2,1)S(1)} %collective-permute-done.21.rest_2_), channel_id=1, source_target_pairs={{0,4},{1,5},{2,6},{3,7},{4,0},{5,1},{6,2},{7,3},{8,12},{9,13},{10,... | collective-permute-start | bytes 2999816 | tf_op jit(solution)/shard_map/ppermute | solution.py:399
  114.2 12.0 %collective-permute-start.24 = (bf16[4,144,868]{2,1,0:T(8,128)(2,1)}, bf16[4,144,868]{2,1,0:T(8,128)(2,1)}, u32[]{:S(2)}, u32[]{:S(2)}) collective-permute-start(bf16[4,144,868]{2,1,0:T(8,128)(2,1)} %collective-permute-done.20.rest_1_), channel_id=1, source_target_pairs={{0,4},{1,5},{2,6},{3,7},{4,0},{5,1},{6,2},{7,3},{8,12},{9,13},{10,... | collective-permute-start | bytes 2999816 | tf_op jit(solution)/shard_map/ppermute | solution.py:399
  114.3 11.9 %collective-permute-start.26 = (bf16[4,144,868]{2,1,0:T(8,128)(2,1)}, bf16[4,144,868]{2,1,0:T(8,128)(2,1)}, u32[]{:S(2)}, u32[]{:S(2)}) collective-permute-start(bf16[4,144,868]{2,1,0:T(8,128)(2,1)} %collective-permute-done.22.rest_3_), channel_id=1, source_target_pairs={{0,4},{1,5},{2,6},{3,7},{4,0},{5,1},{6,2},{7,3},{8,12},{9,13},{10,... | collective-permute-start | bytes 2999816 | tf_op jit(solution)/shard_map/ppermute | solution.py:399
  119.1 27.9 %collective-permute-start.27 = (bf16[144,1152]{1,0:T(8,128)(2,1)S(1)}, bf16[144,1152]{1,0:T(8,128)(2,1)S(1)}, u32[]{:S(2)}, u32[]{:S(2)}) collective-permute-start(bf16[144,1152]{1,0:T(8,128)(2,1)S(1)} %concatenate.53), channel_id=1, source_target_pairs={{0,8},{1,9},{2,10},{3,11},{4,12},{5,13},{6,14},{7,15},{8,16},{9,17... | collective-permute-start | bytes 995336 | tf_op jit(solution)/shard_map/ppermute | solution.py:399
  122.3 39.8 %collective-permute-start.28 = (bf16[144,1152]{1,0:T(8,128)(2,1)S(1)}, bf16[144,1152]{1,0:T(8,128)(2,1)S(1)}, u32[]{:S(2)}, u32[]{:S(2)}) collective-permute-start(bf16[144,1152]{1,0:T(8,128)(2,1)S(1)} %concatenate.53), channel_id=1, source_target_pairs={{0,16},{1,17},{2,18},{3,19},{4,20},{5,21},{6,22},{7,23},{8,24},{9,... | collective-permute-start | bytes 995336 | tf_op jit(solution)/shard_map/ppermute | solution.py:399
  122.8 40.1 %collective-permute-start.29 = (bf16[144,1152]{1,0:T(8,128)(2,1)S(1)}, bf16[144,1152]{1,0:T(8,128)(2,1)S(1)}, u32[]{:S(2)}, u32[]{:S(2)}) collective-permute-start(bf16[144,1152]{1,0:T(8,128)(2,1)S(1)} %concatenate.53), channel_id=1, source_target_pairs={{0,24},{1,25},{2,26},{3,27},{4,28},{5,29},{6,30},{7,31},{8,0},{9,1... | collective-permute-start | bytes 995336 | tf_op jit(solution)/shard_map/ppermute | solution.py:399
  163.1 45.6 %collective-permute-start.30 = (bf16[4,144,1152]{2,1,0:T(8,128)(2,1)S(1)}, bf16[4,144,1152]{2,1,0:T(8,128)(2,1)}, u32[]{:S(2)}, u32[]{:S(2)}) collective-permute-start(bf16[4,144,1152]{2,1,0:T(8,128)(2,1)S(1)} %pad_maximum_fusion.rest_1_), channel_id=1, source_target_pairs={{0,2},{1,3},{2,0},{3,1},{4,5},{5,4},{6,7},{7,6},{8,10},{9,11},{10,... | collective-permute-start | bytes 3981320 | tf_op jit(solution)/shard_map/ppermute | solution.py:399
  208.8 44.3 %collective-permute-start.31 = (bf16[4,144,1152]{2,1,0:T(8,128)(2,1)S(1)}, bf16[4,144,1152]{2,1,0:T(8,128)(2,1)}, u32[]{:S(2)}, u32[]{:S(2)}) collective-permute-start(bf16[4,144,1152]{2,1,0:T(8,128)(2,1)S(1)} %pad_maximum_fusion.rest_1_), channel_id=1, source_target_pairs={{0,1},{1,0},{2,3},{3,2},{4,6},{5,7},{6,4},{7,5},{8,9},{9,8},{10,11... | collective-permute-start | bytes 3981320 | tf_op jit(solution)/shard_map/ppermute | solution.py:399
  210.3 42.8 %collective-permute-start.32 = (bf16[4,144,1152]{2,1,0:T(8,128)(2,1)}, bf16[4,144,1152]{2,1,0:T(8,128)(2,1)}, u32[]{:S(2)}, u32[]{:S(2)}) collective-permute-start(bf16[4,144,1152]{2,1,0:T(8,128)(2,1)} %collective-permute-done.30.rest_3_), channel_id=1, source_target_pairs={{0,1},{1,0},{2,3},{3,2},{4,6},{5,7},{6,4},{7,5},{8,9},{9,8},{10,11... | collective-permute-start | bytes 3981320 | tf_op jit(solution)/shard_map/ppermute | solution.py:399
  266.8 13.7 %collective-permute-start.33 = (bf16[2,2,4,144,1152]{4,3,2,1,0:T(8,128)(2,1)}, bf16[2,2,4,144,1152]{4,3,2,1,0:T(8,128)(2,1)}, u32[]{:S(2)}, u32[]{:S(2)}) collective-permute-start(bf16[2,2,4,144,1152]{4,3,2,1,0:T(8,128)(2,1)} %weight_grads.9), channel_id=1, source_target_pairs={{0,4},{1,5},{2,6},{3,7},{4,0},{5,1},{6,2},{7,3},{8,12},{9,13},{10,... | collective-permute-start | bytes 15925256 | tf_op jit(solution)/shard_map/ppermute | solution.py:399
  287.4 79.9 %collective-permute-start.38 = (bf16[2,4,144,1152]{3,2,1,0:T(8,128)(2,1)}, bf16[2,4,144,1152]{3,2,1,0:T(8,128)(2,1)}, u32[]{:S(2)}, u32[]{:S(2)}) collective-permute-start(bf16[2,4,144,1152]{3,2,1,0:T(8,128)(2,1)} %get-tuple-element.216), channel_id=1, source_target_pairs={{0,2},{1,3},{2,0},{3,1},{4,5},{5,4},{6,7},{7,6},{8,10},{9,11},{10,... | collective-permute-start | bytes 7962632 | tf_op jit(solution)/shard_map/ppermute | solution.py:399
  288.0 5.8 collective-permute-start.34
  289.2 6.7 collective-permute-start.36
  289.7 8.1 %collective-permute-start.37 = (bf16[4,144,1152]{2,1,0:T(8,128)(2,1)}, bf16[4,144,1152]{2,1,0:T(8,128)(2,1)S(1)}, u32[]{:S(2)}, u32[]{:S(2)}) collective-permute-start(bf16[4,144,1152]{2,1,0:T(8,128)(2,1)} %collective-permute-done.32.rest_4_), channel_id=1, source_target_pairs={{0,4},{1,5},{2,6},{3,7},{4,0},{5,1},{6,2},{7,3},{8,12},{9,13},{10,... | collective-permute-start | bytes 3981320 | tf_op jit(solution)/shard_map/ppermute | solution.py:399
  382.5 26.5 %collective-permute-start.39 = (bf16[2,2,4,144,1152]{4,3,2,1,0:T(8,128)(2,1)}, bf16[2,2,4,144,1152]{4,3,2,1,0:T(8,128)(2,1)}, u32[]{:S(2)}, u32[]{:S(2)}) collective-permute-start(bf16[2,2,4,144,1152]{4,3,2,1,0:T(8,128)(2,1)} %weight_grads.10), channel_id=1, source_target_pairs={{0,4},{1,5},{2,6},{3,7},{4,0},{5,1},{6,2},{7,3},{8,12},{9,13},{10,... | collective-permute-start | bytes 15925256 | tf_op jit(solution)/shard_map/ppermute | solution.py:399
  389.3 18.1 %collective-permute-start.41 = (bf16[4,144,1152]{2,1,0:T(8,128)(2,1)}, bf16[4,144,1152]{2,1,0:T(8,128)(2,1)}, u32[]{:S(2)}, u32[]{:S(2)}) collective-permute-start(bf16[4,144,1152]{2,1,0:T(8,128)(2,1)} %get-tuple-element.144), channel_id=1, source_target_pairs={{0,1},{1,0},{2,3},{3,2},{4,6},{5,7},{6,4},{7,5},{8,9},{9,8},{10,11... | collective-permute-start | bytes 3981320 | tf_op jit(solution)/shard_map/ppermute | solution.py:399
  422.0 91.7 %collective-permute-start.42 = (bf16[2,4,144,1152]{3,2,1,0:T(8,128)(2,1)}, bf16[2,4,144,1152]{3,2,1,0:T(8,128)(2,1)}, u32[]{:S(2)}, u32[]{:S(2)}) collective-permute-start(bf16[2,4,144,1152]{3,2,1,0:T(8,128)(2,1)} %get-tuple-element.148), channel_id=1, source_target_pairs={{0,2},{1,3},{2,0},{3,1},{4,5},{5,4},{6,7},{7,6},{8,10},{9,11},{10,... | collective-permute-start | bytes 7962632 | tf_op jit(solution)/shard_map/ppermute | solution.py:399
  422.6 86.7 %collective-permute-start.44 = (bf16[144,1152]{1,0:T(8,128)(2,1)S(1)}, bf16[144,1152]{1,0:T(8,128)(2,1)S(1)}, u32[]{:S(2)}, u32[]{:S(2)}) collective-permute-start(bf16[144,1152]{1,0:T(8,128)(2,1)S(1)} %get-tuple-element.152), channel_id=1, source_target_pairs={{0,8},{1,9},{2,10},{3,11},{4,12},{5,13},{6,14},{7,15},{8,16},{9,17... | collective-permute-start | bytes 995336 | tf_op jit(solution)/shard_map/ppermute | solution.py:399
  433.3 76.0 %collective-permute-start.45 = (bf16[144,1152]{1,0:T(8,128)(2,1)S(1)}, bf16[144,1152]{1,0:T(8,128)(2,1)S(1)}, u32[]{:S(2)}, u32[]{:S(2)}) collective-permute-start(bf16[144,1152]{1,0:T(8,128)(2,1)S(1)} %get-tuple-element.153), channel_id=1, source_target_pairs={{0,16},{1,17},{2,18},{3,19},{4,20},{5,21},{6,22},{7,23},{8,24},{9,... | collective-permute-start | bytes 995336 | tf_op jit(solution)/shard_map/ppermute | solution.py:399
  434.7 75.3 %collective-permute-start.46 = (bf16[144,1152]{1,0:T(8,128)(2,1)S(1)}, bf16[144,1152]{1,0:T(8,128)(2,1)}, u32[]{:S(2)}, u32[]{:S(2)}) collective-permute-start(bf16[144,1152]{1,0:T(8,128)(2,1)S(1)} %get-tuple-element.154), channel_id=1, source_target_pairs={{0,24},{1,25},{2,26},{3,27},{4,28},{5,29},{6,30},{7,31},{8,0},{9,1... | collective-permute-start | bytes 995336 | tf_op jit(solution)/shard_map/ppermute | solution.py:399
  435.7 75.7 %collective-permute-start.43 = (bf16[2,4,144,288]{3,2,1,0:T(8,128)(2,1)}, bf16[2,4,144,288]{3,2,1,0:T(8,128)(2,1)}, u32[]{:S(2)}, u32[]{:S(2)}) collective-permute-start(bf16[2,4,144,288]{3,2,1,0:T(8,128)(2,1)} %get-tuple-element.150), channel_id=1, source_target_pairs={{0,2},{1,3},{2,0},{3,1},{4,5},{5,4},{6,7},{7,6},{8,10},{9,11},{10,... | collective-permute-start | bytes 1990664 | tf_op jit(solution)/shard_map/ppermute | solution.py:399
  517.2 25.2 %collective-permute-start.47 = (bf16[4,144,1152]{2,1,0:T(8,128)(2,1)}, bf16[4,144,1152]{2,1,0:T(8,128)(2,1)}, u32[]{:S(2)}, u32[]{:S(2)}) collective-permute-start(bf16[4,144,1152]{2,1,0:T(8,128)(2,1)} %get-tuple-element.161), channel_id=1, source_target_pairs={{0,1},{1,0},{2,3},{3,2},{4,6},{5,7},{6,4},{7,5},{8,9},{9,8},{10,11... | collective-permute-start | bytes 3981320 | tf_op jit(solution)/shard_map/ppermute | solution.py:399
  517.5 24.1 %collective-permute-start.48 = (bf16[4,144,288]{2,1,0:T(8,128)(2,1)}, bf16[4,144,288]{2,1,0:T(8,128)(2,1)S(1)}, u32[]{:S(2)}, u32[]{:S(2)}) collective-permute-start(bf16[4,144,288]{2,1,0:T(8,128)(2,1)} %get-tuple-element.163), channel_id=1, source_target_pairs={{0,1},{1,0},{2,3},{3,2},{4,6},{5,7},{6,4},{7,5},{8,9},{9,8},{10,11... | collective-permute-start | bytes 995336 | tf_op jit(solution)/shard_map/ppermute | solution.py:399
  557.5 65.2 %collective-permute-start.69 = (bf16[2,2,4,144,868]{4,3,2,1,0:T(8,128)(2,1)}, bf16[2,2,4,144,868]{4,3,2,1,0:T(8,128)(2,1)}, u32[]{:S(2)}, u32[]{:S(2)}) collective-permute-start(bf16[2,2,4,144,868]{4,3,2,1,0:T(8,128)(2,1)} %weight_grads.15), channel_id=1, source_target_pairs={{0,4},{1,5},{2,6},{3,7},{4,0},{5,1},{6,2},{7,3},{8,12},{9,13},{10,... | collective-permute-start | bytes 11999240 | tf_op jit(solution)/shard_map/ppermute | solution.py:399
  562.7 6.8 collective-permute-start.75
  565.6 9.1 %collective-permute-start.52 = (bf16[16,1728]{1,0:T(8,128)(2,1)S(1)}, bf16[16,1728]{1,0:T(8,128)(2,1)S(1)}, u32[]{:S(2)}, u32[]{:S(2)}) collective-permute-start(bf16[16,1728]{1,0:T(8,128)(2,1)S(1)} %pad_maximum_fusion.7), channel_id=1, source_target_pairs={{0,8},{1,9},{2,10},{3,11},{4,12},{5,13},{6,14},{7,15},{8,16},{9,17... | collective-permute-start | bytes 165896 | tf_op jit(solution)/shard_map/ppermute | solution.py:399
  566.6 9.5 %collective-permute-start.53 = (bf16[16,1728]{1,0:T(8,128)(2,1)S(1)}, bf16[16,1728]{1,0:T(8,128)(2,1)S(1)}, u32[]{:S(2)}, u32[]{:S(2)}) collective-permute-start(bf16[16,1728]{1,0:T(8,128)(2,1)S(1)} %pad_maximum_fusion.7), channel_id=1, source_target_pairs={{0,16},{1,17},{2,18},{3,19},{4,20},{5,21},{6,22},{7,23},{8,24},{9,... | collective-permute-start | bytes 165896 | tf_op jit(solution)/shard_map/ppermute | solution.py:399
  568.3 10.8 %collective-permute-start.54 = (bf16[16,1728]{1,0:T(8,128)(2,1)S(1)}, bf16[16,1728]{1,0:T(8,128)(2,1)S(1)}, u32[]{:S(2)}, u32[]{:S(2)}) collective-permute-start(bf16[16,1728]{1,0:T(8,128)(2,1)S(1)} %pad_maximum_fusion.7), channel_id=1, source_target_pairs={{0,24},{1,25},{2,26},{3,27},{4,28},{5,29},{6,30},{7,31},{8,0},{9,1... | collective-permute-start | bytes 165896 | tf_op jit(solution)/shard_map/ppermute | solution.py:399
  573.9 19.8 %collective-permute-start.80 = (bf16[144,288]{1,0:T(8,128)(2,1)S(1)}, bf16[144,288]{1,0:T(8,128)(2,1)S(1)}, u32[]{:S(2)}, u32[]{:S(2)}) collective-permute-start(bf16[144,288]{1,0:T(8,128)(2,1)S(1)} %copy-done.31), channel_id=1, source_target_pairs={{0,8},{1,9},{2,10},{3,11},{4,12},{5,13},{6,14},{7,15},{8,16},{9,17... | collective-permute-start | bytes 248840 | tf_op jit(solution)/shard_map/ppermute | solution.py:399
  574.8 19.5 %collective-permute-start.81 = (bf16[144,288]{1,0:T(8,128)(2,1)S(1)}, bf16[144,288]{1,0:T(8,128)(2,1)}, u32[]{:S(2)}, u32[]{:S(2)}) collective-permute-start(bf16[144,288]{1,0:T(8,128)(2,1)S(1)} %copy-done.30), channel_id=1, source_target_pairs={{0,16},{1,17},{2,18},{3,19},{4,20},{5,21},{6,22},{7,23},{8,24},{9,... | collective-permute-start | bytes 248840 | tf_op jit(solution)/shard_map/ppermute | solution.py:399
  576.1 19.4 %collective-permute-start.82 = (bf16[144,288]{1,0:T(8,128)(2,1)S(1)}, bf16[144,288]{1,0:T(8,128)(2,1)}, u32[]{:S(2)}, u32[]{:S(2)}) collective-permute-start(bf16[144,288]{1,0:T(8,128)(2,1)S(1)} %copy-done.29), channel_id=1, source_target_pairs={{0,24},{1,25},{2,26},{3,27},{4,28},{5,29},{6,30},{7,31},{8,0},{9,1... | collective-permute-start | bytes 248840 | tf_op jit(solution)/shard_map/ppermute | solution.py:399
  579.1 13.7 %collective-permute-start.77 = (f32[14,1152]{1,0:T(8,128)S(1)}, f32[14,1152]{1,0:T(8,128)}, u32[]{:S(2)}, u32[]{:S(2)}) collective-permute-start(f32[14,1152]{1,0:T(8,128)S(1)} %add.1131), channel_id=1, source_target_pairs={{0,4},{1,5},{2,6},{3,7},{4,0},{5,1},{6,2},{7,3},{8,12},{9,13},{10,... | collective-permute-start | bytes 193544 | tf_op jit(solution)/shard_map/ppermute | solution.py:399
  592.8 88.8 %collective-permute-start.83 = (bf16[144,1152]{1,0:T(8,128)(2,1)}, bf16[144,1152]{1,0:T(8,128)(2,1)}, u32[]{:S(2)}, u32[]{:S(2)}) collective-permute-start(bf16[144,1152]{1,0:T(8,128)(2,1)} %get-tuple-element.179), channel_id=1, source_target_pairs={{0,8},{1,9},{2,10},{3,11},{4,12},{5,13},{6,14},{7,15},{8,16},{9,17... | collective-permute-start | bytes 995336 | tf_op jit(solution)/shard_map/ppermute | solution.py:399
  593.7 12.7 %collective-permute-start.55 = (bf16[64,1728]{1,0:T(8,128)(2,1)S(1)}, bf16[64,1728]{1,0:T(8,128)(2,1)}, u32[]{:S(2)}, u32[]{:S(2)}) collective-permute-start(bf16[64,1728]{1,0:T(8,128)(2,1)S(1)} %concatenate.58), channel_id=1, source_target_pairs={{0,4},{1,5},{2,6},{3,7},{4,0},{5,1},{6,2},{7,3},{8,12},{9,13},{10,... | collective-permute-start | bytes 663560 | tf_op jit(solution)/shard_map/ppermute | solution.py:399
  594.3 11.5 %collective-permute-start.78 = (f32[14,1152]{1,0:T(8,128)S(1)}, f32[14,1152]{1,0:T(8,128)S(1)}, u32[]{:S(2)}, u32[]{:S(2)}) collective-permute-start(f32[14,1152]{1,0:T(8,128)S(1)} %add.1132), channel_id=1, source_target_pairs={{0,8},{1,9},{2,10},{3,11},{4,12},{5,13},{6,14},{7,15},{8,0},{9,1},... | collective-permute-start | bytes 193544 | tf_op jit(solution)/shard_map/ppermute | solution.py:399
  610.1 7.9 %collective-permute-start.66 = (f32[1,1728]{1,0:T(1,128)S(1)}, f32[1,1728]{1,0:T(1,128)S(1)}, u32[]{:S(2)}, u32[]{:S(2)}) collective-permute-start(f32[1,1728]{1,0:T(1,128)S(1)} %broadcast_in_dim.40), channel_id=1, source_target_pairs={{0,1},{1,2},{2,3},{3,0},{4,5},{5,6},{6,7},{7,4},{8,9},{9,10},{10,1... | collective-permute-start | bytes 20744 | tf_op jit(solution)/shard_map/ppermute | solution.py:399
  612.3 7.3 %collective-permute-start.67 = (f32[1,1728]{1,0:T(1,128)S(1)}, f32[1,1728]{1,0:T(1,128)S(1)}, u32[]{:S(2)}, u32[]{:S(2)}) collective-permute-start(f32[1,1728]{1,0:T(1,128)S(1)} %broadcast_in_dim.40), channel_id=1, source_target_pairs={{0,2},{1,3},{2,0},{3,1},{4,6},{5,7},{6,4},{7,5},{8,10},{9,11},{10,... | collective-permute-start | bytes 20744 | tf_op jit(solution)/shard_map/ppermute | solution.py:399
  612.6 8.9 %collective-permute-start.68 = (f32[1,1728]{1,0:T(1,128)S(1)}, f32[1,1728]{1,0:T(1,128)S(1)}, u32[]{:S(2)}, u32[]{:S(2)}) collective-permute-start(f32[1,1728]{1,0:T(1,128)S(1)} %broadcast_in_dim.40), channel_id=1, source_target_pairs={{0,3},{1,0},{2,1},{3,2},{4,7},{5,4},{6,5},{7,6},{8,11},{9,8},{10,9... | collective-permute-start | bytes 20744 | tf_op jit(solution)/shard_map/ppermute | solution.py:399
  618.1 66.3 %collective-permute-start.84 = (bf16[144,1152]{1,0:T(8,128)(2,1)}, bf16[144,1152]{1,0:T(8,128)(2,1)}, u32[]{:S(2)}, u32[]{:S(2)}) collective-permute-start(bf16[144,1152]{1,0:T(8,128)(2,1)} %get-tuple-element.180), channel_id=1, source_target_pairs={{0,16},{1,17},{2,18},{3,19},{4,20},{5,21},{6,22},{7,23},{8,24},{9,... | collective-permute-start | bytes 995336 | tf_op jit(solution)/shard_map/ppermute | solution.py:399
  619.6 8.2 %collective-permute-start.56 = (f32[8,4,144]{2,1,0:T(4,128)S(1)}, f32[8,4,144]{2,1,0:T(4,128)S(1)}, u32[]{:S(2)}, u32[]{:S(2)}) collective-permute-start(f32[8,4,144]{2,1,0:T(4,128)S(1)} %get-tuple-element.249), channel_id=1, source_target_pairs={{0,3},{1,0},{2,1},{3,2},{4,7},{5,4},{6,5},{7,6},{8,11},{9,8},{10,9... | collective-permute-start | bytes 55304 | tf_op jit(solution)/shard_map/ppermute | solution.py:399
  621.5 6.8 collective-permute-start.57
  622.7 6.4 collective-permute-start.58
  627.8 56.6 %collective-permute-start.85 = (bf16[144,1152]{1,0:T(8,128)(2,1)}, bf16[144,1152]{1,0:T(8,128)(2,1)S(1)}, u32[]{:S(2)}, u32[]{:S(2)}) collective-permute-start(bf16[144,1152]{1,0:T(8,128)(2,1)} %get-tuple-element.181), channel_id=1, source_target_pairs={{0,24},{1,25},{2,26},{3,27},{4,28},{5,29},{6,30},{7,31},{8,0},{9,1... | collective-permute-start | bytes 995336 | tf_op jit(solution)/shard_map/ppermute | solution.py:399
  628.4 31.0 %collective-permute-start.70 = (bf16[2,4,144,868]{3,2,1,0:T(8,128)(2,1)S(1)}, bf16[2,4,144,868]{3,2,1,0:T(8,128)(2,1)S(1)}, u32[]{:S(2)}, u32[]{:S(2)}) collective-permute-start(bf16[2,4,144,868]{3,2,1,0:T(8,128)(2,1)S(1)} %get-tuple-element.220), channel_id=1, source_target_pairs={{0,2},{1,3},{2,0},{3,1},{4,5},{5,4},{6,7},{7,6},{8,10},{9,11},{10,... | collective-permute-start | bytes 5999624 | tf_op jit(solution)/shard_map/ppermute | solution.py:399
  629.9 11.3 %collective-permute-start.59 = (f32[4,144]{1,0:T(4,128)S(1)}, f32[4,144]{1,0:T(4,128)S(1)}, u32[]{:S(2)}, u32[]{:S(2)}) collective-permute-start(f32[4,144]{1,0:T(4,128)S(1)} %get-tuple-element.278), channel_id=1, source_target_pairs={{0,24},{1,25},{2,26},{3,27},{4,28},{5,29},{6,30},{7,31},{8,0},{9,1... | collective-permute-start | bytes 6920 | tf_op jit(solution)/shard_map/ppermute | solution.py:399
  659.2 6.5 collective-permute-start.79
  664.2 14.8 %collective-permute-start.71 = (bf16[4,144,868]{2,1,0:T(8,128)(2,1)}, bf16[4,144,868]{2,1,0:T(8,128)(2,1)S(1)}, u32[]{:S(2)}, u32[]{:S(2)}) collective-permute-start(bf16[4,144,868]{2,1,0:T(8,128)(2,1)} %get-tuple-element.218), channel_id=1, source_target_pairs={{0,1},{1,0},{2,3},{3,2},{4,6},{5,7},{6,4},{7,5},{8,9},{9,8},{10,11... | collective-permute-start | bytes 2999816 | tf_op jit(solution)/shard_map/ppermute | solution.py:399
  679.2 11.1 %collective-permute-start.72 = (bf16[144,868]{1,0:T(8,128)(2,1)S(1)}, bf16[144,868]{1,0:T(8,128)(2,1)S(1)}, u32[]{:S(2)}, u32[]{:S(2)}) collective-permute-start(bf16[144,868]{1,0:T(8,128)(2,1)S(1)} %get-tuple-element.229), channel_id=1, source_target_pairs={{0,8},{1,9},{2,10},{3,11},{4,12},{5,13},{6,14},{7,15},{8,16},{9,17... | collective-permute-start | bytes 749960 | tf_op jit(solution)/shard_map/ppermute | solution.py:399
  679.8 19.9 %collective-permute-start.73 = (bf16[144,868]{1,0:T(8,128)(2,1)S(1)}, bf16[144,868]{1,0:T(8,128)(2,1)S(1)}, u32[]{:S(2)}, u32[]{:S(2)}) collective-permute-start(bf16[144,868]{1,0:T(8,128)(2,1)S(1)} %get-tuple-element.231), channel_id=1, source_target_pairs={{0,16},{1,17},{2,18},{3,19},{4,20},{5,21},{6,22},{7,23},{8,24},{9,... | collective-permute-start | bytes 749960 | tf_op jit(solution)/shard_map/ppermute | solution.py:399
  681.5 18.2 %collective-permute-start.74 = (bf16[144,868]{1,0:T(8,128)(2,1)S(1)}, bf16[144,868]{1,0:T(8,128)(2,1)S(1)}, u32[]{:S(2)}, u32[]{:S(2)}) collective-permute-start(bf16[144,868]{1,0:T(8,128)(2,1)S(1)} %get-tuple-element.230), channel_id=1, source_target_pairs={{0,24},{1,25},{2,26},{3,27},{4,28},{5,29},{6,30},{7,31},{8,0},{9,1... | collective-permute-start | bytes 749960 | tf_op jit(solution)/shard_map/ppermute | solution.py:399
  (64 other events, 833.2 us)
Sparse Core Ops, SparseCore 0:
  11.5 160.0 all-gather.2

commit v2 on v1

--- a/solution.py
+++ b/solution.py
@@ -122,9 +122,8 @@
     cumul = decay_sums(gate_ref[...], bias_ref[...], chunk)
     cumul_t = jnp.transpose(cumul)
     scaled = cumul + math.log(head_size ** (-0.5))
-    from_start = jnp.exp(scaled)
     last = cumul[chunk - 1 : chunk, :]
-    to_end = jnp.exp(last - cumul)
+    last_scaled = scaled[chunk - 1 : chunk, :]
     whole = jnp.exp(last)
     row_at = lax.broadcasted_iota(jnp.int32, (chunk, chunk), 0)
     col_at = lax.broadcasted_iota(jnp.int32, (chunk, chunk), 1)
@@ -138,22 +137,26 @@
         query = jnp.where(inside, proj_ref[:, start : start + width], 0)
         key = proj_ref[:, features + start : features + start + width]
         value = proj_ref[:, 2 * features + start : 2 * features + start + width]
-        spread = scaled[:, head : head + 1] - cumul_t[head : head + 1, :]
+        scaled_wide = jnp.broadcast_to(scaled[:, head : head + 1], (chunk, LANES))
+        start_wide = jnp.exp(scaled_wide)
+        end_wide = jnp.exp(last_scaled[:, head : head + 1] - scaled_wide)
+        start_wide = jnp.concatenate([start_wide] * (width // LANES), axis=1)
+        end_wide = jnp.concatenate([end_wide] * (width // LANES), axis=1)
+        spread = jnp.concatenate([scaled_wide] * (chunk // LANES), axis=1) - cumul_t[head : head + 1, :]
         weights = jnp.exp(jnp.where(causal, spread, masked_log))
         scores = (dot_nt(query, key) * weights).astype(jnp.bfloat16)
         held = state[head, :width, :width]
         held_low = held.astype(jnp.bfloat16)
         states_ref[0, head, :width, :width] = held_low
-        mixed = dot_nn(scores, value) + from_start[:, head : head + 1] * dot_nn(query, held_low)
+        mixed = dot_nn(scores, value) + start_wide * dot_nn(query, held_low)
         mixed = jnp.where(inside, mixed, 0.0)
         mean_square = jnp.sum(mixed * mixed, axis=1, keepdims=True) / head_size
         ratio = lax.rsqrt(jnp.maximum(mean_square, rms_floor))
-        slope = jnp.where(mean_square > rms_floor, 1.0, jnp.where(mean_square == rms_floor, 0.5, 0.0))
-        ratios = jnp.where(lane_at == head, ratio, ratios)
-        ratios = jnp.where(lane_at == heads + head, slope, ratios)
+        coded = jnp.where(mean_square > rms_floor, -ratio, jnp.where(mean_square == rms_floor, 2.0, 1.0))
+        ratios = jnp.where(lane_at == head, coded, ratios)
         window = normed_ref[rows, start : start + width]
         normed_ref[rows, start : start + width] = jnp.where(inside, mixed * ratio, window)
-        key_end = (jnp.where(inside, key, 0) * to_end[:, head : head + 1]).astype(jnp.bfloat16)
+        key_end = (jnp.where(inside, key, 0) * end_wide).astype(jnp.bfloat16)
         state[head, :width, :width] = held * whole[:, head : head + 1] + dot_tn(key_end, value)
     ratio_ref[...] = ratios
 
@@ -271,9 +274,8 @@
     cumul = decay_sums(gate, bias, chunk)
     cumul_t = jnp.transpose(cumul)
     scaled = cumul + math.log(head_size ** (-0.5))
-    from_start = jnp.exp(scaled)
     last = cumul[chunk - 1 : chunk, :]
-    to_end = jnp.exp(last - cumul)
+    last_scaled = scaled[chunk - 1 : chunk, :]
     whole = jnp.exp(last)
     row_at = lax.broadcasted_iota(jnp.int32, (chunk, chunk), 0)
     col_at = lax.broadcasted_iota(jnp.int32, (chunk, chunk), 1)
@@ -281,7 +283,6 @@
     lane_at = lax.broadcasted_iota(jnp.int32, (1, LANES), 1)
     rows = pl.ds(pl.multiple_of(chunk_at * chunk, chunk), chunk)
     balance = jnp.zeros((chunk, LANES), jnp.float32)
-    outgoing = jnp.zeros((chunk, LANES), jnp.float32)
     through = jnp.zeros((1, LANES), jnp.float32)
     for head in range(heads):
         start, width, offset = head_window(head, head_size)
@@ -291,17 +292,23 @@
         key_in = jnp.where(inside, key, 0)
         value = proj_ref[:, 2 * features + start : 2 * features + start + width]
         value_in = jnp.where(inside, value, 0)
-        start_col = from_start[:, head : head + 1]
-        end_col = to_end[:, head : head + 1]
-        ratio = ratio_ref[:, head : head + 1]
-        slope = ratio_ref[:, heads + head : heads + head + 1]
+        scaled_wide = jnp.broadcast_to(scaled[:, head : head + 1], (chunk, LANES))
+        start_col = jnp.exp(scaled_wide)
+        end_col = jnp.exp(last_scaled[:, head : head + 1] - scaled_wide)
+        start_col = jnp.concatenate([start_col] * (width // LANES), axis=1)
+        end_col = jnp.concatenate([end_col] * (width // LANES), axis=1)
+        coded = jnp.broadcast_to(ratio_ref[:, head : head + 1], (chunk, LANES))
+        ratio = jnp.where(coded < 0.0, -coded, 1.0)
+        ratio = jnp.concatenate([ratio] * (width // LANES), axis=1)
+        slope = jnp.where(coded < 0.0, 1.0, jnp.where(coded > 1.5, 0.5, 0.0)) / head_size
+        slope = jnp.concatenate([slope] * (width // LANES), axis=1)
         normed = jnp.where(inside, normed_ref[rows, start : start + width], 0.0)
         dnorm = jnp.where(inside, dnormed[rows, start : start + width], 0.0)
-        along = jnp.sum(dnorm * normed, axis=1, keepdims=True) * (slope / head_size)
+        along = jnp.sum(dnorm * normed, axis=1, keepdims=True) * slope
         dmixed = (dnorm - normed * along) * ratio
         dmixed_start = (dmixed * start_col).astype(jnp.bfloat16)
         dmixed = dmixed.astype(jnp.bfloat16)
-        spread = scaled[:, head : head + 1] - cumul_t[head : head + 1, :]
+        spread = jnp.concatenate([scaled_wide] * (chunk // LANES), axis=1) - cumul_t[head : head + 1, :]
         weights = jnp.exp(jnp.where(causal, spread, masked_log))
         scores = (dot_nt(query, key) * weights).astype(jnp.bfloat16)
         dscores = (dot_nt(dmixed, value) * weights).astype(jnp.bfloat16)
@@ -314,18 +321,16 @@
         dkey = dkey_inside + dkey_after
         dvalue = dot_tn(scores, dmixed) + end_col * dot_nn(key_in, dnext_low)
         dstate[head, :width, :width] = dnext * whole[:, head : head + 1] + dot_tn(query, dmixed_start)
-        term = jnp.sum(jnp.sum(dnext * held, axis=1, keepdims=True), axis=0, keepdims=True)
+        kept = jnp.sum(dnext * held, axis=0, keepdims=True) * whole[:, head : head + 1]
+        term = jnp.sum(kept + jnp.sum(key_in * dkey_after, axis=0, keepdims=True), axis=1, keepdims=True)
         through = jnp.where(lane_at == head, term, through)
-        balance_one = jnp.sum(query * dquery - key_in * dkey_inside, axis=1, keepdims=True)
+        balance_one = jnp.sum(query * dquery - key_in * dkey, axis=1, keepdims=True)
         balance = jnp.where(lane_at == head, balance_one, balance)
-        outgoing_one = jnp.sum(key_in * dkey_after, axis=1, keepdims=True)
-        outgoing = jnp.where(lane_at == head, outgoing_one, outgoing)
         for place, grad in ((0, dquery), (1, dkey), (2, dvalue)):
             columns = slice(place * features + start, place * features + start + width)
             dproj_ref[:, columns] = jnp.where(inside, grad.astype(dproj_ref.dtype), dproj_ref[:, columns])
     upper = jnp.where(row_at <= col_at, 1.0, 0.0)
-    strict = jnp.where(row_at > col_at, 1.0, 0.0)
-    ddecay = dot_nn(upper, balance, highest) + dot_nn(strict, outgoing, highest) + through * whole
+    ddecay = dot_nn(upper, balance, highest) + through
     dgate = ddecay / (1.0 + jnp.exp(gate + bias)) / normalizer
     dgate_ref[...] = dgate
     dbias_ref[...] += jnp.sum(dgate, axis=0, keepdims=True)
@@ -469,35 +474,43 @@
     return total
 
 
-def add_parts(parts, received):
-    return [add_low(part, received[first]).astype(jnp.bfloat16) for first, part in enumerate(parts)]
-
-
 def cross_sum(joint):
     return send(joint, across_core)
 
 
-def first_sum(parts):
+def first_send(parts, other):
     side = mesh_parts()[1]
-    received = [send(parts[shift], along_first(shift)) for shift in range(1, side)]
+    sent = [add_low(parts[shift], other[shift]).astype(jnp.bfloat16) for shift in range(1, side)]
+    return [send(value, along_first(shift + 1)) for shift, value in enumerate(sent)]
+
+
+def first_add(parts, other, received):
+    side = mesh_parts()[1]
     return [
-        add_low(parts[0][second], *[value[second] for value in received]).astype(jnp.bfloat16)
+        add_low(parts[0][second], other[0, second], *[value[second] for value in received]).astype(jnp.bfloat16)
         for second in range(side)
     ]
 
 
-def second_sum(level):
-    chips, side = mesh_parts()
-    received = [send(level[shift], along_second(shift)) for shift in range(1, side)]
+def second_send(level):
+    side = mesh_parts()[1]
+    return [send(level[shift], along_second(shift)) for shift in range(1, side)]
+
+
+def second_add(level, received):
+    chips = mesh_parts()[0]
     return [
         add_low(level[0][far], *[value[far] for value in received]).astype(jnp.bfloat16)
         for far in range(chips)
     ]
 
 
-def far_sum(level):
+def far_send(level):
     chips = mesh_parts()[0]
-    received = [send(level[shift], along_z(shift)) for shift in range(1, chips)]
+    return [send(level[shift], along_z(shift)) for shift in range(1, chips)]
+
+
+def far_add(level, received):
     return add_low(level[0], *received)
 
 
@@ -514,24 +527,22 @@
     return jnp.concatenate([values[at * height : (at + 1) * height] for at in range(fold)], axis=1)
 
 
-def unfolded(values, fold):
-    width = values.shape[1] // fold
-    return jnp.concatenate([values[:, at * width : (at + 1) * width] for at in range(fold)], axis=0)
-
-
-def sum_everywhere(values):
+def flip_bit(values, bit):
     chips, side = mesh_parts()
-    count = chips * 2 * side * side
-    bit = 1
-    while bit < count:
-
-        def move(z, core, u, v, bit=bit):
-            to = (((z * 2 + core) * side + u) * side + v) ^ bit
-            return to // (2 * side * side), to // (side * side) % 2, to // side % side, to % side
-
-        values = values + send(values, move)
-        bit *= 2
-    return values
+
+    def move(z, core, u, v):
+        to = (((z * 2 + core) * side + u) * side + v) ^ bit
+        return to // (2 * side * side), to // (side * side) % 2, to // side % side, to % side
+
+    return send(values, move)
+
+
+def flip_bits(low, high):
+    bits = []
+    while low < high:
+        bits.append(low)
+        low *= 2
+    return bits
 
 
 def source_place(where, sibling, first, second, far, chips, side):
@@ -676,11 +687,11 @@
 
 
 def gelu_parts(values):
-    inner = gelu_scale * (values + 0.044715 * values * values * values)
-    bent = jnp.tanh(inner)
-    half = 0.5 * (1.0 + bent)
-    slope = half + 0.5 * values * (1.0 - bent * bent) * (gelu_scale * (1.0 + 3 * 0.044715 * values * values))
-    return values * half, slope
+    square = values * values
+    bent = jnp.tanh(values * (gelu_scale + (0.044715 * gelu_scale) * square))
+    half = 0.5 + 0.5 * bent
+    rise = values * (gelu_scale + (3 * 0.044715 * gelu_scale) * square)
+    return values * half, half + half * (1.0 - bent) * rise
 
 
 def middle_kernel(chips, side, where, conv_ref, tokens_ref, cot_ref, mod_ref, bias_ref, gathered, *rest):
@@ -688,7 +699,6 @@
         attended_ref,
         hidden_ref,
         slope_ref,
-        hidden_t_ref,
         normed_t_ref,
         conv_t_ref,
         gradred_ref,
@@ -727,7 +737,6 @@
         low = hidden.astype(jnp.bfloat16)
         hidden_ref[:, span] = low
         slope_ref[:, span] = slope.astype(jnp.bfloat16)
-        hidden_t_ref[span, :] = jnp.transpose(low)
 
 
 def middle_forward(where, conv, tokens, cotangent, mod, bias, gathered, wide):
@@ -754,7 +763,6 @@
             rows_spec(block, features),
             rows_spec(block, hidden),
             rows_spec(block, hidden),
-            across_spec(hidden, block),
             across_spec(features, block),
             across_spec(features, block),
             rows_spec(block, features),
@@ -763,7 +771,6 @@
             shaped((rows, features), jnp.float32),
             shaped((rows, hidden), jnp.bfloat16),
             shaped((rows, hidden), jnp.bfloat16),
-            shaped((hidden, rows), jnp.bfloat16),
             shaped((features, rows), jnp.bfloat16),
             shaped((features, rows), jnp.bfloat16),
             shaped((rows, features), jnp.bfloat16),
@@ -781,8 +788,7 @@
 def middle_back_kernel(
     chips, side, where, hidden_ref, slope_ref, attended_ref, tokens_ref, cot_ref, mod_ref, *rest
 ):
-    count = 2 * side * side
-    gathered, reduce_pieces, rest = rest[0], rest[1 : 1 + count], rest[1 + count :]
+    gathered, reduce_pieces, rest = rest[0], rest[1], rest[2:]
     (
         out_ref,
         gradpre_ref,
@@ -801,48 +807,42 @@
     hidden = hidden_ref.shape[1]
     wide = hidden // columns
     narrow = weight.shape[2] - wide
-    height = reduce_pieces[0].shape[1]
-    fold = reduce_pieces[0].shape[2] // narrow
+    height = reduce_pieces.shape[1]
+    fold = reduce_pieces.shape[2] // narrow
     copies = whole_copies(gathered, weight, sems)
 
     @pl.when(pl.program_id(0) == 0)
     def _():
         biassum_ref[...] = jnp.zeros_like(biassum_ref)
 
-        def staged(turn):
-            sibling, far = turn // chips, turn % chips
-            slot = turn % 2
-            found = []
-            for first in range(side):
-                for second in range(side):
-                    at = first * side + second
-                    block, column = source_place(where, sibling, first, second, far, chips, side)
-                    found.append(
-                        pltpu.make_async_copy(
-                            reduce_pieces[sibling * columns + at].at[far],
-                            stage.at[slot, column],
-                            reduce_sems.at[slot, at],
-                        )
-                    )
-            return block, found
-
-        turns = [staged(turn) for turn in range(2 * chips)]
-        for copy in turns[0][1]:
+        def staged(block):
+            slot = block % 2
+            return [
+                pltpu.make_async_copy(
+                    reduce_pieces.at[block * columns + column],
+                    stage.at[slot, column],
+                    reduce_sems.at[slot, column],
+                )
+                for column in range(columns)
+            ]
+
+        turns = [staged(block) for block in range(2 * chips)]
+        for copy in turns[0]:
             copy.start()
-        for turn, (block, found) in enumerate(turns):
-            if turn + 1 < len(turns):
-                for copy in turns[turn + 1][1]:
+        for block, found in enumerate(turns):
+            if block + 1 < len(turns):
+                for copy in turns[block + 1]:
                     copy.start()
-            if turn == 0:
+            if block == 0:
                 for copy in copies:
                     copy.start()
             for copy in found:
                 copy.wait()
             for at in range(fold):
-                target = pl.ds(pl.multiple_of((block * fold + at) * height, 8), height)
+                target = slice((block * fold + at) * height, (block * fold + at + 1) * height)
                 for column in range(columns):
                     reduce_weight[target, column * narrow : (column + 1) * narrow] = stage[
-                        turn % 2, column, :, at * narrow : (at + 1) * narrow
+                        block % 2, column, :, at * narrow : (at + 1) * narrow
                     ]
 
     cot = cot_ref[...].astype(jnp.float32)
@@ -890,11 +890,11 @@
     columns = side * side
     inner = hidden.shape[1]
     width = gathered.shape[2]
-    depth, narrow = reduce_pieces[0].shape[1:]
+    depth, narrow = reduce_pieces.shape[1:]
     return call(
         functools.partial(middle_back_kernel, chips, side),
         where,
-        (hidden, slope, attended, tokens, cotangent, mod, gathered, *reduce_pieces),
+        (hidden, slope, attended, tokens, cotangent, mod, gathered, reduce_pieces),
         (steps,),
         [
             rows_spec(block, inner),
@@ -904,7 +904,7 @@
             rows_spec(block, features),
             mod_spec(features, steps),
         ]
-        + any_specs(1 + len(reduce_pieces)),
+        + any_specs(2),
         [
             rows_spec(block, features),
             rows_spec(block, inner),
@@ -1003,160 +1003,245 @@
     )
 
 
-def target_core(where, sibling):
-    return 1 - where[CORE_AT] if sibling else where[CORE_AT]
-
-
 def target_block(where, sibling, far, chips):
-    return 2 * lax.rem(where[Z_AT] + far, chips) + target_core(where, sibling)
-
-
-def target_column(where, sibling, first, second, side):
-    core = target_core(where, sibling)
+    core = 1 - where[CORE_AT] if sibling else where[CORE_AT]
+    return 2 * lax.rem(where[Z_AT] + far, chips) + core
+
+
+def target_column(where, first, second, side):
+    core = where[CORE_AT]
     to_u = lax.rem(where[U_AT] + jnp.where(core == 0, first, second), side)
     to_v = lax.rem(where[V_AT] + jnp.where(core == 0, second, first), side)
     return to_u * side + to_v
 
 
-def relative_column(where, sibling, column, side):
-    core = target_core(where, sibling)
+def relative_column(where, column, side):
+    core = where[CORE_AT]
     by_u = lax.rem(column // side - where[U_AT] + side, side)
     by_v = lax.rem(column % side - where[V_AT] + side, side)
     return jnp.where(core == 0, by_u, by_v), jnp.where(core == 0, by_v, by_u)
 
 
-def grads_by_column_kernel(side, depth, fars, sibling, added, where, *rest):
-    lefts, rest = rest[:fars], rest[fars:]
-    right_ref, rest = rest[0], rest[1:]
-    received, outs = (rest[0], rest[1:]) if added else (None, rest)
-    product = dot_nn(jnp.concatenate([left[...] for left in lefts], axis=0), right_ref[...])
-
-    def store(out):
-        for far in range(fars):
-            value = product[far * depth : (far + 1) * depth]
-            if added:
-                value = value + received[0, 0, far].astype(jnp.float32)
-            out[far] = value.astype(jnp.bfloat16)
-
-    if sibling:
-        store(outs[0].at[0, 0])
-        return
+def grads_product(left, right, chips):
+    product = dot_nn(left, right)
+    return product.reshape(chips, product.shape[0] // chips, product.shape[1]).astype(jnp.bfloat16)
+
+
+def stack_lefts(lefts, left_all):
+    depth = lefts[0].shape[0]
+    for at, left in enumerate(lefts):
+        left_all[at * depth : (at + 1) * depth, :] = left[...]
+
+
+def grads_by_column_kernel(side, chips, where, *rest):
+    lefts, right_ref, other, rest = rest[: 2 * chips], rest[2 * chips], rest[2 * chips + 1], rest[2 * chips + 2 :]
+    outs, left_all = rest[:side], rest[side]
+    half = left_all.shape[0] // 2
+
+    @pl.when(pl.program_id(0) == 0)
+    def _():
+        stack_lefts(lefts, left_all)
+
+    other[0, 0] = grads_product(left_all[half:, :], right_ref[...], chips)
     for first in range(side):
 
         @pl.when(pl.program_id(0) // side == first)
         def _(first=first):
-            store(outs[first].at[0])
-
-
-def grads_by_row_kernel(side, depth, fars, fold, sibling, added, extra, where, *rest):
-    lefts, rest = rest[:fars], rest[fars:]
-    right_ref, rest = rest[0], rest[1:]
+            outs[first][0] = grads_product(left_all[:half, :], right_ref[...], chips)
+
+
+def grads_joint_kernel(blocks, aligned, where, left_ref, small_left_ref, right_ref, small_right_ref, out, *scratch):
+    small = scratch[0]
+    wide = scratch[1].shape[1] if not aligned else right_ref.shape[1]
+    narrow = small.shape[1]
+    count = small_right_ref.shape[1] // narrow
+    for column in range(count):
+
+        @pl.when(pl.program_id(0) == column)
+        def _(column=column):
+            small[...] = small_right_ref[:, column * narrow : (column + 1) * narrow]
+            if not aligned:
+                scratch[1][...] = right_ref[:, column * wide : (column + 1) * wide]
+
+    right = right_ref if aligned else scratch[1]
+    out[:, 0, :, :wide] = grads_product(left_ref[...], right[...], blocks)
+    out[:, 0, :, wide:] = grads_product(small_left_ref[...], small[...], blocks)
+
+
+def grads_joint(where, left_t, right, small_left_t, small_right):
+    chips, side = mesh_parts()
+    columns, blocks = side * side, 2 * chips
+    height, rows = left_t.shape
+    depth = height // blocks
+    wide, narrow = right.shape[1] // columns, small_right.shape[1] // columns
+    aligned = wide % LANES == 0
+    fixed = lambda at, where: (0, 0)
+    scratch = [pltpu.VMEM((rows, narrow), jnp.bfloat16)]
+    if not aligned:
+        scratch.append(pltpu.VMEM((rows, wide), jnp.bfloat16))
+    found = call(
+        functools.partial(grads_joint_kernel, blocks, aligned),
+        where,
+        (left_t, small_left_t, right, small_right),
+        (columns,),
+        [
+            pl.BlockSpec(left_t.shape, fixed),
+            pl.BlockSpec(small_left_t.shape, fixed),
+            pl.BlockSpec((rows, wide), lambda at, where: (0, at)) if aligned else pl.BlockSpec(right.shape, fixed),
+            pl.BlockSpec(small_right.shape, fixed),
+        ],
+        pl.BlockSpec((blocks, 1, depth, wide + narrow), lambda at, where: (0, at, 0, 0)),
+        shaped((blocks, columns, depth, wide + narrow), jnp.bfloat16),
+        scratch,
+        "grads_joint",
+        2 * rows * height * columns * (wide + narrow),
+        30 * 10**6,
+    )
+    return found.reshape(blocks * columns, depth, wide + narrow)
+
+
+def grads_by_row_kernel(side, chips, extra, where, *rest):
+    lefts, right_ref, rest = rest[: 2 * chips], rest[2 * chips], rest[2 * chips + 1 :]
     if extra:
         extra_ref, rest = rest[0], rest[1:]
-    received, rest = (rest[0], rest[1:]) if added else (None, rest)
-    outs, product, small = rest[:-2], rest[-2], rest[-1]
-    if sibling:
-        outs = [outs[0].at[first] for first in range(side)]
+    other, outs, left_all, both = rest[0], rest[1 : 1 + side], rest[1 + side], rest[2 + side]
     columns = side * side
     wide = right_ref.shape[1] // columns
-    width = outs[0].shape[-1]
-    left = jnp.concatenate([piece[...] for piece in lefts], axis=0)
-    product[...] = dot_nn(left, right_ref[...])
-    if extra:
-        small[...] = dot_nn(left, extra_ref[...].astype(jnp.bfloat16))
+    narrow = both.shape[1] - wide
+    half = left_all.shape[0] // 2
+    stack_lefts(lefts, left_all)
     for column in range(columns):
-        by_first, by_second = relative_column(where, sibling, column, side)
+        by_first, by_second = relative_column(where, column, side)
+        both[:, :wide] = right_ref[:, column * wide : (column + 1) * wide]
+        if extra:
+            both[:, wide:] = extra_ref[:, column * narrow : (column + 1) * narrow].astype(jnp.bfloat16)
+        other[by_second, by_first] = grads_product(left_all[half:, :], both[...], chips)
         for first in range(side):
 
             @pl.when(by_first == first)
-            def _(first=first, column=column, by_second=by_second):
-                for far in range(fars):
-                    height = depth // fold
-                    for at in range(fold):
-                        span = slice(far * depth + at * height, far * depth + (at + 1) * height)
-                        lanes = slice(at * wide, (at + 1) * wide)
-                        value = product[span, column * wide : (column + 1) * wide]
-                        if added:
-                            value = value + received[first, by_second, far, :, lanes].astype(jnp.float32)
-                        outs[first][by_second, far, :, lanes] = value.astype(jnp.bfloat16)
-                    if extra:
-                        span = slice(far * depth, (far + 1) * depth)
-                        narrow = width - wide
-                        value = small[span, column * narrow : (column + 1) * narrow]
-                        if added:
-                            value = value + received[first, by_second, far, :, wide:].astype(jnp.float32)
-                        outs[first][by_second, far, :, wide:] = value.astype(jnp.bfloat16)
-
-
-def weight_grads(where, left_t, right, sibling, received=None, extra=None, narrow=0, fold=1):
+            def _(first=first, by_second=by_second):
+                outs[first][by_second] = grads_product(left_all[:half, :], both[...], chips)
+
+
+def grads_across_kernel(side, chips, where, right_ref, hidden_ref, other, *rest):
+    outs, right_t, product = rest[:side], rest[side], rest[side + 1]
+    columns = side * side
+    wide = right_ref.shape[1] // columns
+    depth = hidden_ref.shape[1] // 2
+
+    @pl.when(pl.program_id(0) == 0)
+    def _():
+        right_t[...] = jnp.transpose(right_ref[...])
+
+    product[...] = dot_nn(right_t[...], hidden_ref[...]).astype(jnp.bfloat16)
+    for core in range(2):
+        mine = slice(core * depth, (core + 1) * depth)
+        theirs = slice((1 - core) * depth, (2 - core) * depth)
+        for column in range(columns):
+            by_first, by_second = relative_column(where, column, side)
+            span = slice(column * wide, (column + 1) * wide)
+
+            @pl.when(where[CORE_AT] == core)
+            def _(span=span, theirs=theirs, by_first=by_first, by_second=by_second):
+                other[by_second, by_first, 0] = product[span, theirs]
+
+            for first in range(side):
+
+                @pl.when(jnp.logical_and(where[CORE_AT] == core, by_first == first))
+                def _(first=first, span=span, mine=mine, by_second=by_second):
+                    outs[first][by_second, 0] = product[span, mine]
+
+
+def piece_shapes(side, chips, piece):
+    other = shaped((side, side, chips, *piece), jnp.bfloat16)
+    return [other] + [shaped((side, chips, *piece), jnp.bfloat16)] * side
+
+
+def grads_across(where, hidden, right):
+    chips, side = mesh_parts()
+    columns = side * side
+    rows, inner = hidden.shape
+    depth, wide = inner // (2 * chips), right.shape[1] // columns
+    piece = (wide, depth)
+    found = call(
+        functools.partial(grads_across_kernel, side, chips),
+        where,
+        (right, hidden),
+        (chips,),
+        [
+            pl.BlockSpec(right.shape, lambda at, where: (0, 0)),
+            pl.BlockSpec((rows, 2 * depth), lambda at, where: (0, lax.rem(where[Z_AT] + at, chips))),
+        ],
+        [pl.BlockSpec((side, side, 1, *piece), lambda at, where: (0, 0, at, 0, 0))]
+        + [pl.BlockSpec((side, 1, *piece), lambda at, where: (0, at, 0, 0))] * side,
+        piece_shapes(side, chips, piece),
+        [
+            pltpu.VMEM((right.shape[1], rows), jnp.bfloat16),
+            pltpu.VMEM((right.shape[1], 2 * depth), jnp.bfloat16),
+        ],
+        "grads_across",
+        2 * rows * inner * right.shape[1],
+        24 * 10**6,
+    )
+    return found[0], found[1:]
+
+
+def weight_grads(where, left_t, right, extra=None, narrow=0):
     chips, side = mesh_parts()
     columns = side * side
     height, rows = left_t.shape
     depth = height // (2 * chips)
     wide = right.shape[1] // columns
-    width = wide * fold + narrow
-    added = received is not None
-    piece = (depth // fold, width)
-    flops = 2 * rows * (height // 2) * columns * width
-    moved = 2 * (rows * height // 2 + rows * columns * width + height // 2 * columns * width * (2 if added else 1))
-
-    def left_spec(far, moving):
-        return pl.BlockSpec(
-            (depth, rows),
-            lambda at, where: (target_block(where, sibling, at if moving else far, chips), 0),
-        )
-
-    if wide % LANES == 0 and extra is None and fold == 1 and depth < 2 * LANES:
+    piece = (depth, wide + narrow)
+
+    def left_spec(sibling, far):
+        return pl.BlockSpec((depth, rows), lambda at, where: (target_block(where, sibling, far, chips), 0))
+
+    specs = [left_spec(sibling, far) for sibling in (False, True) for far in range(chips)]
+    args = [left_t] * (2 * chips) + [right]
+    if wide % LANES == 0 and extra is None:
         steps = columns
-        specs = [left_spec(far, False) for far in range(chips)]
         specs.append(
             pl.BlockSpec(
-                (rows, wide),
-                lambda at, where: (0, target_column(where, sibling, at // side, lax.rem(at, side), side)),
+                (rows, wide), lambda at, where: (0, target_column(where, at // side, lax.rem(at, side), side))
             )
         )
-        args = [left_t] * chips + [right]
-        joint = pl.BlockSpec((1, 1, chips, *piece), lambda at, where: (at // side, lax.rem(at, side), 0, 0, 0))
+        joint = pl.BlockSpec((1, 1, chips, *piece), lambda at, where: (lax.rem(at, side), at // side, 0, 0, 0))
 
         def out_spec(first):
             return pl.BlockSpec(
                 (1, chips, *piece), lambda at, where: (jnp.clip(at - first * side, 0, side - 1), 0, 0, 0)
             )
 
-        kernel = functools.partial(grads_by_column_kernel, side, depth, chips, sibling, added)
-        scratch = []
+        kernel = functools.partial(grads_by_column_kernel, side, chips)
+        scratch = [pltpu.VMEM((height, rows), jnp.bfloat16)]
     else:
-        moving = depth >= 2 * LANES
-        fars = 1 if moving else chips
-        steps = chips if moving else 1
-        specs = [left_spec(far, moving) for far in range(fars)]
+        steps = 1
         specs.append(pl.BlockSpec(right.shape, lambda at, where: (0, 0)))
-        args = [left_t] * fars + [right]
         if extra is not None:
             specs.append(pl.BlockSpec(extra.shape, lambda at, where: (0, 0)))
             args.append(extra)
-        joint = pl.BlockSpec((side, side, fars, *piece), lambda at, where: (0, 0, at, 0, 0))
+        joint = pl.BlockSpec((side, side, chips, *piece), lambda at, where: (0, 0, 0, 0, 0))
 
         def out_spec(first):
-            return pl.BlockSpec((side, fars, *piece), lambda at, where: (0, at, 0, 0))
-
-        kernel = functools.partial(
-            grads_by_row_kernel, side, depth, fars, fold, sibling, added, extra is not None
-        )
-        scratch = [
-            pltpu.VMEM((fars * depth, right.shape[1]), jnp.float32),
-            pltpu.VMEM((fars * depth, LANES), jnp.float32),
-        ]
-    if added:
-        specs.append(joint)
-        args.append(received)
-    if sibling:
-        outs, arrays = [joint], [shaped((side, side, chips, *piece), jnp.bfloat16)]
-    else:
-        outs = [out_spec(first) for first in range(side)]
-        arrays = [shaped((side, chips, *piece), jnp.bfloat16)] * side
-    found = call(kernel, where, args, (steps,), specs, outs, arrays, scratch, "weight_grads", flops, moved)
-    return found[0] if sibling else found
+            return pl.BlockSpec((side, chips, *piece), lambda at, where: (0, 0, 0, 0))
+
+        kernel = functools.partial(grads_by_row_kernel, side, chips, extra is not None)
+        scratch = [pltpu.VMEM((height, rows), jnp.bfloat16), pltpu.VMEM((rows, wide + narrow), jnp.bfloat16)]
+    found = call(
+        kernel,
+        where,
+        args,
+        (steps,),
+        specs,
+        [joint] + [out_spec(first) for first in range(side)],
+        piece_shapes(side, chips, piece),
+        scratch,
+        "weight_grads",
+        2 * rows * height * columns * wide,
+        2 * (rows * height + rows * columns * wide + height * columns * wide),
+    )
+    return found[0], found[1:]
 
 
 def pick(values, at):
@@ -1235,68 +1320,71 @@
     middle_pieces = lax.all_gather(
         jnp.concatenate([expand_weight, output_weight], axis=1), ("fsdp", "dp"), axis=0, tiled=False
     )
-    attend_first, reduce_shard = tied(attend_pieces[0], folded(reduce_weight, fold))
-    attend_pieces[0] = attend_first
-    reduce_far = far_pieces(reduce_shard)
 
     projected, gate_logit, normed_in_t = front_forward(
         where, tokens, modulation, attend_pieces, attend_weight.shape[1]
     )
-    projected, reduce_far = tied(projected, reduce_far)
-    reduce_level = first_pieces(jnp.stack(reduce_far))
+    projected, reduce_shard = tied(projected, folded(reduce_weight, fold))
+    reduce_pieces = lax.all_gather(reduce_shard, ("fsdp", "dp"), axis=0, tiled=False)
     bias_wide = jnp.pad(forget_bias[None, :], ((0, 0), (0, LANES - heads)))
     conv_low, normed_heads, ratios, states = attention_forward(
         resolution, projected, gate_logit, bias_wide, conv_taps, heads
     )
-    conv_low, reduce_level = tied(conv_low, reduce_level)
-    reduce_pieces = second_pieces(reduce_level)
-    attended, hidden, slope, hidden_t, normed_mid_t, conv_t, grad_reduced = middle_forward(
+    attended, hidden, slope, normed_mid_t, conv_t, grad_reduced = middle_forward(
         where, conv_low, tokens, cotangent, modulation, expandbias_whole, middle_pieces, expand_weight.shape[1]
     )
-    hidden_t, reduce_pieces = tied(hidden_t, reduce_pieces)
-    reduce_pieces = core_pieces(reduce_pieces)
-    reduce_other = cross_sum(weight_grads(where, hidden_t, grad_reduced, True, fold=fold))
-    reduce_parts = weight_grads(where, hidden_t, grad_reduced, False, fold=fold)
+    across = (2 * reduce_weight.shape[0]) % LANES == 0
+    if across:
+        reduce_other, reduce_parts = grads_across(where, hidden, grad_reduced)
+    else:
+        reduce_other, reduce_parts = weight_grads(where, hidden.T, grad_reduced)
+    reduce_other = cross_sum(reduce_other)
     hidden, reduce_parts, reduce_other = tied(hidden, reduce_parts, reduce_other)
-    reduce_level = first_sum(add_parts(reduce_parts, reduce_other))
-    block_out, grad_preact, grad_after, grad_attended, grad_conv, middle_sums, bias_sums = middle_backward(
+    moving = first_send(reduce_parts, reduce_other)
+    back = middle_backward(
         where, hidden, slope, attended, tokens, cotangent, modulation, middle_pieces, reduce_pieces
     )
-    grad_preact, reduce_level = tied(grad_preact, reduce_level)
-    reduce_level = second_sum(reduce_level)
-    expand_other = weight_grads(where, normed_mid_t, grad_preact, True)
-    expand_other, conv_t = tied(expand_other, conv_t)
-    expand_other = cross_sum(expand_other)
-    output_other = cross_sum(weight_grads(where, conv_t, grad_attended, True))
-    expand_parts = weight_grads(where, normed_mid_t, grad_preact, False, expand_other)
-    output_parts = weight_grads(where, conv_t, grad_attended, False, output_other)
-    grad_conv, expand_parts, output_parts, reduce_level = tied(grad_conv, expand_parts, output_parts, reduce_level)
-    reduce_grad = far_sum(reduce_level)
-    expand_level = first_sum(expand_parts)
-    output_level = first_sum(output_parts)
-    grad_projected, grad_gate, forgetbias_local, taps_local = attention_backward(
+    back, moving = tied(back, moving)
+    block_out, grad_preact, grad_after, grad_attended, grad_conv, middle_sums, bias_sums = back
+    reduce_level = first_add(reduce_parts, reduce_other, moving)
+    moving = second_send(reduce_level)
+    joint = grads_joint(where, normed_mid_t, grad_preact, conv_t, grad_attended)
+    joint, moving = tied(joint, moving)
+    reduce_level = second_add(reduce_level, moving)
+    joint = lax.psum_scatter(joint, ("fsdp", "dp"), scatter_dimension=0, tiled=True)
+    grad_conv, reduce_level = tied(grad_conv, reduce_level)
+    moving = far_send(reduce_level)
+    back = attention_backward(
         resolution, projected, gate_logit, bias_wide, conv_taps, normed_heads, ratios, states, grad_conv, heads
     )
-    grad_projected, expand_level, output_level, reduce_grad = tied(
-        grad_projected, expand_level, output_level, reduce_grad
-    )
-    reduce_grad = unfolded(reduce_grad, fold)
-    expand_level = second_sum(expand_level)
-    output_level = second_sum(output_level)
-    tokens_grad, front_sums = front_backward(
+    back, moving = tied(back, moving)
+    grad_projected, grad_gate, forgetbias_local, taps_local = back
+    reduce_grad = far_add(reduce_level, moving)
+    reduce_grad = reduce_grad.T if across else reduce_grad
+    sums = jnp.concatenate(
+        [
+            taps_local,
+            jnp.pad(forgetbias_local, ((0, 0), (0, features - LANES))),
+            bias_sums.reshape(-1, features),
+        ],
+        axis=0,
+    )
+    bits = flip_bits(1, columns)
+    for bit in bits[:-1]:
+        sums = sums + flip_bit(sums, bit)
+    attend_other, attend_parts = weight_grads(
+        where, normed_in_t, grad_projected, grad_gate, heads // columns
+    )
+    attend_other, attend_parts, grad_projected, sums = tied(attend_other, attend_parts, grad_projected, sums)
+    attend_other = cross_sum(attend_other)
+    sums_moving = flip_bit(sums, bits[-1])
+    back = front_backward(
         where, grad_projected, grad_gate, grad_after, tokens, modulation, attend_pieces
     )
-    grad_projected, front_sums, expand_level, output_level = tied(
-        grad_projected, front_sums, expand_level, output_level
-    )
-    narrow = heads // columns
-    attend_other = cross_sum(weight_grads(where, normed_in_t, grad_projected, True, None, grad_gate, narrow))
-    attend_parts = weight_grads(where, normed_in_t, grad_projected, False, None, grad_gate, narrow)
-    attend_level = first_sum(add_parts(attend_parts, attend_other))
-    expand_grad = far_sum(expand_level)
-    output_grad = far_sum(output_level)
-    attend_both = far_sum(second_sum(attend_level))
-    attend_grad, forget_grad = attend_both[:, : attend_weight.shape[1]], attend_both[:, attend_weight.shape[1] :]
+    back, attend_other, sums_moving = tied(back, attend_other, sums_moving)
+    tokens_grad, front_sums = back
+    sums = sums + sums_moving
+    attend_moving = first_send(attend_parts, attend_other)
 
     middle_sums = jnp.sum(middle_sums.reshape(QUARTERS, -1, 8, features), axis=1)
     grad_modulation = jnp.concatenate([front_sums[:, :2], middle_sums[:, :4]], axis=1)
@@ -1306,14 +1394,23 @@
     )
     grad_modulation = grad_modulation.reshape(slots, columns, own_columns).astype(jnp.bfloat16)
     grad_modulation = jnp.swapaxes(grad_modulation, 0, 1)
-    rows_here = [pick(grad_modulation, dp_at)]
-    for shift in range(1, columns):
-        rows_here.append(send(pick(grad_modulation, (dp_at + shift) % columns), along_dp(shift)))
-    rows_here = jnp.concatenate(rows_here, axis=0)
+    rows_here = [
+        send(pick(grad_modulation, (dp_at + shift) % columns), along_dp(shift)) for shift in range(1, columns)
+    ]
+    rows_here, attend_moving = tied(rows_here, attend_moving)
+    attend_level = first_add(attend_parts, attend_other, attend_moving)
+    attend_moving = second_send(attend_level)
+    rows_here = jnp.concatenate([pick(grad_modulation, dp_at)] + rows_here, axis=0)
+    sums_moving = flip_bit(sums, columns)
     rows_here = jnp.concatenate(
         [rows_here] + [send(rows_here, along_z(shift)) for shift in range(1, chips)], axis=0
     )
-    rows_here = jnp.concatenate([rows_here, send(rows_here, across_core)], axis=0)
+    rows_other = send(rows_here, across_core)
+    rows_other, attend_moving, sums_moving = tied(rows_other, attend_moving, sums_moving)
+    attend_level = second_add(attend_level, attend_moving)
+    attend_moving = far_send(attend_level)
+    sums = sums + sums_moving
+    rows_here = jnp.concatenate([rows_here, rows_other], axis=0)
     order = []
     for sibling in range(2):
         for far in range(chips):
@@ -1338,35 +1435,29 @@
         rows_here, modulate_weight, (((1,), (1,)), ((), ())), preferred_element_type=jnp.float32
     )
     grad_cond = jnp.moveaxis(grad_cond.reshape(blocks, columns, slots, own_rows), 1, 0)
-    cond_sum = grad_cond[0]
-    for shift in range(1, columns):
-        cond_sum = cond_sum + send(grad_cond[shift], along_dp(-shift))
-    cond_sum = cond_sum.reshape(2, chips, slots, own_rows)
-    cond_parts = []
-    for sibling in range(2):
-        for far in range(chips):
-            def move(z, core, u, v, sibling=sibling, far=far):
-                return (z - far) % chips, core ^ sibling, u, v
-            part = cond_sum[sibling, far]
-            cond_parts.append(part if sibling + far == 0 else send(part, move))
-    cond_parts = jnp.stack(cond_parts)
+    bits = flip_bits(2 * columns, blocks * columns)
+    sums_moving = flip_bit(sums, bits[0])
+    cond_sum = [send(grad_cond[shift], along_dp(-shift)) for shift in range(1, columns)]
+    cond_sum, attend_moving, sums_moving = tied(cond_sum, attend_moving, sums_moving)
+    attend_both = far_add(attend_level, attend_moving)
+    attend_grad, forget_grad = attend_both[:, : attend_weight.shape[1]], attend_both[:, attend_weight.shape[1] :]
+    sums = sums + sums_moving
+    for bit in bits[1:]:
+        sums = sums + flip_bit(sums, bit)
+    cond_sum = sum(cond_sum, grad_cond[0]).reshape(2, chips, slots, own_rows)
+    cond_sum = jnp.stack([cond_sum[0], send(cond_sum[1], across_core)], axis=1)
+    joint = joint[0].astype(jnp.float32)
+    expand_grad, output_grad = joint[:, : expand_weight.shape[1]], joint[:, expand_weight.shape[1] :]
+    cond_parts = jnp.concatenate(
+        [cond_sum[0]] + [send(cond_sum[far], along_z(-far)) for far in range(1, chips)], axis=0
+    )
     cond_columns_all = []
     for block in range(blocks):
         sibling = jnp.abs(block % 2 - core_at)
-        cond_columns_all.append(pick(cond_parts, sibling * chips + (block // 2 - z_at) % chips))
+        cond_columns_all.append(pick(cond_parts, (block // 2 - z_at) % chips * 2 + sibling))
     grad_cond_low = jnp.concatenate(cond_columns_all, axis=1)
     conditions_grad = silu_back(grad_cond_low)[0].astype(jnp.bfloat16)
 
-    sums = jnp.concatenate(
-        [
-            taps_local,
-            jnp.pad(forgetbias_local, ((0, 0), (0, features - LANES))),
-            bias_sums.reshape(-1, features),
-        ],
-        axis=0,
-    )
-    sums, front_sums = tied(sums, front_sums)
-    sums = sum_everywhere(sums)
     taps_count = conv_taps.shape[0]
     taps_grad = sums[:taps_count]
     forgetbias_grad = sums[taps_count, :heads]

time: 716 us -> 601 us (0.84)
  Pallas kernels: 358 us -> 311 us
  waiting for transfers between devices: 154 us -> 113 us
  starting transfers between devices: 101 us -> 81.2 us
  other arithmetic: 45.5 us -> 36.5 us
    ppermute x86 -> x61, waiting for transfers between devices: 154 us -> 113 us  [send(): return lax.ppermute(values, ('fsdp', 'dp'), pairs)]
    pallas_call x12 -> x7, Pallas kernels: 243 us -> 219 us  [call(): pl.pallas_call(kernel, grid_spec=pltpu.PrefetchScalarGridSpec(num_scalar_...]
    ppermute x86 -> x61, starting transfers between devices: 101 us -> 80.6 us  [send(): return lax.ppermute(values, ('fsdp', 'dp'), pairs)]
    pallas_call x1, Pallas kernels: 43.3 us -> 30.3 us  [attention_forward(): pl.pallas_call(functools.partial(attention_forward_kernel, heads, head_si...]
    pallas_call x1, Pallas kernels: 71.6 us -> 62.2 us  [attention_backward(): pl.pallas_call(functools.partial(attention_backward_kernel, heads, head_s...]
    convert_element_type x10 -> x7, other arithmetic: 27.3 us -> 21.7 us  [the longest x2 9.12 us: first_send(): add_low(parts[shift], other[shift]).astype(jnp.bfloat16)]
  transfers between devices with their start and end apart: 87 -> 64, of which waited for: 33 -> 19; matrix products, arithmetic and copies ran while one was open for 7% -> 10% of each run, Pallas kernels for 43% -> 53%
where the time goes in v2:
time: 601 us; the launch traced here: 593 us
  Pallas kernels  311 us (52%)
  waiting for transfers between devices  113 us (19%)
  starting transfers between devices  81.2 us (14%)
  other arithmetic  36.5 us (6%)
  local copies, waits for them, and re-layouts  31.3 us (5%)
  between operations  15.8 us (3%)
    pallas_call x7, Pallas kernels, call(): pl.pallas_call(kernel, grid_spec=pltpu.PrefetchScalarGridSpec(num_scalar_...  219 us
    ppermute x61, waiting for transfers between devices, send(): return lax.ppermute(values, ('fsdp', 'dp'), pairs)  113 us
    ppermute x61, starting transfers between devices, send(): return lax.ppermute(values, ('fsdp', 'dp'), pairs)  80.6 us
    pallas_call x1, Pallas kernels, attention_backward(): pl.pallas_call(functools.partial(attention_backward_kernel, heads, head_s...  62.2 us
    pallas_call x1, Pallas kernels, attention_forward(): pl.pallas_call(functools.partial(attention_forward_kernel, heads, head_si...  30.3 us
  transfers between devices with their start and end apart: 64, of which 19 were waited for; matrix products, arithmetic and copies ran while one was open for 10% of the time, Pallas kernels for 53%

profile of v2, /device:TPU:0, one launch (start us, length us, event | category | flops | bytes accessed | tf_op | source)
XLA Modules:
  0.0 593.0 jit_solution(1438723054153356838)
XLA Ops:
  7.2 1.9 pad_maximum_fusion.1
  9.9 1.4 concatenate.49
  11.4 5.1 collective-permute-start.2
  19.3 2.0 collective-permute-start.18
  21.3 1.5 collective-permute-start.17
  22.8 2.4 collective-permute-start.19
  25.3 1.6 collective-permute-start.4
  26.9 1.5 collective-permute-start.3
  30.9 1.5 collective-permute-start.5
  32.5 2.4 collective-permute-done.5
  39.5 10.5 %collective-permute-done.18 = bf16[144,868]{1,0:T(8,128)(2,1)S(1)} collective-permute-done((bf16[144,868]{1,0:T(8,128)(2,1)S(1)}, bf16[144,868]{1,0:T(8,128)(2,1)S(1)}, u32[]{:S(2)}, u32[]{:S(2)}) %collective-permute-start.18) | collective-permute-done | bytes 250016 | tf_op jit(solution)/shard_map/ppermute | solution.py:404
  50.2 1.6 collective-permute-start.21
  52.6 1.5 collective-permute-start.20
  55.9 24.6 %collective-permute-done.21.rest_2_ = bf16[4,144,868]{2,1,0:T(8,128)(2,1)S(1)} collective-permute-done((bf16[4,144,868]{2,1,0:T(8,128)(2,1)S(1)}, bf16[4,144,868]{2,1,0:T(8,128)(2,1)S(1)}, u32[]{:S(2)}, u32[]{:S(2)}) %collective-permute-start.21) | collective-permute-done | bytes 999968 | tf_op jit(solution)/shard_map/ppermute | solution.py:404
  80.5 1.5 collective-permute-start.22
  82.0 5.3 collective-permute-start.11
  87.4 3.2 collective-permute-start.12
  91.8 2.6 collective-permute-done.13
  94.4 2.4 collective-permute-done.12
  98.4 1.7 collective-permute-start.15
  100.0 3.8 collective-permute-start.23
  105.0 2.1 collective-permute-start.25
  107.7 1.4 fusion.62
  113.0 20.7 %front_forward.1 = (bf16[1024,3456]{1,0:T(8,128)(2,1)}, f32[1024,128]{1,0:T(8,128)}, bf16[1152,1024]{1,0:T(8,128)(2,1)}) custom-call(s32[5]{0:T(128)} %stack.302.where, bf16[1024,1152]{1,0:T(8,128)(2,1)} %tokens_ref.7, f32[4,8,1152]{2,1,0:T(8,128)} %pad.12.mod_ref, bf16[4,144,868]{2,1,0:T(8,128)(2,1)} %copy-done.1, ...), custom_call_target="tpu_custom_call" | custom-call | flops 163829520 | bytes 400000 | tf_op jit(solution)/shard_map/front_forward/pallas_call | solution.py:649
  135.5 30.3 %attention_forward.1 = (bf16[1024,1152]{1,0:T(8,128)(2,1)}, f32[1024,1152]{1,0:T(8,128)}, f32[1024,128]{1,0:T(8,128)}, bf16[4,16,256,256]{3,2,1,0:T(8,128)(2,1)}) custom-call(s32[1]{0:T(128)S(6)} %copy.102.flag_ref, bf16[1024,3456]{1,0:T(8,128)(2,1)} %get-tuple-element.97.proj_ref, f32[1024,128]{1,0:T(8,128)} %get-tuple-element.98.gate_ref, ...), custom_call_target="tpu_custom_call" | custom-call | flops 340000000 | bytes 400000 | tf_op jit(solution)/shard_map/attention_forward/pallas_call | solution.py:188
  165.9 40.0 %middle_forward.1 = (f32[1024,1152]{1,0:T(8,128)}, bf16[1024,4608]{1,0:T(8,128)(2,1)}, bf16[1024,4608]{1,0:T(8,128)(2,1)}, bf16[1152,1024]{1,0:T(8,128)(2,1)}, b...) custom-call(s32[5]{0:T(128)} %stack.302.where, bf16[1024,1152]{1,0:T(8,128)(2,1)} %get-tuple-element.99.conv_ref, ...), custom_call_target="tpu_custom_call" | custom-call | flops 271790912 | bytes 1200000 | tf_op jit(solution)/shard_map/middle_forward/pallas_call | solution.py:649
  205.8 22.5 %grads_across.1 = (bf16[2,2,4,288,576]{4,3,2,1,0:T(8,128)(2,1)}, bf16[2,4,288,576]{3,2,1,0:T(8,128)(2,1)}, bf16[2,4,288,576]{3,2,1,0:T(8,128)(2,1)}) custom-call(s32[5]{0:T(128)} %stack.302.where, bf16[1024,1152]{1,0:T(8,128)(2,1)} %get-tuple-element.101.right_ref, bf16[1024,4608]{1,0:T(8,128)(2,1)} %get-tuple-element.105.hidden_ref), custom_call_target="tpu_custom_call" | custom-call | flops 217432720 | bytes 480000 | tf_op jit(solution)/shard_map/grads_across/pallas_call | solution.py:649
  228.7 11.0 %collective-permute-done.27 = bf16[2,2,4,288,576]{4,3,2,1,0:T(8,128)(2,1)S(1)} collective-permute-done((bf16[2,2,4,288,576]{4,3,2,1,0:T(8,128)(2,1)}, bf16[2,2,4,288,576]{4,3,2,1,0:T(8,128)(2,1)S(1)}, u32[]{:S(2)}, u32[]{:S(2)}) %collective-permute-start.27) | collective-permute-done | bytes 5308448 | tf_op jit(solution)/shard_map/ppermute | solution.py:404
  239.8 6.2 %fusion = bf16[2,4,288,576]{3,2,1,0:T(8,128)(2,1)} fusion(bf16[2,4,288,576]{3,2,1,0:T(8,128)(2,1)} %get-tuple-element.116, bf16[2,2,4,288,576]{4,3,2,1,0:T(8,128)(2,1)S(1)} %collective-permute-done.27), kind=kLoop, calls=%fused_computation.1 | loop fusion | flops 5308416 | bytes 7962624 | tf_op jit(solution)/shard_map/convert_element_type | solution.py:483
  246.0 2.6 collective-permute-start.28
  248.6 68.2 %middle_backward.1 = (bf16[1024,1152]{1,0:T(8,128)(2,1)}, bf16[1024,4608]{1,0:T(8,128)(2,1)}, f32[1024,1152]{1,0:T(8,128)}, bf16[1024,1152]{1,0:T(8,128)(2,1)}, ...) custom-call(s32[5]{0:T(128)} %stack.302.where, bf16[1024,4608]{1,0:T(8,128)(2,1)} %get-tuple-element.105.hidden_ref, ...), custom_call_target="tpu_custom_call" | custom-call | flops 652298176 | bytes 1600000 | tf_op jit(solution)/shard_map/middle_backward/pallas_call | solution.py:649
  316.8 1.6 copy-done.4
  318.5 4.9 fusion.2
  323.4 25.2 %grads_joint.1 = bf16[8,4,144,1440]{3,2,1,0:T(8,128)(2,1)} custom-call(s32[5]{0:T(128)} %stack.302.where, bf16[1152,1024]{1,0:T(8,128)(2,1)} %get-tuple-element.126.left_ref, bf16[1152,1024]{1,0:T(8,128)(2,1)} %get-tuple-element.127.small_left_ref, bf16[1024,4608]{1,0:T(8,128)(2,1)} %get-tuple-element.128.right_ref, ...), custom_call_target="tpu_custom_call" | custom-call | flops 271790912 | bytes 600000 | tf_op jit(solution)/shard_map/grads_joint/pallas_call | solution.py:649
  348.7 1.4 fusion.12
  350.0 1.9 collective-permute-start.30
  352.0 3.6 collective-permute-start.31
  355.6 2.9 collective-permute-start.32
  358.6 62.2 %attention_backward.1 = (bf16[1024,3456]{1,0:T(8,128)(2,1)}, f32[1024,128]{1,0:T(8,128)}, f32[1,128]{1,0:T(1,128)}, f32[9,1152]{1,0:T(8,128)}) custom-call(s32[1]{0:T(128)S(6)} %copy.102.flag_ref, bf16[1024,3456]{1,0:T(8,128)(2,1)} %get-tuple-element.97.proj_ref, f32[1024,128]{1,0:T(8,128)} %get-tuple-element.98.gate_ref, f32[1,128]{1,0:T(1,128)} %pad.13.bias_ref, ...), custom_call_target="tpu_custom_call" | custom-call | flops 760000000 | bytes 800000 | tf_op jit(solution)/shard_map/attention_backward/pallas_call | solution.py:346
  422.1 19.8 %weight_grads.1 = (bf16[2,2,4,144,868]{4,3,2,1,0:T(8,128)(2,1)}, bf16[2,4,144,868]{3,2,1,0:T(8,128)(2,1)}, bf16[2,4,144,868]{3,2,1,0:T(8,128)(2,1)}) custom-call(s32[5]{0:T(128)} %stack.302.where, bf16[1152,1024]{1,0:T(8,128)(2,1)} %get-tuple-element.119.rest_0_.rest_1_.rest_2_.rest_3_.rest_4_.rest_5_.rest_6_.rest_7_, ...), custom_call_target="tpu_custom_call" | custom-call | flops 163074544 | bytes 347996 | tf_op jit(solution)/shard_map/weight_grads/pallas_call | solution.py:649
  442.8 22.5 %front_backward.1 = (bf16[1024,1152]{1,0:T(8,128)(2,1)}, f32[4,8,1152]{2,1,0:T(8,128)}) custom-call(s32[5]{0:T(128)} %stack.302.where, bf16[1024,3456]{1,0:T(8,128)(2,1)} %get-tuple-element.147.rest_8_.gradproj_ref, f32[1024,128]{1,0:T(8,128)} %get-tuple-element.140.rest_9_.gradgate_ref, f32[1024,1152]{1,0:T(8,128)} %get-tuple-element.148.gradafter_ref, ...), custom_call_target="tpu_custom_call" | custom-call | flops 163829520 | bytes 500000 | tf_op jit(solution)/shard_map/front_backward/pallas_call | solution.py:649
  465.3 2.9 fusion.1
  471.0 2.4 collective-permute-start.36
  473.4 1.5 collective-permute-start.38
  476.1 28.6 %collective-permute-done.37 = bf16[4,1728]{1,0:T(4,128)(2,1)S(1)} collective-permute-done((bf16[4,1728]{1,0:T(4,128)(2,1)S(1)}, bf16[4,1728]{1,0:T(4,128)(2,1)S(1)}, u32[]{:S(2)}, u32[]{:S(2)}) %collective-permute-start.37) | collective-permute-done | bytes 13856 | tf_op jit(solution)/shard_map/ppermute | solution.py:404
  504.7 3.8 fusion.4
  508.6 1.5 collective-permute-start.44
  510.9 3.1 collective-permute-start.42
  517.1 5.8 collective-permute-done.41
  522.9 5.5 concatenate.59
  528.4 2.1 add_bitcast_fusion
  531.2 3.4 concatenate.60
  538.7 1.6 collective-permute-start.48
  540.3 2.4 fusion.6
  542.7 1.4 fusion.15
  544.1 1.4 collective-permute-start.46
  546.3 1.4 collective-permute-start.50
  548.3 1.5 collective-permute-start.49
  551.3 1.9 collective-permute-start.47
  555.2 8.1 %collective-permute-done.52 = f32[14,1152]{1,0:T(8,128)S(1)} collective-permute-done((f32[14,1152]{1,0:T(8,128)S(1)}, f32[14,1152]{1,0:T(8,128)S(1)}, u32[]{:S(2)}, u32[]{:S(2)}) %collective-permute-start.52) | collective-permute-done | bytes 64544 | tf_op jit(solution)/shard_map/ppermute | solution.py:404
  563.3 5.7 collective-permute-done.50
  570.5 2.0 collective-permute-start.56
  572.5 1.6 collective-permute-start.55
  578.1 4.2 collective-permute-done.60
  (242 shorter events, 52.2 us)
Async XLA Ops:
  7.2 158.7 %all-gather.5.cloned.1.call-start = ((), (), s32[]{:S(2)}) async-start(), calls=%async_computation.2 | async-start | bytes 14598144 | tf_op jit(solution)/shard_map/all_gather | solution.py:1320
  9.1 239.5 %all-gather.7.cloned.1.call-start = ((), (), s32[]{:S(2)}) async-start(), calls=%async_computation.3 | async-start | bytes 10948608 | tf_op jit(solution)/shard_map/all_gather | solution.py:1328
  11.4 11.4 %collective-permute-start.2 = (bf16[1,4968]{1,0:T(2,128)(2,1)S(1)}, bf16[1,4968]{1,0:T(2,128)(2,1)S(1)}, u32[]{:S(2)}, u32[]{:S(2)}) collective-permute-start(bf16[1,4968]{1,0:T(2,128)(2,1)S(1)} %reshape.435), channel_id=1, source_target_pairs={{0,24},{1,25},{2,26},{3,27},{4,28},{5,29},{6,30},{7,31},{8,0},{9,1... | collective-permute-start | bytes 29816 | tf_op jit(solution)/shard_map/ppermute | solution.py:404
  16.5 8.8 %collective-permute-start.1 = (bf16[1,4968]{1,0:T(2,128)(2,1)S(1)}, bf16[1,4968]{1,0:T(2,128)(2,1)S(1)}, u32[]{:S(2)}, u32[]{:S(2)}) collective-permute-start(bf16[1,4968]{1,0:T(2,128)(2,1)S(1)} %reshape.435), channel_id=1, source_target_pairs={{0,16},{1,17},{2,18},{3,19},{4,20},{5,21},{6,22},{7,23},{8,24},{9,... | collective-permute-start | bytes 29816 | tf_op jit(solution)/shard_map/ppermute | solution.py:404
  16.5 8.8 %collective-permute-start = (bf16[1,4968]{1,0:T(2,128)(2,1)S(1)}, bf16[1,4968]{1,0:T(2,128)(2,1)S(1)}, u32[]{:S(2)}, u32[]{:S(2)}) collective-permute-start(bf16[1,4968]{1,0:T(2,128)(2,1)S(1)} %reshape.435), channel_id=1, source_target_pairs={{0,8},{1,9},{2,10},{3,11},{4,12},{5,13},{6,14},{7,15},{8,16},{9,17... | collective-permute-start | bytes 29816 | tf_op jit(solution)/shard_map/ppermute | solution.py:404
  19.3 30.7 %collective-permute-start.18 = (bf16[144,868]{1,0:T(8,128)(2,1)S(1)}, bf16[144,868]{1,0:T(8,128)(2,1)S(1)}, u32[]{:S(2)}, u32[]{:S(2)}) collective-permute-start(bf16[144,868]{1,0:T(8,128)(2,1)S(1)} %pad_maximum_fusion.2), channel_id=1, source_target_pairs={{0,16},{1,17},{2,18},{3,19},{4,20},{5,21},{6,22},{7,23},{8,24},{9,... | collective-permute-start | bytes 749960 | tf_op jit(solution)/shard_map/ppermute | solution.py:404
  21.3 28.7 %collective-permute-start.17 = (bf16[144,868]{1,0:T(8,128)(2,1)S(1)}, bf16[144,868]{1,0:T(8,128)(2,1)S(1)}, u32[]{:S(2)}, u32[]{:S(2)}) collective-permute-start(bf16[144,868]{1,0:T(8,128)(2,1)S(1)} %pad_maximum_fusion.2), channel_id=1, source_target_pairs={{0,8},{1,9},{2,10},{3,11},{4,12},{5,13},{6,14},{7,15},{8,16},{9,17... | collective-permute-start | bytes 749960 | tf_op jit(solution)/shard_map/ppermute | solution.py:404
  22.8 27.2 %collective-permute-start.19 = (bf16[144,868]{1,0:T(8,128)(2,1)S(1)}, bf16[144,868]{1,0:T(8,128)(2,1)S(1)}, u32[]{:S(2)}, u32[]{:S(2)}) collective-permute-start(bf16[144,868]{1,0:T(8,128)(2,1)S(1)} %pad_maximum_fusion.2), channel_id=1, source_target_pairs={{0,24},{1,25},{2,26},{3,27},{4,28},{5,29},{6,30},{7,31},{8,0},{9,1... | collective-permute-start | bytes 749960 | tf_op jit(solution)/shard_map/ppermute | solution.py:404
  25.3 4.4 collective-permute-start.4
  26.9 4.0 collective-permute-start.3
  29.8 5.2 collective-permute-start.6
  30.9 4.0 collective-permute-start.5
  34.9 1.9 collective-permute-start.8
  35.0 1.4 collective-permute-start.7
  36.4 1.2 collective-permute-start.9
  50.2 30.3 %collective-permute-start.21 = (bf16[4,144,868]{2,1,0:T(8,128)(2,1)S(1)}, bf16[4,144,868]{2,1,0:T(8,128)(2,1)S(1)}, u32[]{:S(2)}, u32[]{:S(2)}) collective-permute-start(bf16[4,144,868]{2,1,0:T(8,128)(2,1)S(1)} %pad_maximum_fusion.rest_0_), channel_id=1, source_target_pairs={{0,2},{1,3},{2,0},{3,1},{4,5},{5,4},{6,7},{7,6},{8,10},{9,11},{10,... | collective-permute-start | bytes 2999816 | tf_op jit(solution)/shard_map/ppermute | solution.py:404
  52.6 2.2 collective-permute-start.10
  52.6 54.6 %collective-permute-start.20 = (bf16[4,144,868]{2,1,0:T(8,128)(2,1)S(1)}, bf16[4,144,868]{2,1,0:T(8,128)(2,1)}, u32[]{:S(2)}, u32[]{:S(2)}) collective-permute-start(bf16[4,144,868]{2,1,0:T(8,128)(2,1)S(1)} %pad_maximum_fusion.rest_0_), channel_id=1, source_target_pairs={{0,1},{1,0},{2,3},{3,2},{4,6},{5,7},{6,4},{7,5},{8,9},{9,8},{10,11... | collective-permute-start | bytes 2999816 | tf_op jit(solution)/shard_map/ppermute | solution.py:404
  80.5 26.7 %collective-permute-start.22 = (bf16[4,144,868]{2,1,0:T(8,128)(2,1)S(1)}, bf16[4,144,868]{2,1,0:T(8,128)(2,1)}, u32[]{:S(2)}, u32[]{:S(2)}) collective-permute-start(bf16[4,144,868]{2,1,0:T(8,128)(2,1)S(1)} %collective-permute-done.21.rest_2_), channel_id=1, source_target_pairs={{0,1},{1,0},{2,3},{3,2},{4,6},{5,7},{6,4},{7,5},{8,9},{9,8},{10,11... | collective-permute-start | bytes 2999816 | tf_op jit(solution)/shard_map/ppermute | solution.py:404
  82.0 9.8 %collective-permute-start.11 = (f32[16,1728]{1,0:T(8,128)S(1)}, f32[16,1728]{1,0:T(8,128)S(1)}, u32[]{:S(2)}, u32[]{:S(2)}) collective-permute-start(f32[16,1728]{1,0:T(8,128)S(1)} %get-tuple-element.231), channel_id=1, source_target_pairs={{0,8},{1,9},{2,10},{3,11},{4,12},{5,13},{6,14},{7,15},{8,16},{9,17... | collective-permute-start | bytes 331784 | tf_op jit(solution)/shard_map/ppermute | solution.py:404
  87.4 7.0 %collective-permute-start.13 = (f32[16,1728]{1,0:T(8,128)S(1)}, f32[16,1728]{1,0:T(8,128)S(1)}, u32[]{:S(2)}, u32[]{:S(2)}) collective-permute-start(f32[16,1728]{1,0:T(8,128)S(1)} %get-tuple-element.232), channel_id=1, source_target_pairs={{0,24},{1,25},{2,26},{3,27},{4,28},{5,29},{6,30},{7,31},{8,0},{9,1... | collective-permute-start | bytes 331784 | tf_op jit(solution)/shard_map/ppermute | solution.py:404
  87.4 9.5 %collective-permute-start.12 = (f32[16,1728]{1,0:T(8,128)S(1)}, f32[16,1728]{1,0:T(8,128)S(1)}, u32[]{:S(2)}, u32[]{:S(2)}) collective-permute-start(f32[16,1728]{1,0:T(8,128)S(1)} %get-tuple-element.233), channel_id=1, source_target_pairs={{0,16},{1,17},{2,18},{3,19},{4,20},{5,21},{6,22},{7,23},{8,24},{9,... | collective-permute-start | bytes 331784 | tf_op jit(solution)/shard_map/ppermute | solution.py:404
  97.9 6.0 %collective-permute-start.16 = (f32[4,1728]{1,0:T(4,128)S(1)}, f32[4,1728]{1,0:T(4,128)S(1)}, u32[]{:S(2)}, u32[]{:S(2)}) collective-permute-start(f32[4,1728]{1,0:T(4,128)S(1)} %get-tuple-element.246), channel_id=1, source_target_pairs={{0,3},{1,0},{2,1},{3,2},{4,7},{5,4},{6,5},{7,6},{8,11},{9,8},{10,9... | collective-permute-start | bytes 82952 | tf_op jit(solution)/shard_map/ppermute | solution.py:404
  98.4 6.7 %collective-permute-start.15 = (f32[4,1728]{1,0:T(4,128)S(1)}, f32[4,1728]{1,0:T(4,128)S(1)}, u32[]{:S(2)}, u32[]{:S(2)}) collective-permute-start(f32[4,1728]{1,0:T(4,128)S(1)} %get-tuple-element.247), channel_id=1, source_target_pairs={{0,2},{1,3},{2,0},{3,1},{4,6},{5,7},{6,4},{7,5},{8,10},{9,11},{10,... | collective-permute-start | bytes 82952 | tf_op jit(solution)/shard_map/ppermute | solution.py:404
  100.0 13.0 %collective-permute-start.23 = (bf16[4,144,868]{2,1,0:T(8,128)(2,1)S(1)}, bf16[4,144,868]{2,1,0:T(8,128)(2,1)}, u32[]{:S(2)}, u32[]{:S(2)}) collective-permute-start(bf16[4,144,868]{2,1,0:T(8,128)(2,1)S(1)} %pad_maximum_fusion.rest_0_), channel_id=1, source_target_pairs={{0,4},{1,5},{2,6},{3,7},{4,0},{5,1},{6,2},{7,3},{8,12},{9,13},{10,... | collective-permute-start | bytes 2999816 | tf_op jit(solution)/shard_map/ppermute | solution.py:404
  103.9 8.1 %collective-permute-start.14 = (f32[4,1728]{1,0:T(4,128)S(1)}, f32[4,1728]{1,0:T(4,128)S(1)}, u32[]{:S(2)}, u32[]{:S(2)}) collective-permute-start(f32[4,1728]{1,0:T(4,128)S(1)} %get-tuple-element.248), channel_id=1, source_target_pairs={{0,1},{1,2},{2,3},{3,0},{4,5},{5,6},{6,7},{7,4},{8,9},{9,10},{10,1... | collective-permute-start | bytes 82952 | tf_op jit(solution)/shard_map/ppermute | solution.py:404
  105.0 7.9 %collective-permute-start.25 = (bf16[4,144,868]{2,1,0:T(8,128)(2,1)S(1)}, bf16[4,144,868]{2,1,0:T(8,128)(2,1)}, u32[]{:S(2)}, u32[]{:S(2)}) collective-permute-start(bf16[4,144,868]{2,1,0:T(8,128)(2,1)S(1)} %collective-permute-done.21.rest_2_), channel_id=1, source_target_pairs={{0,4},{1,5},{2,6},{3,7},{4,0},{5,1},{6,2},{7,3},{8,12},{9,13},{10,... | collective-permute-start | bytes 2999816 | tf_op jit(solution)/shard_map/ppermute | solution.py:404
  107.2 5.8 collective-permute-start.24
  107.2 5.8 collective-permute-start.26
  133.7 449.8 %reduce-scatter.2.cloned.1.call-start = ((), (), s32[]{:S(2)}) async-start(), calls=%async_computation.1 | async-start | bytes 14598144 | tf_op jit(solution)/shard_map/reduce_scatter | solution.py:1354
  228.3 11.4 %collective-permute-start.27 = (bf16[2,2,4,288,576]{4,3,2,1,0:T(8,128)(2,1)}, bf16[2,2,4,288,576]{4,3,2,1,0:T(8,128)(2,1)S(1)}, u32[]{:S(2)}, u32[]{:S(2)}) collective-permute-start(bf16[2,2,4,288,576]{4,3,2,1,0:T(8,128)(2,1)} %get-tuple-element.104), channel_id=1, source_target_pairs={{0,4},{1,5},{2,6},{3,7},{4,0},{5,1},{6,2},{7,3},{8,12},{9,13},{10,... | collective-permute-start | bytes 15925256 | tf_op jit(solution)/shard_map/ppermute | solution.py:404
  246.0 70.8 %collective-permute-start.28 = (bf16[2,4,288,576]{3,2,1,0:T(8,128)(2,1)}, bf16[2,4,288,576]{3,2,1,0:T(8,128)(2,1)S(1)}, u32[]{:S(2)}, u32[]{:S(2)}) collective-permute-start(bf16[2,4,288,576]{3,2,1,0:T(8,128)(2,1)} %fusion), channel_id=1, source_target_pairs={{0,2},{1,3},{2,0},{3,1},{4,5},{5,4},{6,7},{7,6},{8,10},{9,11},{10,... | collective-permute-start | bytes 7962632 | tf_op jit(solution)/shard_map/ppermute | solution.py:404
  323.4 25.2 %collective-permute-start.29 = (bf16[4,288,576]{2,1,0:T(8,128)(2,1)}, bf16[4,288,576]{2,1,0:T(8,128)(2,1)S(1)}, u32[]{:S(2)}, u32[]{:S(2)}) collective-permute-start(bf16[4,288,576]{2,1,0:T(8,128)(2,1)} %get-tuple-element.220), channel_id=1, source_target_pairs={{0,1},{1,0},{2,3},{3,2},{4,6},{5,7},{6,4},{7,5},{8,9},{9,8},{10,11... | collective-permute-start | bytes 3981320 | tf_op jit(solution)/shard_map/ppermute | solution.py:404
  350.0 70.8 %collective-permute-start.30 = (bf16[288,576]{1,0:T(8,128)(2,1)}, bf16[288,576]{1,0:T(8,128)(2,1)S(1)}, u32[]{:S(2)}, u32[]{:S(2)}) collective-permute-start(bf16[288,576]{1,0:T(8,128)(2,1)} %get-tuple-element.136), channel_id=1, source_target_pairs={{0,8},{1,9},{2,10},{3,11},{4,12},{5,13},{6,14},{7,15},{8,16},{9,17... | collective-permute-start | bytes 995336 | tf_op jit(solution)/shard_map/ppermute | solution.py:404
  352.0 68.9 %collective-permute-start.31 = (bf16[288,576]{1,0:T(8,128)(2,1)}, bf16[288,576]{1,0:T(8,128)(2,1)S(1)}, u32[]{:S(2)}, u32[]{:S(2)}) collective-permute-start(bf16[288,576]{1,0:T(8,128)(2,1)} %get-tuple-element.137), channel_id=1, source_target_pairs={{0,16},{1,17},{2,18},{3,19},{4,20},{5,21},{6,22},{7,23},{8,24},{9,... | collective-permute-start | bytes 995336 | tf_op jit(solution)/shard_map/ppermute | solution.py:404
  355.6 65.3 %collective-permute-start.32 = (bf16[288,576]{1,0:T(8,128)(2,1)}, bf16[288,576]{1,0:T(8,128)(2,1)S(1)}, u32[]{:S(2)}, u32[]{:S(2)}) collective-permute-start(bf16[288,576]{1,0:T(8,128)(2,1)} %get-tuple-element.138), channel_id=1, source_target_pairs={{0,24},{1,25},{2,26},{3,27},{4,28},{5,29},{6,30},{7,31},{8,0},{9,1... | collective-permute-start | bytes 995336 | tf_op jit(solution)/shard_map/ppermute | solution.py:404
  421.9 19.9 %collective-permute-start.33 = (f32[14,1152]{1,0:T(8,128)S(1)}, f32[14,1152]{1,0:T(8,128)S(1)}, u32[]{:S(2)}, u32[]{:S(2)}) collective-permute-start(f32[14,1152]{1,0:T(8,128)S(1)} %fusion.19), channel_id=1, source_target_pairs={{0,1},{1,0},{2,3},{3,2},{4,5},{5,4},{6,7},{7,6},{8,9},{9,8},{10,11... | collective-permute-start | bytes 193544 | tf_op jit(solution)/shard_map/ppermute | solution.py:404
  441.9 23.3 %collective-permute-start.34 = (bf16[2,2,4,144,868]{4,3,2,1,0:T(8,128)(2,1)}, bf16[2,2,4,144,868]{4,3,2,1,0:T(8,128)(2,1)}, u32[]{:S(2)}, u32[]{:S(2)}) collective-permute-start(bf16[2,2,4,144,868]{4,3,2,1,0:T(8,128)(2,1)} %get-tuple-element.151), channel_id=1, source_target_pairs={{0,4},{1,5},{2,6},{3,7},{4,0},{5,1},{6,2},{7,3},{8,12},{9,13},{10,... | collective-permute-start | bytes 11999240 | tf_op jit(solution)/shard_map/ppermute | solution.py:404
  442.0 23.2 %collective-permute-start.35 = (f32[14,1152]{1,0:T(8,128)S(1)}, f32[14,1152]{1,0:T(8,128)S(1)}, u32[]{:S(2)}, u32[]{:S(2)}) collective-permute-start(f32[14,1152]{1,0:T(8,128)S(1)} %fusion.69), channel_id=1, source_target_pairs={{0,2},{1,3},{2,0},{3,1},{4,6},{5,7},{6,4},{7,5},{8,10},{9,11},{10,... | collective-permute-start | bytes 193544 | tf_op jit(solution)/shard_map/ppermute | solution.py:404
  468.2 36.6 %collective-permute-start.39 = (bf16[2,4,144,868]{3,2,1,0:T(8,128)(2,1)S(1)}, bf16[2,4,144,868]{3,2,1,0:T(8,128)(2,1)}, u32[]{:S(2)}, u32[]{:S(2)}) collective-permute-start(bf16[2,4,144,868]{3,2,1,0:T(8,128)(2,1)S(1)} %fusion.1), channel_id=1, source_target_pairs={{0,2},{1,3},{2,0},{3,1},{4,5},{5,4},{6,7},{7,6},{8,10},{9,11},{10,... | collective-permute-start | bytes 5999624 | tf_op jit(solution)/shard_map/ppermute | solution.py:404
  471.0 5.1 collective-permute-start.36
  473.4 31.3 %collective-permute-start.37 = (bf16[4,1728]{1,0:T(4,128)(2,1)S(1)}, bf16[4,1728]{1,0:T(4,128)(2,1)S(1)}, u32[]{:S(2)}, u32[]{:S(2)}) collective-permute-start(bf16[4,1728]{1,0:T(4,128)(2,1)S(1)} %bitcast.310), channel_id=1, source_target_pairs={{0,2},{1,3},{2,0},{3,1},{4,6},{5,7},{6,4},{7,5},{8,10},{9,11},{10,... | collective-permute-start | bytes 41480 | tf_op jit(solution)/shard_map/ppermute | solution.py:404
  473.4 31.3 %collective-permute-start.38 = (bf16[4,1728]{1,0:T(4,128)(2,1)S(1)}, bf16[4,1728]{1,0:T(4,128)(2,1)S(1)}, u32[]{:S(2)}, u32[]{:S(2)}) collective-permute-start(bf16[4,1728]{1,0:T(4,128)(2,1)S(1)} %bitcast.309), channel_id=1, source_target_pairs={{0,3},{1,0},{2,1},{3,2},{4,7},{5,4},{6,5},{7,6},{8,11},{9,8},{10,9... | collective-permute-start | bytes 41480 | tf_op jit(solution)/shard_map/ppermute | solution.py:404
  508.6 22.7 %collective-permute-start.44 = (bf16[4,144,868]{2,1,0:T(8,128)(2,1)S(1)}, bf16[4,144,868]{2,1,0:T(8,128)(2,1)}, u32[]{:S(2)}, u32[]{:S(2)}) collective-permute-start(bf16[4,144,868]{2,1,0:T(8,128)(2,1)S(1)} %get-tuple-element.223), channel_id=1, source_target_pairs={{0,1},{1,0},{2,3},{3,2},{4,6},{5,7},{6,4},{7,5},{8,9},{9,8},{10,11... | collective-permute-start | bytes 2999816 | tf_op jit(solution)/shard_map/ppermute | solution.py:404
  510.9 6.1 %collective-permute-start.42 = (bf16[16,1728]{1,0:T(8,128)(2,1)}, bf16[16,1728]{1,0:T(8,128)(2,1)S(1)}, u32[]{:S(2)}, u32[]{:S(2)}) collective-permute-start(bf16[16,1728]{1,0:T(8,128)(2,1)} %pad_maximum_fusion.5), channel_id=1, source_target_pairs={{0,24},{1,25},{2,26},{3,27},{4,28},{5,29},{6,30},{7,31},{8,0},{9,1... | collective-permute-start | bytes 165896 | tf_op jit(solution)/shard_map/ppermute | solution.py:404
  514.0 8.8 %collective-permute-start.41 = (bf16[16,1728]{1,0:T(8,128)(2,1)}, bf16[16,1728]{1,0:T(8,128)(2,1)}, u32[]{:S(2)}, u32[]{:S(2)}) collective-permute-start(bf16[16,1728]{1,0:T(8,128)(2,1)} %pad_maximum_fusion.5), channel_id=1, source_target_pairs={{0,16},{1,17},{2,18},{3,19},{4,20},{5,21},{6,22},{7,23},{8,24},{9,... | collective-permute-start | bytes 165896 | tf_op jit(solution)/shard_map/ppermute | solution.py:404
  514.0 8.8 %collective-permute-start.40 = (bf16[16,1728]{1,0:T(8,128)(2,1)}, bf16[16,1728]{1,0:T(8,128)(2,1)}, u32[]{:S(2)}, u32[]{:S(2)}) collective-permute-start(bf16[16,1728]{1,0:T(8,128)(2,1)} %pad_maximum_fusion.5), channel_id=1, source_target_pairs={{0,8},{1,9},{2,10},{3,11},{4,12},{5,13},{6,14},{7,15},{8,16},{9,17... | collective-permute-start | bytes 165896 | tf_op jit(solution)/shard_map/ppermute | solution.py:404
  516.8 13.8 %collective-permute-start.45 = (f32[14,1152]{1,0:T(8,128)S(1)}, f32[14,1152]{1,0:T(8,128)S(1)}, u32[]{:S(2)}, u32[]{:S(2)}) collective-permute-start(f32[14,1152]{1,0:T(8,128)S(1)} %add.978), channel_id=1, source_target_pairs={{0,4},{1,5},{2,6},{3,7},{4,0},{5,1},{6,2},{7,3},{8,12},{9,13},{10,... | collective-permute-start | bytes 193544 | tf_op jit(solution)/shard_map/ppermute | solution.py:404
  528.4 2.1 collective-permute-start.43
  534.7 10.7 %collective-permute-start.59 = (f32[1,1728]{1,0:T(1,128)S(1)}, f32[1,1728]{1,0:T(1,128)S(1)}, u32[]{:S(2)}, u32[]{:S(2)}) collective-permute-start(f32[1,1728]{1,0:T(1,128)S(1)} %broadcast_in_dim.40), channel_id=1, source_target_pairs={{0,3},{1,0},{2,1},{3,2},{4,7},{5,4},{6,5},{7,6},{8,11},{9,8},{10,9... | collective-permute-start | bytes 20744 | tf_op jit(solution)/shard_map/ppermute | solution.py:404
  535.8 10.0 %collective-permute-start.58 = (f32[1,1728]{1,0:T(1,128)S(1)}, f32[1,1728]{1,0:T(1,128)S(1)}, u32[]{:S(2)}, u32[]{:S(2)}) collective-permute-start(f32[1,1728]{1,0:T(1,128)S(1)} %broadcast_in_dim.40), channel_id=1, source_target_pairs={{0,2},{1,3},{2,0},{3,1},{4,6},{5,7},{6,4},{7,5},{8,10},{9,11},{10,... | collective-permute-start | bytes 20744 | tf_op jit(solution)/shard_map/ppermute | solution.py:404
  536.7 11.0 %collective-permute-start.57 = (f32[1,1728]{1,0:T(1,128)S(1)}, f32[1,1728]{1,0:T(1,128)S(1)}, u32[]{:S(2)}, u32[]{:S(2)}) collective-permute-start(f32[1,1728]{1,0:T(1,128)S(1)} %broadcast_in_dim.40), channel_id=1, source_target_pairs={{0,1},{1,2},{2,3},{3,0},{4,5},{5,6},{6,7},{7,4},{8,9},{9,10},{10,1... | collective-permute-start | bytes 20744 | tf_op jit(solution)/shard_map/ppermute | solution.py:404
  538.7 11.9 %collective-permute-start.48 = (f32[8,4,144]{2,1,0:T(4,128)}, f32[8,4,144]{2,1,0:T(4,128)S(1)}, u32[]{:S(2)}, u32[]{:S(2)}) collective-permute-start(f32[8,4,144]{2,1,0:T(4,128)} %get-tuple-element.238), channel_id=1, source_target_pairs={{0,1},{1,2},{2,3},{3,0},{4,5},{5,6},{6,7},{7,4},{8,9},{9,10},{10,1... | collective-permute-start | bytes 55304 | tf_op jit(solution)/shard_map/ppermute | solution.py:404
  544.1 7.1 %collective-permute-start.46 = (f32[8,4,144]{2,1,0:T(4,128)}, f32[8,4,144]{2,1,0:T(4,128)S(1)}, u32[]{:S(2)}, u32[]{:S(2)}) collective-permute-start(f32[8,4,144]{2,1,0:T(4,128)} %get-tuple-element.239), channel_id=1, source_target_pairs={{0,3},{1,0},{2,1},{3,2},{4,7},{5,4},{6,5},{7,6},{8,11},{9,8},{10,9... | collective-permute-start | bytes 55304 | tf_op jit(solution)/shard_map/ppermute | solution.py:404
  545.5 17.8 %collective-permute-start.51 = (bf16[144,868]{1,0:T(8,128)(2,1)S(1)}, bf16[144,868]{1,0:T(8,128)(2,1)S(1)}, u32[]{:S(2)}, u32[]{:S(2)}) collective-permute-start(bf16[144,868]{1,0:T(8,128)(2,1)S(1)} %get-tuple-element.228), channel_id=1, source_target_pairs={{0,24},{1,25},{2,26},{3,27},{4,28},{5,29},{6,30},{7,31},{8,0},{9,1... | collective-permute-start | bytes 749960 | tf_op jit(solution)/shard_map/ppermute | solution.py:404
  546.3 22.6 %collective-permute-start.50 = (bf16[144,868]{1,0:T(8,128)(2,1)S(1)}, bf16[144,868]{1,0:T(8,128)(2,1)S(1)}, u32[]{:S(2)}, u32[]{:S(2)}) collective-permute-start(bf16[144,868]{1,0:T(8,128)(2,1)S(1)} %get-tuple-element.229), channel_id=1, source_target_pairs={{0,16},{1,17},{2,18},{3,19},{4,20},{5,21},{6,22},{7,23},{8,24},{9,... | collective-permute-start | bytes 749960 | tf_op jit(solution)/shard_map/ppermute | solution.py:404
  548.3 20.6 %collective-permute-start.49 = (bf16[144,868]{1,0:T(8,128)(2,1)S(1)}, bf16[144,868]{1,0:T(8,128)(2,1)S(1)}, u32[]{:S(2)}, u32[]{:S(2)}) collective-permute-start(bf16[144,868]{1,0:T(8,128)(2,1)S(1)} %get-tuple-element.230), channel_id=1, source_target_pairs={{0,8},{1,9},{2,10},{3,11},{4,12},{5,13},{6,14},{7,15},{8,16},{9,17... | collective-permute-start | bytes 749960 | tf_op jit(solution)/shard_map/ppermute | solution.py:404
  550.5 12.7 %collective-permute-start.52 = (f32[14,1152]{1,0:T(8,128)S(1)}, f32[14,1152]{1,0:T(8,128)S(1)}, u32[]{:S(2)}, u32[]{:S(2)}) collective-permute-start(f32[14,1152]{1,0:T(8,128)S(1)} %add.984), channel_id=1, source_target_pairs={{0,8},{1,9},{2,10},{3,11},{4,12},{5,13},{6,14},{7,15},{8,0},{9,1},... | collective-permute-start | bytes 193544 | tf_op jit(solution)/shard_map/ppermute | solution.py:404
  551.3 3.9 collective-permute-start.47
  569.0 1.4 collective-permute-start.53
  570.4 6.9 %collective-permute-start.54 = (f32[2,4,144]{2,1,0:T(4,128)S(1)}, f32[2,4,144]{2,1,0:T(4,128)S(1)}, u32[]{:S(2)}, u32[]{:S(2)}) collective-permute-start(f32[2,4,144]{2,1,0:T(4,128)S(1)} %get-tuple-element.262), channel_id=1, source_target_pairs={{0,24},{1,25},{2,26},{3,27},{4,28},{5,29},{6,30},{7,31},{8,0},{9,1... | collective-permute-start | bytes 13832 | tf_op jit(solution)/shard_map/ppermute | solution.py:404
  570.5 6.8 %collective-permute-start.56 = (f32[2,4,144]{2,1,0:T(4,128)S(1)}, f32[2,4,144]{2,1,0:T(4,128)S(1)}, u32[]{:S(2)}, u32[]{:S(2)}) collective-permute-start(f32[2,4,144]{2,1,0:T(4,128)S(1)} %get-tuple-element.263), channel_id=1, source_target_pairs={{0,8},{1,9},{2,10},{3,11},{4,12},{5,13},{6,14},{7,15},{8,16},{9,17... | collective-permute-start | bytes 13832 | tf_op jit(solution)/shard_map/ppermute | solution.py:404
  572.5 4.8 collective-permute-start.55
  576.0 6.3 %collective-permute-start.60 = (f32[14,1152]{1,0:T(8,128)S(1)}, f32[14,1152]{1,0:T(8,128)S(1)}, u32[]{:S(2)}, u32[]{:S(2)}) collective-permute-start(f32[14,1152]{1,0:T(8,128)S(1)} %add.1058), channel_id=1, source_target_pairs={{0,16},{1,17},{2,18},{3,19},{4,20},{5,21},{6,22},{7,23},{8,24},{9,... | collective-permute-start | bytes 193544 | tf_op jit(solution)/shard_map/ppermute | solution.py:404
  (28 other events, 497.6 us)
Sparse Core Ops, SparseCore 0:
  10.9 137.7 all-gather.4
  152.2 89.1 all-gather.6
  348.8 175.3 reduce-scatter.1

commit v3 on v2

--- a/solution.py
+++ b/solution.py
@@ -730,12 +730,14 @@
     unit, ignored = normalize(after)
     normed = (unit * (1.0 + mod_ref[0, 4:5, :]) + mod_ref[0, 3:4, :]).astype(jnp.bfloat16)
     normed_t_ref[...] = jnp.transpose(normed)
+    ahead = dot_nn(normed, weight[0, :, :wide])
     for column in range(columns):
         span = slice(column * wide, (column + 1) * wide)
-        preact = dot_nn(normed, weight[column, :, :wide]) + bias_ref[:, span]
+        preact = ahead + bias_ref[:, span]
+        if column + 1 < columns:
+            ahead = dot_nn(normed, weight[column + 1, :, :wide])
         hidden, slope = gelu_parts(preact)
-        low = hidden.astype(jnp.bfloat16)
-        hidden_ref[:, span] = low
+        hidden_ref[:, span] = hidden.astype(jnp.bfloat16)
         slope_ref[:, span] = slope.astype(jnp.bfloat16)
 
 
@@ -860,9 +862,12 @@
             copy.wait()
 
     gradmid = jnp.zeros(after.shape, jnp.float32)
+    ahead = dot_nt(gradred, reduce_weight[:wide, :])
     for column in range(columns):
         span = slice(column * wide, (column + 1) * wide)
-        gradact = dot_nt(gradred, reduce_weight[span, :])
+        gradact = ahead
+        if column + 1 < columns:
+            ahead = dot_nt(gradred, reduce_weight[(column + 1) * wide : (column + 2) * wide, :])
         gradpre = (gradact * slope_ref[:, span].astype(jnp.float32)).astype(jnp.bfloat16)
         gradpre_ref[:, span] = gradpre
         biassum_ref[:, span] += jnp.sum(gradpre.astype(jnp.float32), axis=0, keepdims=True)
@@ -1378,13 +1383,15 @@
     attend_other, attend_parts, grad_projected, sums = tied(attend_other, attend_parts, grad_projected, sums)
     attend_other = cross_sum(attend_other)
     sums_moving = flip_bit(sums, bits[-1])
+    grad_projected, attend_other, sums_moving = tied(grad_projected, attend_other, sums_moving)
+    sums = sums + sums_moving
+    attend_moving = first_send(attend_parts, attend_other)
     back = front_backward(
         where, grad_projected, grad_gate, grad_after, tokens, modulation, attend_pieces
     )
-    back, attend_other, sums_moving = tied(back, attend_other, sums_moving)
+    back, attend_moving = tied(back, attend_moving)
     tokens_grad, front_sums = back
-    sums = sums + sums_moving
-    attend_moving = first_send(attend_parts, attend_other)
+    attend_level = first_add(attend_parts, attend_other, attend_moving)
 
     middle_sums = jnp.sum(middle_sums.reshape(QUARTERS, -1, 8, features), axis=1)
     grad_modulation = jnp.concatenate([front_sums[:, :2], middle_sums[:, :4]], axis=1)
@@ -1397,20 +1404,19 @@
     rows_here = [
         send(pick(grad_modulation, (dp_at + shift) % columns), along_dp(shift)) for shift in range(1, columns)
     ]
-    rows_here, attend_moving = tied(rows_here, attend_moving)
-    attend_level = first_add(attend_parts, attend_other, attend_moving)
+    rows_here, attend_level = tied(rows_here, attend_level)
     attend_moving = second_send(attend_level)
-    rows_here = jnp.concatenate([pick(grad_modulation, dp_at)] + rows_here, axis=0)
+    rows_here = jnp.stack([pick(grad_modulation, dp_at)] + rows_here).reshape(columns * slots, own_columns)
     sums_moving = flip_bit(sums, columns)
-    rows_here = jnp.concatenate(
-        [rows_here] + [send(rows_here, along_z(shift)) for shift in range(1, chips)], axis=0
-    )
+    rows_here = jnp.stack([rows_here] + [send(rows_here, along_z(shift)) for shift in range(1, chips)])
     rows_other = send(rows_here, across_core)
     rows_other, attend_moving, sums_moving = tied(rows_other, attend_moving, sums_moving)
     attend_level = second_add(attend_level, attend_moving)
     attend_moving = far_send(attend_level)
     sums = sums + sums_moving
-    rows_here = jnp.concatenate([rows_here, rows_other], axis=0)
+    bits = flip_bits(2 * columns, blocks * columns)
+    sums_moving = flip_bit(sums, bits[0])
+    rows_here = jnp.stack([rows_here, rows_other]).reshape(-1, own_columns)
     order = []
     for sibling in range(2):
         for far in range(chips):
@@ -1424,6 +1430,13 @@
         cond_here, rows_here, (((0,), (0,)), ((), ())), preferred_element_type=jnp.float32
     )
     modbias_here = jnp.sum(rows_here.astype(jnp.float32), axis=0, keepdims=True)
+    grad_cond = lax.dot_general(
+        rows_here, modulate_weight, (((1,), (1,)), ((), ())), preferred_element_type=jnp.float32
+    )
+    grad_cond = jnp.moveaxis(grad_cond.reshape(blocks, columns, slots, own_rows), 1, 0)
+    modulate_grad, grad_cond, modbias_here, attend_moving, sums_moving = tied(
+        modulate_grad, grad_cond, modbias_here, attend_moving, sums_moving
+    )
     modbias_all = jnp.stack(
         [modbias_here] + [send(modbias_here, along_dp(shift)) for shift in range(1, columns)]
     )
@@ -1431,14 +1444,7 @@
     own_bias = modulate_bias.shape[0]
     linear_at = fsdp_at * columns + dp_at
     modbias_grad = lax.dynamic_slice_in_dim(modbias_all, linear_at * own_bias, own_bias, axis=1).reshape(-1)
-    grad_cond = lax.dot_general(
-        rows_here, modulate_weight, (((1,), (1,)), ((), ())), preferred_element_type=jnp.float32
-    )
-    grad_cond = jnp.moveaxis(grad_cond.reshape(blocks, columns, slots, own_rows), 1, 0)
-    bits = flip_bits(2 * columns, blocks * columns)
-    sums_moving = flip_bit(sums, bits[0])
     cond_sum = [send(grad_cond[shift], along_dp(-shift)) for shift in range(1, columns)]
-    cond_sum, attend_moving, sums_moving = tied(cond_sum, attend_moving, sums_moving)
     attend_both = far_add(attend_level, attend_moving)
     attend_grad, forget_grad = attend_both[:, : attend_weight.shape[1]], attend_both[:, attend_weight.shape[1] :]
     sums = sums + sums_moving
@@ -1448,9 +1454,9 @@
     cond_sum = jnp.stack([cond_sum[0], send(cond_sum[1], across_core)], axis=1)
     joint = joint[0].astype(jnp.float32)
     expand_grad, output_grad = joint[:, : expand_weight.shape[1]], joint[:, expand_weight.shape[1] :]
-    cond_parts = jnp.concatenate(
-        [cond_sum[0]] + [send(cond_sum[far], along_z(-far)) for far in range(1, chips)], axis=0
-    )
+    cond_parts = jnp.stack(
+        [cond_sum[0]] + [send(cond_sum[far], along_z(-far)) for far in range(1, chips)]
+    ).reshape(blocks, slots, own_rows)
     cond_columns_all = []
     for block in range(blocks):
         sibling = jnp.abs(block % 2 - core_at)

time: 601 us -> 588 us (0.978)
  local copies, waits for them, and re-layouts: 31.3 us -> 18.9 us
    concatenate x2 -> x0, local copies, waits for them, and re-layouts: 8.92 us -> none  [the longest x1 5.52 us: on_device(): jnp.concatenate([rows_here] + [send(rows_here, along_z(shift)) for shift...]
  transfers between devices with their start and end apart: 64 -> 64, of which waited for: 19 -> 24; matrix products, arithmetic and copies ran while one was open for 10% -> 9% of each run, Pallas kernels for 53% -> 54%
where the time goes in v3:
time: 588 us; the launch traced here: 580 us
  Pallas kernels  313 us (53%)
  waiting for transfers between devices  111 us (19%)
  starting transfers between devices  76.4 us (13%)
  other arithmetic  41.1 us (7%)
  local copies, waits for them, and re-layouts  18.9 us (3%)
  between operations  15.8 us (3%)
    pallas_call x7, Pallas kernels, call(): pl.pallas_call(kernel, grid_spec=pltpu.PrefetchScalarGridSpec(num_scalar_...  219 us
    ppermute x61, waiting for transfers between devices, send(): return lax.ppermute(values, ('fsdp', 'dp'), pairs)  111 us
    ppermute x61, starting transfers between devices, send(): return lax.ppermute(values, ('fsdp', 'dp'), pairs)  75.9 us
    pallas_call x1, Pallas kernels, attention_backward(): pl.pallas_call(functools.partial(attention_backward_kernel, heads, head_s...  63 us
    pallas_call x1, Pallas kernels, attention_forward(): pl.pallas_call(functools.partial(attention_forward_kernel, heads, head_si...  31 us
  transfers between devices with their start and end apart: 64, of which 24 were waited for; matrix products, arithmetic and copies ran while one was open for 9% of the time, Pallas kernels for 54%

profile of v3, /device:TPU:0, one launch (start us, length us, event | category | flops | bytes accessed | tf_op | source)
XLA Modules:
  0.0 579.6 jit_solution(1050665392939322445)
XLA Ops:
  7.2 1.9 pad_maximum_fusion.2
  9.9 1.4 concatenate.35
  11.4 5.1 collective-permute-start.2
  19.4 2.0 collective-permute-start.18
  21.3 1.5 collective-permute-start.17
  22.8 2.4 collective-permute-start.19
  25.4 1.6 collective-permute-start.4
  26.9 1.5 collective-permute-start.3
  30.9 1.5 collective-permute-start.5
  32.5 2.4 collective-permute-done.5
  39.5 10.5 %collective-permute-done.18 = bf16[144,868]{1,0:T(8,128)(2,1)S(1)} collective-permute-done((bf16[144,868]{1,0:T(8,128)(2,1)S(1)}, bf16[144,868]{1,0:T(8,128)(2,1)S(1)}, u32[]{:S(2)}, u32[]{:S(2)}) %collective-permute-start.18) | collective-permute-done | bytes 250016 | tf_op jit(solution)/shard_map/ppermute | solution.py:404
  50.2 1.6 collective-permute-start.21
  52.6 1.5 collective-permute-start.20
  55.9 24.6 %collective-permute-done.21.rest_2_ = bf16[4,144,868]{2,1,0:T(8,128)(2,1)S(1)} collective-permute-done((bf16[4,144,868]{2,1,0:T(8,128)(2,1)S(1)}, bf16[4,144,868]{2,1,0:T(8,128)(2,1)S(1)}, u32[]{:S(2)}, u32[]{:S(2)}) %collective-permute-start.21) | collective-permute-done | bytes 999968 | tf_op jit(solution)/shard_map/ppermute | solution.py:404
  80.5 1.5 collective-permute-start.22
  82.0 5.3 collective-permute-start.11
  87.4 3.2 collective-permute-start.12
  90.6 1.3 collective-permute-done.11
  91.9 2.6 collective-permute-done.13
  94.4 2.4 collective-permute-done.12
  98.4 1.7 collective-permute-start.15
  100.0 3.8 collective-permute-start.23
  103.9 1.2 collective-permute-start.14
  105.1 2.1 collective-permute-start.25
  107.7 1.4 fusion.60
  113.0 20.7 %front_forward.1 = (bf16[1024,3456]{1,0:T(8,128)(2,1)}, f32[1024,128]{1,0:T(8,128)}, bf16[1152,1024]{1,0:T(8,128)(2,1)}) custom-call(s32[5]{0:T(128)} %stack.351.where, bf16[1024,1152]{1,0:T(8,128)(2,1)} %tokens_ref.7, f32[4,8,1152]{2,1,0:T(8,128)} %pad.12.mod_ref, bf16[4,144,868]{2,1,0:T(8,128)(2,1)} %copy-done.1, ...), custom_call_target="tpu_custom_call" | custom-call | flops 163829520 | bytes 400000 | tf_op jit(solution)/shard_map/front_forward/pallas_call | solution.py:649
  135.5 31.0 %attention_forward.1 = (bf16[1024,1152]{1,0:T(8,128)(2,1)}, f32[1024,1152]{1,0:T(8,128)}, f32[1024,128]{1,0:T(8,128)}, bf16[4,16,256,256]{3,2,1,0:T(8,128)(2,1)}) custom-call(s32[1]{0:T(128)S(6)} %copy.95.flag_ref, bf16[1024,3456]{1,0:T(8,128)(2,1)} %get-tuple-element.100.proj_ref, f32[1024,128]{1,0:T(8,128)} %get-tuple-element.101.gate_ref, ...), custom_call_target="tpu_custom_call" | custom-call | flops 340000000 | bytes 400000 | tf_op jit(solution)/shard_map/attention_forward/pallas_call | solution.py:188
  166.6 39.5 %middle_forward.1 = (f32[1024,1152]{1,0:T(8,128)}, bf16[1024,4608]{1,0:T(8,128)(2,1)}, bf16[1024,4608]{1,0:T(8,128)(2,1)}, bf16[1152,1024]{1,0:T(8,128)(2,1)}, b...) custom-call(s32[5]{0:T(128)} %stack.351.where, bf16[1024,1152]{1,0:T(8,128)(2,1)} %get-tuple-element.102.conv_ref, ...), custom_call_target="tpu_custom_call" | custom-call | flops 271790912 | bytes 1200000 | tf_op jit(solution)/shard_map/middle_forward/pallas_call | solution.py:649
  206.1 22.5 %grads_across.1 = (bf16[2,2,4,288,576]{4,3,2,1,0:T(8,128)(2,1)}, bf16[2,4,288,576]{3,2,1,0:T(8,128)(2,1)}, bf16[2,4,288,576]{3,2,1,0:T(8,128)(2,1)}) custom-call(s32[5]{0:T(128)} %stack.351.where, bf16[1024,1152]{1,0:T(8,128)(2,1)} %get-tuple-element.104.right_ref, bf16[1024,4608]{1,0:T(8,128)(2,1)} %get-tuple-element.108.hidden_ref), custom_call_target="tpu_custom_call" | custom-call | flops 217432720 | bytes 480000 | tf_op jit(solution)/shard_map/grads_across/pallas_call | solution.py:649
  228.7 11.3 %collective-permute-done.27 = bf16[2,2,4,288,576]{4,3,2,1,0:T(8,128)(2,1)S(1)} collective-permute-done((bf16[2,2,4,288,576]{4,3,2,1,0:T(8,128)(2,1)}, bf16[2,2,4,288,576]{4,3,2,1,0:T(8,128)(2,1)S(1)}, u32[]{:S(2)}, u32[]{:S(2)}) %collective-permute-start.27) | collective-permute-done | bytes 5308448 | tf_op jit(solution)/shard_map/ppermute | solution.py:404
  240.0 6.2 %fusion = bf16[2,4,288,576]{3,2,1,0:T(8,128)(2,1)} fusion(bf16[2,4,288,576]{3,2,1,0:T(8,128)(2,1)} %get-tuple-element.119, bf16[2,2,4,288,576]{4,3,2,1,0:T(8,128)(2,1)S(1)} %collective-permute-done.27), kind=kLoop, calls=%fused_computation.1 | loop fusion | flops 5308416 | bytes 7962624 | tf_op jit(solution)/shard_map/convert_element_type | solution.py:483
  246.2 2.4 collective-permute-start.28
  248.6 68.2 %middle_backward.1 = (bf16[1024,1152]{1,0:T(8,128)(2,1)}, bf16[1024,4608]{1,0:T(8,128)(2,1)}, f32[1024,1152]{1,0:T(8,128)}, bf16[1024,1152]{1,0:T(8,128)(2,1)}, ...) custom-call(s32[5]{0:T(128)} %stack.351.where, bf16[1024,4608]{1,0:T(8,128)(2,1)} %get-tuple-element.108.hidden_ref, ...), custom_call_target="tpu_custom_call" | custom-call | flops 652298176 | bytes 1600000 | tf_op jit(solution)/shard_map/middle_backward/pallas_call | solution.py:649
  316.8 1.6 copy-done.5
  318.5 4.9 fusion.2
  323.4 25.3 %grads_joint.1 = bf16[8,4,144,1440]{3,2,1,0:T(8,128)(2,1)} custom-call(s32[5]{0:T(128)} %stack.351.where, bf16[1152,1024]{1,0:T(8,128)(2,1)} %get-tuple-element.129.left_ref, bf16[1152,1024]{1,0:T(8,128)(2,1)} %get-tuple-element.130.small_left_ref, bf16[1024,4608]{1,0:T(8,128)(2,1)} %get-tuple-element.131.right_ref, ...), custom_call_target="tpu_custom_call" | custom-call | flops 271790912 | bytes 600000 | tf_op jit(solution)/shard_map/grads_joint/pallas_call | solution.py:649
  348.7 1.4 fusion.14
  350.9 3.8 collective-permute-start.31
  354.7 2.9 collective-permute-start.32
  357.7 63.0 %attention_backward.1 = (bf16[1024,3456]{1,0:T(8,128)(2,1)}, f32[1024,128]{1,0:T(8,128)}, f32[1,128]{1,0:T(1,128)}, f32[9,1152]{1,0:T(8,128)}) custom-call(s32[1]{0:T(128)S(6)} %copy.95.flag_ref, bf16[1024,3456]{1,0:T(8,128)(2,1)} %get-tuple-element.100.proj_ref, f32[1024,128]{1,0:T(8,128)} %get-tuple-element.101.gate_ref, f32[1,128]{1,0:T(1,128)} %pad.13.bias_ref, ...), custom_call_target="tpu_custom_call" | custom-call | flops 760000000 | bytes 800000 | tf_op jit(solution)/shard_map/attention_backward/pallas_call | solution.py:346
  422.0 20.0 %weight_grads.1 = (bf16[2,2,4,144,868]{4,3,2,1,0:T(8,128)(2,1)}, bf16[2,4,144,868]{3,2,1,0:T(8,128)(2,1)}, bf16[2,4,144,868]{3,2,1,0:T(8,128)(2,1)}) custom-call(s32[5]{0:T(128)} %stack.351.where, bf16[1152,1024]{1,0:T(8,128)(2,1)} %get-tuple-element.122.rest_0_.rest_1_.rest_2_.rest_3_.rest_4_.rest_5_.rest_6_.rest_7_, ...), custom_call_target="tpu_custom_call" | custom-call | flops 163074544 | bytes 347996 | tf_op jit(solution)/shard_map/weight_grads/pallas_call | solution.py:649
  442.7 5.7 collective-permute-done.35
  449.4 3.7 fusion.1
  453.8 22.6 %front_backward.1 = (bf16[1024,1152]{1,0:T(8,128)(2,1)}, f32[4,8,1152]{2,1,0:T(8,128)}) custom-call(s32[5]{0:T(128)} %stack.351.where, bf16[1024,3456]{1,0:T(8,128)(2,1)} %get-tuple-element.153.rest_8_.gradproj_ref, f32[1024,128]{1,0:T(8,128)} %get-tuple-element.143.rest_9_.gradgate_ref, f32[1024,1152]{1,0:T(8,128)} %get-tuple-element.154.gradafter_ref, ...), custom_call_target="tpu_custom_call" | custom-call | flops 163829520 | bytes 500000 | tf_op jit(solution)/shard_map/front_backward/pallas_call | solution.py:649
  476.5 15.4 %collective-permute-done.36 = bf16[2,4,144,868]{3,2,1,0:T(8,128)(2,1)} collective-permute-done((bf16[2,4,144,868]{3,2,1,0:T(8,128)(2,1)S(1)}, bf16[2,4,144,868]{3,2,1,0:T(8,128)(2,1)}, u32[]{:S(2)}, u32[]{:S(2)}) %collective-permute-start.36) | collective-permute-done | bytes 1999904 | tf_op jit(solution)/shard_map/ppermute | solution.py:404
  493.4 2.0 collective-permute-start.37
  496.9 4.5 fusion.4
  505.7 1.3 collective-permute-done.42
  507.9 2.1 collective-permute-done.40
  511.6 2.3 add_bitcast_fusion
  513.9 5.6 collective-permute-done.44
  519.5 1.7 add.1028
  521.4 2.2 fusion.17
  524.7 2.4 collective-permute-start.47
  527.1 2.4 fusion.6
  529.9 1.7 collective-permute-done.48
  531.7 13.5 %collective-permute-done.47 = bf16[144,868]{1,0:T(8,128)(2,1)} collective-permute-done((bf16[144,868]{1,0:T(8,128)(2,1)}, bf16[144,868]{1,0:T(8,128)(2,1)}, u32[]{:S(2)}, u32[]{:S(2)}) %collective-permute-start.47) | collective-permute-done | bytes 250016 | tf_op jit(solution)/shard_map/ppermute | solution.py:404
  545.2 1.6 collective-permute-start.59
  547.5 1.2 collective-permute-start.57
  549.6 1.4 fusion.8
  552.8 1.8 collective-permute-start.50
  556.8 2.6 collective-permute-done.52
  560.7 2.0 collective-permute-start.55
  562.7 3.8 collective-permute-start.54
  (241 shorter events, 49.7 us)
Async XLA Ops:
  7.2 159.4 %all-gather.5.cloned.1.call-start = ((), (), s32[]{:S(2)}) async-start(), calls=%async_computation.2 | async-start | bytes 14598144 | tf_op jit(solution)/shard_map/all_gather | solution.py:1325
  9.1 239.5 %all-gather.7.cloned.1.call-start = ((), (), s32[]{:S(2)}) async-start(), calls=%async_computation.3 | async-start | bytes 10948608 | tf_op jit(solution)/shard_map/all_gather | solution.py:1333
  11.4 11.4 %collective-permute-start.2 = (bf16[1,4968]{1,0:T(2,128)(2,1)S(1)}, bf16[1,4968]{1,0:T(2,128)(2,1)S(1)}, u32[]{:S(2)}, u32[]{:S(2)}) collective-permute-start(bf16[1,4968]{1,0:T(2,128)(2,1)S(1)} %reshape.443), channel_id=1, source_target_pairs={{0,24},{1,25},{2,26},{3,27},{4,28},{5,29},{6,30},{7,31},{8,0},{9,1... | collective-permute-start | bytes 29816 | tf_op jit(solution)/shard_map/ppermute | solution.py:404
  16.5 8.8 %collective-permute-start.1 = (bf16[1,4968]{1,0:T(2,128)(2,1)S(1)}, bf16[1,4968]{1,0:T(2,128)(2,1)S(1)}, u32[]{:S(2)}, u32[]{:S(2)}) collective-permute-start(bf16[1,4968]{1,0:T(2,128)(2,1)S(1)} %reshape.443), channel_id=1, source_target_pairs={{0,16},{1,17},{2,18},{3,19},{4,20},{5,21},{6,22},{7,23},{8,24},{9,... | collective-permute-start | bytes 29816 | tf_op jit(solution)/shard_map/ppermute | solution.py:404
  16.5 8.8 %collective-permute-start = (bf16[1,4968]{1,0:T(2,128)(2,1)S(1)}, bf16[1,4968]{1,0:T(2,128)(2,1)S(1)}, u32[]{:S(2)}, u32[]{:S(2)}) collective-permute-start(bf16[1,4968]{1,0:T(2,128)(2,1)S(1)} %reshape.443), channel_id=1, source_target_pairs={{0,8},{1,9},{2,10},{3,11},{4,12},{5,13},{6,14},{7,15},{8,16},{9,17... | collective-permute-start | bytes 29816 | tf_op jit(solution)/shard_map/ppermute | solution.py:404
  19.4 30.7 %collective-permute-start.18 = (bf16[144,868]{1,0:T(8,128)(2,1)S(1)}, bf16[144,868]{1,0:T(8,128)(2,1)S(1)}, u32[]{:S(2)}, u32[]{:S(2)}) collective-permute-start(bf16[144,868]{1,0:T(8,128)(2,1)S(1)} %pad_maximum_fusion.3), channel_id=1, source_target_pairs={{0,16},{1,17},{2,18},{3,19},{4,20},{5,21},{6,22},{7,23},{8,24},{9,... | collective-permute-start | bytes 749960 | tf_op jit(solution)/shard_map/ppermute | solution.py:404
  21.3 28.7 %collective-permute-start.17 = (bf16[144,868]{1,0:T(8,128)(2,1)S(1)}, bf16[144,868]{1,0:T(8,128)(2,1)S(1)}, u32[]{:S(2)}, u32[]{:S(2)}) collective-permute-start(bf16[144,868]{1,0:T(8,128)(2,1)S(1)} %pad_maximum_fusion.3), channel_id=1, source_target_pairs={{0,8},{1,9},{2,10},{3,11},{4,12},{5,13},{6,14},{7,15},{8,16},{9,17... | collective-permute-start | bytes 749960 | tf_op jit(solution)/shard_map/ppermute | solution.py:404
  22.8 27.2 %collective-permute-start.19 = (bf16[144,868]{1,0:T(8,128)(2,1)S(1)}, bf16[144,868]{1,0:T(8,128)(2,1)S(1)}, u32[]{:S(2)}, u32[]{:S(2)}) collective-permute-start(bf16[144,868]{1,0:T(8,128)(2,1)S(1)} %pad_maximum_fusion.3), channel_id=1, source_target_pairs={{0,24},{1,25},{2,26},{3,27},{4,28},{5,29},{6,30},{7,31},{8,0},{9,1... | collective-permute-start | bytes 749960 | tf_op jit(solution)/shard_map/ppermute | solution.py:404
  25.4 4.4 collective-permute-start.4
  26.9 4.0 collective-permute-start.3
  29.8 5.2 collective-permute-start.6
  30.9 4.0 collective-permute-start.5
  34.9 1.9 collective-permute-start.8
  35.0 1.4 collective-permute-start.7
  36.4 1.2 collective-permute-start.9
  50.2 30.3 %collective-permute-start.21 = (bf16[4,144,868]{2,1,0:T(8,128)(2,1)S(1)}, bf16[4,144,868]{2,1,0:T(8,128)(2,1)S(1)}, u32[]{:S(2)}, u32[]{:S(2)}) collective-permute-start(bf16[4,144,868]{2,1,0:T(8,128)(2,1)S(1)} %pad_maximum_fusion.rest_0_), channel_id=1, source_target_pairs={{0,2},{1,3},{2,0},{3,1},{4,5},{5,4},{6,7},{7,6},{8,10},{9,11},{10,... | collective-permute-start | bytes 2999816 | tf_op jit(solution)/shard_map/ppermute | solution.py:404
  52.6 2.2 collective-permute-start.10
  52.6 54.6 %collective-permute-start.20 = (bf16[4,144,868]{2,1,0:T(8,128)(2,1)S(1)}, bf16[4,144,868]{2,1,0:T(8,128)(2,1)}, u32[]{:S(2)}, u32[]{:S(2)}) collective-permute-start(bf16[4,144,868]{2,1,0:T(8,128)(2,1)S(1)} %pad_maximum_fusion.rest_0_), channel_id=1, source_target_pairs={{0,1},{1,0},{2,3},{3,2},{4,6},{5,7},{6,4},{7,5},{8,9},{9,8},{10,11... | collective-permute-start | bytes 2999816 | tf_op jit(solution)/shard_map/ppermute | solution.py:404
  80.5 26.7 %collective-permute-start.22 = (bf16[4,144,868]{2,1,0:T(8,128)(2,1)S(1)}, bf16[4,144,868]{2,1,0:T(8,128)(2,1)}, u32[]{:S(2)}, u32[]{:S(2)}) collective-permute-start(bf16[4,144,868]{2,1,0:T(8,128)(2,1)S(1)} %collective-permute-done.21.rest_2_), channel_id=1, source_target_pairs={{0,1},{1,0},{2,3},{3,2},{4,6},{5,7},{6,4},{7,5},{8,9},{9,8},{10,11... | collective-permute-start | bytes 2999816 | tf_op jit(solution)/shard_map/ppermute | solution.py:404
  82.0 9.8 %collective-permute-start.11 = (f32[16,1728]{1,0:T(8,128)S(1)}, f32[16,1728]{1,0:T(8,128)S(1)}, u32[]{:S(2)}, u32[]{:S(2)}) collective-permute-start(f32[16,1728]{1,0:T(8,128)S(1)} %get-tuple-element.237), channel_id=1, source_target_pairs={{0,8},{1,9},{2,10},{3,11},{4,12},{5,13},{6,14},{7,15},{8,16},{9,17... | collective-permute-start | bytes 331784 | tf_op jit(solution)/shard_map/ppermute | solution.py:404
  87.4 7.0 %collective-permute-start.13 = (f32[16,1728]{1,0:T(8,128)S(1)}, f32[16,1728]{1,0:T(8,128)S(1)}, u32[]{:S(2)}, u32[]{:S(2)}) collective-permute-start(f32[16,1728]{1,0:T(8,128)S(1)} %get-tuple-element.238), channel_id=1, source_target_pairs={{0,24},{1,25},{2,26},{3,27},{4,28},{5,29},{6,30},{7,31},{8,0},{9,1... | collective-permute-start | bytes 331784 | tf_op jit(solution)/shard_map/ppermute | solution.py:404
  87.4 9.5 %collective-permute-start.12 = (f32[16,1728]{1,0:T(8,128)S(1)}, f32[16,1728]{1,0:T(8,128)S(1)}, u32[]{:S(2)}, u32[]{:S(2)}) collective-permute-start(f32[16,1728]{1,0:T(8,128)S(1)} %get-tuple-element.239), channel_id=1, source_target_pairs={{0,16},{1,17},{2,18},{3,19},{4,20},{5,21},{6,22},{7,23},{8,24},{9,... | collective-permute-start | bytes 331784 | tf_op jit(solution)/shard_map/ppermute | solution.py:404
  97.9 6.0 %collective-permute-start.16 = (f32[4,1728]{1,0:T(4,128)S(1)}, f32[4,1728]{1,0:T(4,128)S(1)}, u32[]{:S(2)}, u32[]{:S(2)}) collective-permute-start(f32[4,1728]{1,0:T(4,128)S(1)} %get-tuple-element.254), channel_id=1, source_target_pairs={{0,3},{1,0},{2,1},{3,2},{4,7},{5,4},{6,5},{7,6},{8,11},{9,8},{10,9... | collective-permute-start | bytes 82952 | tf_op jit(solution)/shard_map/ppermute | solution.py:404
  98.4 6.7 %collective-permute-start.15 = (f32[4,1728]{1,0:T(4,128)S(1)}, f32[4,1728]{1,0:T(4,128)S(1)}, u32[]{:S(2)}, u32[]{:S(2)}) collective-permute-start(f32[4,1728]{1,0:T(4,128)S(1)} %get-tuple-element.255), channel_id=1, source_target_pairs={{0,2},{1,3},{2,0},{3,1},{4,6},{5,7},{6,4},{7,5},{8,10},{9,11},{10,... | collective-permute-start | bytes 82952 | tf_op jit(solution)/shard_map/ppermute | solution.py:404
  100.0 13.0 %collective-permute-start.23 = (bf16[4,144,868]{2,1,0:T(8,128)(2,1)S(1)}, bf16[4,144,868]{2,1,0:T(8,128)(2,1)}, u32[]{:S(2)}, u32[]{:S(2)}) collective-permute-start(bf16[4,144,868]{2,1,0:T(8,128)(2,1)S(1)} %pad_maximum_fusion.rest_0_), channel_id=1, source_target_pairs={{0,4},{1,5},{2,6},{3,7},{4,0},{5,1},{6,2},{7,3},{8,12},{9,13},{10,... | collective-permute-start | bytes 2999816 | tf_op jit(solution)/shard_map/ppermute | solution.py:404
  103.9 8.1 %collective-permute-start.14 = (f32[4,1728]{1,0:T(4,128)S(1)}, f32[4,1728]{1,0:T(4,128)S(1)}, u32[]{:S(2)}, u32[]{:S(2)}) collective-permute-start(f32[4,1728]{1,0:T(4,128)S(1)} %get-tuple-element.256), channel_id=1, source_target_pairs={{0,1},{1,2},{2,3},{3,0},{4,5},{5,6},{6,7},{7,4},{8,9},{9,10},{10,1... | collective-permute-start | bytes 82952 | tf_op jit(solution)/shard_map/ppermute | solution.py:404
  105.1 7.9 %collective-permute-start.25 = (bf16[4,144,868]{2,1,0:T(8,128)(2,1)S(1)}, bf16[4,144,868]{2,1,0:T(8,128)(2,1)}, u32[]{:S(2)}, u32[]{:S(2)}) collective-permute-start(bf16[4,144,868]{2,1,0:T(8,128)(2,1)S(1)} %collective-permute-done.21.rest_2_), channel_id=1, source_target_pairs={{0,4},{1,5},{2,6},{3,7},{4,0},{5,1},{6,2},{7,3},{8,12},{9,13},{10,... | collective-permute-start | bytes 2999816 | tf_op jit(solution)/shard_map/ppermute | solution.py:404
  107.2 5.8 %collective-permute-start.24 = (bf16[4,144,868]{2,1,0:T(8,128)(2,1)}, bf16[4,144,868]{2,1,0:T(8,128)(2,1)}, u32[]{:S(2)}, u32[]{:S(2)}) collective-permute-start(bf16[4,144,868]{2,1,0:T(8,128)(2,1)} %collective-permute-done.20.rest_1_), channel_id=1, source_target_pairs={{0,4},{1,5},{2,6},{3,7},{4,0},{5,1},{6,2},{7,3},{8,12},{9,13},{10,... | collective-permute-start | bytes 2999816 | tf_op jit(solution)/shard_map/ppermute | solution.py:404
  107.2 5.8 collective-permute-start.26
  133.7 436.5 %reduce-scatter.2.cloned.1.call-start = ((), (), s32[]{:S(2)}) async-start(), calls=%async_computation.1 | async-start | bytes 14598144 | tf_op jit(solution)/shard_map/reduce_scatter | solution.py:1359
  228.6 11.4 %collective-permute-start.27 = (bf16[2,2,4,288,576]{4,3,2,1,0:T(8,128)(2,1)}, bf16[2,2,4,288,576]{4,3,2,1,0:T(8,128)(2,1)S(1)}, u32[]{:S(2)}, u32[]{:S(2)}) collective-permute-start(bf16[2,2,4,288,576]{4,3,2,1,0:T(8,128)(2,1)} %get-tuple-element.107), channel_id=1, source_target_pairs={{0,4},{1,5},{2,6},{3,7},{4,0},{5,1},{6,2},{7,3},{8,12},{9,13},{10,... | collective-permute-start | bytes 15925256 | tf_op jit(solution)/shard_map/ppermute | solution.py:404
  246.2 70.6 %collective-permute-start.28 = (bf16[2,4,288,576]{3,2,1,0:T(8,128)(2,1)}, bf16[2,4,288,576]{3,2,1,0:T(8,128)(2,1)S(1)}, u32[]{:S(2)}, u32[]{:S(2)}) collective-permute-start(bf16[2,4,288,576]{3,2,1,0:T(8,128)(2,1)} %fusion), channel_id=1, source_target_pairs={{0,2},{1,3},{2,0},{3,1},{4,5},{5,4},{6,7},{7,6},{8,10},{9,11},{10,... | collective-permute-start | bytes 7962632 | tf_op jit(solution)/shard_map/ppermute | solution.py:404
  323.4 25.3 %collective-permute-start.29 = (bf16[4,288,576]{2,1,0:T(8,128)(2,1)}, bf16[4,288,576]{2,1,0:T(8,128)(2,1)S(1)}, u32[]{:S(2)}, u32[]{:S(2)}) collective-permute-start(bf16[4,288,576]{2,1,0:T(8,128)(2,1)} %get-tuple-element.226), channel_id=1, source_target_pairs={{0,1},{1,0},{2,3},{3,2},{4,6},{5,7},{6,4},{7,5},{8,9},{9,8},{10,11... | collective-permute-start | bytes 3981320 | tf_op jit(solution)/shard_map/ppermute | solution.py:404
  350.0 70.7 %collective-permute-start.30 = (bf16[288,576]{1,0:T(8,128)(2,1)}, bf16[288,576]{1,0:T(8,128)(2,1)S(1)}, u32[]{:S(2)}, u32[]{:S(2)}) collective-permute-start(bf16[288,576]{1,0:T(8,128)(2,1)} %get-tuple-element.139), channel_id=1, source_target_pairs={{0,8},{1,9},{2,10},{3,11},{4,12},{5,13},{6,14},{7,15},{8,16},{9,17... | collective-permute-start | bytes 995336 | tf_op jit(solution)/shard_map/ppermute | solution.py:404
  350.9 69.8 %collective-permute-start.31 = (bf16[288,576]{1,0:T(8,128)(2,1)}, bf16[288,576]{1,0:T(8,128)(2,1)S(1)}, u32[]{:S(2)}, u32[]{:S(2)}) collective-permute-start(bf16[288,576]{1,0:T(8,128)(2,1)} %get-tuple-element.140), channel_id=1, source_target_pairs={{0,16},{1,17},{2,18},{3,19},{4,20},{5,21},{6,22},{7,23},{8,24},{9,... | collective-permute-start | bytes 995336 | tf_op jit(solution)/shard_map/ppermute | solution.py:404
  354.7 66.1 %collective-permute-start.32 = (bf16[288,576]{1,0:T(8,128)(2,1)}, bf16[288,576]{1,0:T(8,128)(2,1)S(1)}, u32[]{:S(2)}, u32[]{:S(2)}) collective-permute-start(bf16[288,576]{1,0:T(8,128)(2,1)} %get-tuple-element.141), channel_id=1, source_target_pairs={{0,24},{1,25},{2,26},{3,27},{4,28},{5,29},{6,30},{7,31},{8,0},{9,1... | collective-permute-start | bytes 995336 | tf_op jit(solution)/shard_map/ppermute | solution.py:404
  421.8 20.1 %collective-permute-start.33 = (f32[14,1152]{1,0:T(8,128)S(1)}, f32[14,1152]{1,0:T(8,128)S(1)}, u32[]{:S(2)}, u32[]{:S(2)}) collective-permute-start(f32[14,1152]{1,0:T(8,128)S(1)} %fusion.21), channel_id=1, source_target_pairs={{0,1},{1,0},{2,3},{3,2},{4,5},{5,4},{6,7},{7,6},{8,9},{9,8},{10,11... | collective-permute-start | bytes 193544 | tf_op jit(solution)/shard_map/ppermute | solution.py:404
  442.0 7.3 %collective-permute-start.34 = (bf16[2,2,4,144,868]{4,3,2,1,0:T(8,128)(2,1)}, bf16[2,2,4,144,868]{4,3,2,1,0:T(8,128)(2,1)S(1)}, u32[]{:S(2)}, u32[]{:S(2)}) collective-permute-start(bf16[2,2,4,144,868]{4,3,2,1,0:T(8,128)(2,1)} %get-tuple-element.151), channel_id=1, source_target_pairs={{0,4},{1,5},{2,6},{3,7},{4,0},{5,1},{6,2},{7,3},{8,12},{9,13},{10,... | collective-permute-start | bytes 11999240 | tf_op jit(solution)/shard_map/ppermute | solution.py:404
  442.1 6.3 %collective-permute-start.35 = (f32[14,1152]{1,0:T(8,128)S(1)}, f32[14,1152]{1,0:T(8,128)S(1)}, u32[]{:S(2)}, u32[]{:S(2)}) collective-permute-start(f32[14,1152]{1,0:T(8,128)S(1)} %fusion.64), channel_id=1, source_target_pairs={{0,2},{1,3},{2,0},{3,1},{4,6},{5,7},{6,4},{7,5},{8,10},{9,11},{10,... | collective-permute-start | bytes 193544 | tf_op jit(solution)/shard_map/ppermute | solution.py:404
  453.1 38.8 %collective-permute-start.36 = (bf16[2,4,144,868]{3,2,1,0:T(8,128)(2,1)S(1)}, bf16[2,4,144,868]{3,2,1,0:T(8,128)(2,1)}, u32[]{:S(2)}, u32[]{:S(2)}) collective-permute-start(bf16[2,4,144,868]{3,2,1,0:T(8,128)(2,1)S(1)} %fusion.1), channel_id=1, source_target_pairs={{0,2},{1,3},{2,0},{3,1},{4,5},{5,4},{6,7},{7,6},{8,10},{9,11},{10,... | collective-permute-start | bytes 5999624 | tf_op jit(solution)/shard_map/ppermute | solution.py:404
  493.4 8.1 %collective-permute-start.37 = (bf16[4,1728]{1,0:T(4,128)(2,1)S(1)}, bf16[4,1728]{1,0:T(4,128)(2,1)S(1)}, u32[]{:S(2)}, u32[]{:S(2)}) collective-permute-start(bf16[4,1728]{1,0:T(4,128)(2,1)S(1)} %bitcast.326), channel_id=1, source_target_pairs={{0,1},{1,2},{2,3},{3,0},{4,5},{5,6},{6,7},{7,4},{8,9},{9,10},{10,1... | collective-permute-start | bytes 41480 | tf_op jit(solution)/shard_map/ppermute | solution.py:404
  495.4 6.1 %collective-permute-start.38 = (bf16[4,1728]{1,0:T(4,128)(2,1)S(1)}, bf16[4,1728]{1,0:T(4,128)(2,1)S(1)}, u32[]{:S(2)}, u32[]{:S(2)}) collective-permute-start(bf16[4,1728]{1,0:T(4,128)(2,1)S(1)} %bitcast.325), channel_id=1, source_target_pairs={{0,2},{1,3},{2,0},{3,1},{4,6},{5,7},{6,4},{7,5},{8,10},{9,11},{10,... | collective-permute-start | bytes 41480 | tf_op jit(solution)/shard_map/ppermute | solution.py:404
  496.0 5.5 collective-permute-start.39
  501.5 18.1 %collective-permute-start.44 = (bf16[4,144,868]{2,1,0:T(8,128)(2,1)}, bf16[4,144,868]{2,1,0:T(8,128)(2,1)S(1)}, u32[]{:S(2)}, u32[]{:S(2)}) collective-permute-start(bf16[4,144,868]{2,1,0:T(8,128)(2,1)} %get-tuple-element.167), channel_id=1, source_target_pairs={{0,1},{1,0},{2,3},{3,2},{4,6},{5,7},{6,4},{7,5},{8,9},{9,8},{10,11... | collective-permute-start | bytes 2999816 | tf_op jit(solution)/shard_map/ppermute | solution.py:404
  502.7 4.2 collective-permute-start.42
  502.8 5.1 collective-permute-start.41
  503.9 6.2 %collective-permute-start.40 = (bf16[16,1728]{1,0:T(8,128)(2,1)S(1)}, bf16[16,1728]{1,0:T(8,128)(2,1)S(1)}, u32[]{:S(2)}, u32[]{:S(2)}) collective-permute-start(bf16[16,1728]{1,0:T(8,128)(2,1)S(1)} %reshape.451), channel_id=1, source_target_pairs={{0,8},{1,9},{2,10},{3,11},{4,12},{5,13},{6,14},{7,15},{8,16},{9,17... | collective-permute-start | bytes 165896 | tf_op jit(solution)/shard_map/ppermute | solution.py:404
  505.7 8.2 %collective-permute-start.45 = (f32[14,1152]{1,0:T(8,128)}, f32[14,1152]{1,0:T(8,128)}, u32[]{:S(2)}, u32[]{:S(2)}) collective-permute-start(f32[14,1152]{1,0:T(8,128)} %add.1024), channel_id=1, source_target_pairs={{0,4},{1,5},{2,6},{3,7},{4,0},{5,1},{6,2},{7,3},{8,12},{9,13},{10,... | collective-permute-start | bytes 193544 | tf_op jit(solution)/shard_map/ppermute | solution.py:404
  511.5 2.4 collective-permute-start.43
  521.3 8.7 %collective-permute-start.49 = (f32[14,1152]{1,0:T(8,128)}, f32[14,1152]{1,0:T(8,128)}, u32[]{:S(2)}, u32[]{:S(2)}) collective-permute-start(f32[14,1152]{1,0:T(8,128)} %add.1028), channel_id=1, source_target_pairs={{0,8},{1,9},{2,10},{3,11},{4,12},{5,13},{6,14},{7,15},{8,0},{9,1},... | collective-permute-start | bytes 193544 | tf_op jit(solution)/shard_map/ppermute | solution.py:404
  523.6 8.1 %collective-permute-start.48 = (bf16[144,868]{1,0:T(8,128)(2,1)}, bf16[144,868]{1,0:T(8,128)(2,1)S(1)}, u32[]{:S(2)}, u32[]{:S(2)}) collective-permute-start(bf16[144,868]{1,0:T(8,128)(2,1)} %get-tuple-element.234), channel_id=1, source_target_pairs={{0,24},{1,25},{2,26},{3,27},{4,28},{5,29},{6,30},{7,31},{8,0},{9,1... | collective-permute-start | bytes 749960 | tf_op jit(solution)/shard_map/ppermute | solution.py:404
  524.7 20.5 %collective-permute-start.47 = (bf16[144,868]{1,0:T(8,128)(2,1)}, bf16[144,868]{1,0:T(8,128)(2,1)}, u32[]{:S(2)}, u32[]{:S(2)}) collective-permute-start(bf16[144,868]{1,0:T(8,128)(2,1)} %get-tuple-element.235), channel_id=1, source_target_pairs={{0,16},{1,17},{2,18},{3,19},{4,20},{5,21},{6,22},{7,23},{8,24},{9,... | collective-permute-start | bytes 749960 | tf_op jit(solution)/shard_map/ppermute | solution.py:404
  527.1 18.1 %collective-permute-start.46 = (bf16[144,868]{1,0:T(8,128)(2,1)}, bf16[144,868]{1,0:T(8,128)(2,1)}, u32[]{:S(2)}, u32[]{:S(2)}) collective-permute-start(bf16[144,868]{1,0:T(8,128)(2,1)} %get-tuple-element.236), channel_id=1, source_target_pairs={{0,8},{1,9},{2,10},{3,11},{4,12},{5,13},{6,14},{7,15},{8,16},{9,17... | collective-permute-start | bytes 749960 | tf_op jit(solution)/shard_map/ppermute | solution.py:404
  545.2 9.4 %collective-permute-start.59 = (f32[1,1728]{1,0:T(1,128)S(1)}, f32[1,1728]{1,0:T(1,128)S(1)}, u32[]{:S(2)}, u32[]{:S(2)}) collective-permute-start(f32[1,1728]{1,0:T(1,128)S(1)} %broadcast_in_dim.40), channel_id=1, source_target_pairs={{0,3},{1,0},{2,1},{3,2},{4,7},{5,4},{6,5},{7,6},{8,11},{9,8},{10,9... | collective-permute-start | bytes 20744 | tf_op jit(solution)/shard_map/ppermute | solution.py:404
  546.9 8.0 %collective-permute-start.58 = (f32[1,1728]{1,0:T(1,128)S(1)}, f32[1,1728]{1,0:T(1,128)S(1)}, u32[]{:S(2)}, u32[]{:S(2)}) collective-permute-start(f32[1,1728]{1,0:T(1,128)S(1)} %broadcast_in_dim.40), channel_id=1, source_target_pairs={{0,2},{1,3},{2,0},{3,1},{4,6},{5,7},{6,4},{7,5},{8,10},{9,11},{10,... | collective-permute-start | bytes 20744 | tf_op jit(solution)/shard_map/ppermute | solution.py:404
  547.5 8.5 %collective-permute-start.57 = (f32[1,1728]{1,0:T(1,128)S(1)}, f32[1,1728]{1,0:T(1,128)S(1)}, u32[]{:S(2)}, u32[]{:S(2)}) collective-permute-start(f32[1,1728]{1,0:T(1,128)S(1)} %broadcast_in_dim.40), channel_id=1, source_target_pairs={{0,1},{1,2},{2,3},{3,0},{4,5},{5,6},{6,7},{7,4},{8,9},{9,10},{10,1... | collective-permute-start | bytes 20744 | tf_op jit(solution)/shard_map/ppermute | solution.py:404
  551.8 17.2 %collective-permute-start.60 = (f32[14,1152]{1,0:T(8,128)S(1)}, f32[14,1152]{1,0:T(8,128)S(1)}, u32[]{:S(2)}, u32[]{:S(2)}) collective-permute-start(f32[14,1152]{1,0:T(8,128)S(1)} %add.1058), channel_id=1, source_target_pairs={{0,16},{1,17},{2,18},{3,19},{4,20},{5,21},{6,22},{7,23},{8,24},{9,... | collective-permute-start | bytes 193544 | tf_op jit(solution)/shard_map/ppermute | solution.py:404
  552.8 4.0 collective-permute-start.50
  554.6 4.8 collective-permute-start.52
  554.9 4.5 collective-permute-start.51
  559.4 1.2 collective-permute-start.53
  560.7 6.4 %collective-permute-start.55 = (f32[2,4,144]{2,1,0:T(4,128)S(1)}, f32[2,4,144]{2,1,0:T(4,128)S(1)}, u32[]{:S(2)}, u32[]{:S(2)}) collective-permute-start(f32[2,4,144]{2,1,0:T(4,128)S(1)} %bitcast.329), channel_id=1, source_target_pairs={{0,16},{1,17},{2,18},{3,19},{4,20},{5,21},{6,22},{7,23},{8,24},{9,... | collective-permute-start | bytes 13832 | tf_op jit(solution)/shard_map/ppermute | solution.py:404
  562.7 5.4 collective-permute-start.56
  562.7 5.4 collective-permute-start.54
  (25 other events, 484.7 us)
Sparse Core Ops, SparseCore 0:
  10.9 137.7 all-gather.4
  152.2 89.1 all-gather.6
  348.8 175.4 reduce-scatter.1

commit v4 on v3

--- a/solution.py
+++ b/solution.py
@@ -487,7 +487,7 @@
 def first_add(parts, other, received):
     side = mesh_parts()[1]
     return [
-        add_low(parts[0][second], other[0, second], *[value[second] for value in received]).astype(jnp.bfloat16)
+        add_low(parts[0, second], other[0, second], *[value[second] for value in received]).astype(jnp.bfloat16)
         for second in range(side)
     ]
 
@@ -1038,23 +1038,6 @@
         left_all[at * depth : (at + 1) * depth, :] = left[...]
 
 
-def grads_by_column_kernel(side, chips, where, *rest):
-    lefts, right_ref, other, rest = rest[: 2 * chips], rest[2 * chips], rest[2 * chips + 1], rest[2 * chips + 2 :]
-    outs, left_all = rest[:side], rest[side]
-    half = left_all.shape[0] // 2
-
-    @pl.when(pl.program_id(0) == 0)
-    def _():
-        stack_lefts(lefts, left_all)
-
-    other[0, 0] = grads_product(left_all[half:, :], right_ref[...], chips)
-    for first in range(side):
-
-        @pl.when(pl.program_id(0) // side == first)
-        def _(first=first):
-            outs[first][0] = grads_product(left_all[:half, :], right_ref[...], chips)
-
-
 def grads_joint_kernel(blocks, aligned, where, left_ref, small_left_ref, right_ref, small_right_ref, out, *scratch):
     small = scratch[0]
     wide = scratch[1].shape[1] if not aligned else right_ref.shape[1]
@@ -1109,27 +1092,23 @@
     lefts, right_ref, rest = rest[: 2 * chips], rest[2 * chips], rest[2 * chips + 1 :]
     if extra:
         extra_ref, rest = rest[0], rest[1:]
-    other, outs, left_all, both = rest[0], rest[1 : 1 + side], rest[1 + side], rest[2 + side]
+    other, mine, left_all, both = rest
     columns = side * side
     wide = right_ref.shape[1] // columns
-    narrow = both.shape[1] - wide
+    narrow = both.shape[2] - wide
     half = left_all.shape[0] // 2
     stack_lefts(lefts, left_all)
     for column in range(columns):
         by_first, by_second = relative_column(where, column, side)
-        both[:, :wide] = right_ref[:, column * wide : (column + 1) * wide]
+        right = both.at[column % 2]
+        right[:, :wide] = right_ref[:, column * wide : (column + 1) * wide]
         if extra:
-            both[:, wide:] = extra_ref[:, column * narrow : (column + 1) * narrow].astype(jnp.bfloat16)
-        other[by_second, by_first] = grads_product(left_all[half:, :], both[...], chips)
-        for first in range(side):
-
-            @pl.when(by_first == first)
-            def _(first=first, by_second=by_second):
-                outs[first][by_second] = grads_product(left_all[:half, :], both[...], chips)
-
-
-def grads_across_kernel(side, chips, where, right_ref, hidden_ref, other, *rest):
-    outs, right_t, product = rest[:side], rest[side], rest[side + 1]
+            right[:, wide:] = extra_ref[:, column * narrow : (column + 1) * narrow].astype(jnp.bfloat16)
+        other[by_second, by_first] = grads_product(left_all[half:, :], right[...], chips)
+        mine[by_first, by_second] = grads_product(left_all[:half, :], right[...], chips)
+
+
+def grads_across_kernel(side, chips, where, right_ref, hidden_ref, other, mine, right_t):
     columns = side * side
     wide = right_ref.shape[1] // columns
     depth = hidden_ref.shape[1] // 2
@@ -1138,28 +1117,17 @@
     def _():
         right_t[...] = jnp.transpose(right_ref[...])
 
-    product[...] = dot_nn(right_t[...], hidden_ref[...]).astype(jnp.bfloat16)
-    for core in range(2):
-        mine = slice(core * depth, (core + 1) * depth)
-        theirs = slice((1 - core) * depth, (2 - core) * depth)
-        for column in range(columns):
-            by_first, by_second = relative_column(where, column, side)
-            span = slice(column * wide, (column + 1) * wide)
-
-            @pl.when(where[CORE_AT] == core)
-            def _(span=span, theirs=theirs, by_first=by_first, by_second=by_second):
-                other[by_second, by_first, 0] = product[span, theirs]
-
-            for first in range(side):
-
-                @pl.when(jnp.logical_and(where[CORE_AT] == core, by_first == first))
-                def _(first=first, span=span, mine=mine, by_second=by_second):
-                    outs[first][by_second, 0] = product[span, mine]
+    low_core = where[CORE_AT] == 0
+    for column in range(columns):
+        by_first, by_second = relative_column(where, column, side)
+        product = dot_nn(right_t[column * wide : (column + 1) * wide, :], hidden_ref[...]).astype(jnp.bfloat16)
+        former, latter = product[:, :depth], product[:, depth:]
+        other[by_second, by_first, 0] = jnp.where(low_core, latter, former)
+        mine[by_first, by_second, 0] = jnp.where(low_core, former, latter)
 
 
 def piece_shapes(side, chips, piece):
-    other = shaped((side, side, chips, *piece), jnp.bfloat16)
-    return [other] + [shaped((side, chips, *piece), jnp.bfloat16)] * side
+    return [shaped((side, side, chips, *piece), jnp.bfloat16)] * 2
 
 
 def grads_across(where, hidden, right):
@@ -1177,18 +1145,16 @@
             pl.BlockSpec(right.shape, lambda at, where: (0, 0)),
             pl.BlockSpec((rows, 2 * depth), lambda at, where: (0, lax.rem(where[Z_AT] + at, chips))),
         ],
-        [pl.BlockSpec((side, side, 1, *piece), lambda at, where: (0, 0, at, 0, 0))]
-        + [pl.BlockSpec((side, 1, *piece), lambda at, where: (0, at, 0, 0))] * side,
+        [pl.BlockSpec((side, side, 1, *piece), lambda at, where: (0, 0, at, 0, 0))] * 2,
         piece_shapes(side, chips, piece),
         [
             pltpu.VMEM((right.shape[1], rows), jnp.bfloat16),
-            pltpu.VMEM((right.shape[1], 2 * depth), jnp.bfloat16),
         ],
         "grads_across",
         2 * rows * inner * right.shape[1],
         24 * 10**6,
     )
-    return found[0], found[1:]
+    return found[0], found[1]
 
 
 def weight_grads(where, left_t, right, extra=None, narrow=0):
@@ -1204,49 +1170,28 @@
 
     specs = [left_spec(sibling, far) for sibling in (False, True) for far in range(chips)]
     args = [left_t] * (2 * chips) + [right]
-    if wide % LANES == 0 and extra is None:
-        steps = columns
-        specs.append(
-            pl.BlockSpec(
-                (rows, wide), lambda at, where: (0, target_column(where, at // side, lax.rem(at, side), side))
-            )
-        )
-        joint = pl.BlockSpec((1, 1, chips, *piece), lambda at, where: (lax.rem(at, side), at // side, 0, 0, 0))
-
-        def out_spec(first):
-            return pl.BlockSpec(
-                (1, chips, *piece), lambda at, where: (jnp.clip(at - first * side, 0, side - 1), 0, 0, 0)
-            )
-
-        kernel = functools.partial(grads_by_column_kernel, side, chips)
-        scratch = [pltpu.VMEM((height, rows), jnp.bfloat16)]
-    else:
-        steps = 1
-        specs.append(pl.BlockSpec(right.shape, lambda at, where: (0, 0)))
-        if extra is not None:
-            specs.append(pl.BlockSpec(extra.shape, lambda at, where: (0, 0)))
-            args.append(extra)
-        joint = pl.BlockSpec((side, side, chips, *piece), lambda at, where: (0, 0, 0, 0, 0))
-
-        def out_spec(first):
-            return pl.BlockSpec((side, chips, *piece), lambda at, where: (0, 0, 0, 0))
-
-        kernel = functools.partial(grads_by_row_kernel, side, chips, extra is not None)
-        scratch = [pltpu.VMEM((height, rows), jnp.bfloat16), pltpu.VMEM((rows, wide + narrow), jnp.bfloat16)]
+    fixed = lambda at, where: (0, 0)
+    specs.append(pl.BlockSpec(right.shape, fixed))
+    if extra is not None:
+        specs.append(pl.BlockSpec(extra.shape, fixed))
+        args.append(extra)
+    joint = pl.BlockSpec((side, side, chips, *piece), lambda at, where: (0, 0, 0, 0, 0))
+    kernel = functools.partial(grads_by_row_kernel, side, chips, extra is not None)
+    scratch = [pltpu.VMEM((height, rows), jnp.bfloat16), pltpu.VMEM((2, rows, wide + narrow), jnp.bfloat16)]
     found = call(
         kernel,
         where,
         args,
-        (steps,),
+        (1,),
         specs,
-        [joint] + [out_spec(first) for first in range(side)],
+        [joint] * 2,
         piece_shapes(side, chips, piece),
         scratch,
         "weight_grads",
         2 * rows * height * columns * wide,
         2 * (rows * height + rows * columns * wide + height * columns * wide),
     )
-    return found[0], found[1:]
+    return found[0], found[1]
 
 
 def pick(values, at):

time: 588 us -> 587 us (level)
  Pallas kernels: 313 us -> 304 us
    pallas_call x7, Pallas kernels: 219 us -> 211 us  [call(): pl.pallas_call(kernel, grid_spec=pltpu.PrefetchScalarGridSpec(num_scalar_...]
  transfers between devices with their start and end apart: 64 -> 64, of which waited for: 24 -> 24; matrix products, arithmetic and copies ran while one was open for 9% -> 9% of each run, Pallas kernels for 54% -> 53%
where the time goes in v4:
time: 587 us; the launch traced here: 578 us
  Pallas kernels  304 us (52%)
  waiting for transfers between devices  116 us (20%)
  starting transfers between devices  76.9 us (13%)
  other arithmetic  42.8 us (7%)
  local copies, waits for them, and re-layouts  20 us (3%)
  between operations  15.8 us (3%)
    pallas_call x7, Pallas kernels, call(): pl.pallas_call(kernel, grid_spec=pltpu.PrefetchScalarGridSpec(num_scalar_...  211 us
    ppermute x61, waiting for transfers between devices, send(): return lax.ppermute(values, ('fsdp', 'dp'), pairs)  115 us
    ppermute x61, starting transfers between devices, send(): return lax.ppermute(values, ('fsdp', 'dp'), pairs)  76.4 us
    pallas_call x1, Pallas kernels, attention_backward(): pl.pallas_call(functools.partial(attention_backward_kernel, heads, head_s...  62.3 us
    pallas_call x1, Pallas kernels, attention_forward(): pl.pallas_call(functools.partial(attention_forward_kernel, heads, head_si...  30.3 us
  transfers between devices with their start and end apart: 64, of which 24 were waited for; matrix products, arithmetic and copies ran while one was open for 9% of the time, Pallas kernels for 53%

profile of v4, /device:TPU:0, one launch (start us, length us, event | category | flops | bytes accessed | tf_op | source)
XLA Modules:
  0.0 578.3 jit_solution(3448180339415393618)
XLA Ops:
  7.2 1.9 pad_maximum_fusion.2
  9.9 1.4 concatenate.35
  11.4 5.1 collective-permute-start.2
  19.4 2.0 collective-permute-start.18
  21.3 1.5 collective-permute-start.17
  22.8 2.4 collective-permute-start.19
  25.4 1.6 collective-permute-start.4
  26.9 1.5 collective-permute-start.3
  30.9 1.5 collective-permute-start.5
  32.5 2.4 collective-permute-done.5
  39.5 10.5 %collective-permute-done.18 = bf16[144,868]{1,0:T(8,128)(2,1)S(1)} collective-permute-done((bf16[144,868]{1,0:T(8,128)(2,1)S(1)}, bf16[144,868]{1,0:T(8,128)(2,1)S(1)}, u32[]{:S(2)}, u32[]{:S(2)}) %collective-permute-start.18) | collective-permute-done | bytes 250016 | tf_op jit(solution)/shard_map/ppermute | solution.py:404
  50.2 1.6 collective-permute-start.21
  52.0 1.6 collective-permute-start.20
  55.1 26.1 %collective-permute-done.21.rest_2_ = bf16[4,144,868]{2,1,0:T(8,128)(2,1)S(1)} collective-permute-done((bf16[4,144,868]{2,1,0:T(8,128)(2,1)S(1)}, bf16[4,144,868]{2,1,0:T(8,128)(2,1)S(1)}, u32[]{:S(2)}, u32[]{:S(2)}) %collective-permute-start.21) | collective-permute-done | bytes 999968 | tf_op jit(solution)/shard_map/ppermute | solution.py:404
  81.2 1.5 collective-permute-start.22
  83.4 4.9 collective-permute-start.11
  88.3 3.3 collective-permute-start.12
  91.7 2.1 collective-permute-done.11
  95.0 2.2 collective-permute-done.12
  97.2 1.7 fusion.20
  99.9 1.3 collective-permute-start.16
  102.2 4.0 collective-permute-start.23
  106.2 1.3 collective-permute-start.14
  107.5 2.2 collective-permute-start.25
  116.6 20.7 %front_forward.1 = (bf16[1024,3456]{1,0:T(8,128)(2,1)}, f32[1024,128]{1,0:T(8,128)}, bf16[1152,1024]{1,0:T(8,128)(2,1)}) custom-call(s32[5]{0:T(128)} %stack.351.where, bf16[1024,1152]{1,0:T(8,128)(2,1)} %tokens_ref.7, f32[4,8,1152]{2,1,0:T(8,128)} %pad.12.mod_ref, bf16[4,144,868]{2,1,0:T(8,128)(2,1)} %copy-done.1, ...), custom_call_target="tpu_custom_call" | custom-call | flops 163829520 | bytes 400000 | tf_op jit(solution)/shard_map/front_forward/pallas_call | solution.py:649
  139.1 30.3 %attention_forward.1 = (bf16[1024,1152]{1,0:T(8,128)(2,1)}, f32[1024,1152]{1,0:T(8,128)}, f32[1024,128]{1,0:T(8,128)}, bf16[4,16,256,256]{3,2,1,0:T(8,128)(2,1)}) custom-call(s32[1]{0:T(128)S(6)} %copy.95.flag_ref, bf16[1024,3456]{1,0:T(8,128)(2,1)} %get-tuple-element.96.proj_ref, f32[1024,128]{1,0:T(8,128)} %get-tuple-element.97.gate_ref, ...), custom_call_target="tpu_custom_call" | custom-call | flops 340000000 | bytes 400000 | tf_op jit(solution)/shard_map/attention_forward/pallas_call | solution.py:188
  169.4 39.2 %middle_forward.1 = (f32[1024,1152]{1,0:T(8,128)}, bf16[1024,4608]{1,0:T(8,128)(2,1)}, bf16[1024,4608]{1,0:T(8,128)(2,1)}, bf16[1152,1024]{1,0:T(8,128)(2,1)}, b...) custom-call(s32[5]{0:T(128)} %stack.351.where, bf16[1024,1152]{1,0:T(8,128)(2,1)} %get-tuple-element.98.conv_ref, ...), custom_call_target="tpu_custom_call" | custom-call | flops 271790912 | bytes 1200000 | tf_op jit(solution)/shard_map/middle_forward/pallas_call | solution.py:649
  208.6 19.0 %grads_across.1 = (bf16[2,2,4,288,576]{4,3,2,1,0:T(8,128)(2,1)}, bf16[2,2,4,288,576]{4,3,2,1,0:T(8,128)(2,1)}) custom-call(s32[5]{0:T(128)} %stack.351.where, bf16[1024,1152]{1,0:T(8,128)(2,1)} %get-tuple-element.100.right_ref, bf16[1024,4608]{1,0:T(8,128)(2,1)} %get-tuple-element.103.hidden_ref), custom_call_target="tpu_custom_call" | custom-call | flops 217432720 | bytes 480000 | tf_op jit(solution)/shard_map/grads_across/pallas_call | solution.py:649
  227.7 9.9 %collective-permute-done.27 = bf16[2,2,4,288,576]{4,3,2,1,0:T(8,128)(2,1)S(1)} collective-permute-done((bf16[2,2,4,288,576]{4,3,2,1,0:T(8,128)(2,1)}, bf16[2,2,4,288,576]{4,3,2,1,0:T(8,128)(2,1)S(1)}, u32[]{:S(2)}, u32[]{:S(2)}) %collective-permute-start.27) | collective-permute-done | bytes 5308448 | tf_op jit(solution)/shard_map/ppermute | solution.py:404
  237.6 6.2 %fusion = bf16[2,4,288,576]{3,2,1,0:T(8,128)(2,1)} fusion(bf16[2,2,4,288,576]{4,3,2,1,0:T(8,128)(2,1)S(1)} %collective-permute-done.27, bf16[2,2,4,288,576]{4,3,2,1,0:T(8,128)(2,1)} %get-tuple-element.114), kind=kLoop, calls=%fused_computation.2 | loop fusion | flops 5308416 | bytes 7962624 | tf_op jit(solution)/shard_map/convert_element_type | solution.py:483
  243.8 2.7 collective-permute-start.28
  246.6 68.1 %middle_backward.1 = (bf16[1024,1152]{1,0:T(8,128)(2,1)}, bf16[1024,4608]{1,0:T(8,128)(2,1)}, f32[1024,1152]{1,0:T(8,128)}, bf16[1024,1152]{1,0:T(8,128)(2,1)}, ...) custom-call(s32[5]{0:T(128)} %stack.351.where, bf16[1024,4608]{1,0:T(8,128)(2,1)} %get-tuple-element.103.hidden_ref, ...), custom_call_target="tpu_custom_call" | custom-call | flops 652298176 | bytes 1600000 | tf_op jit(solution)/shard_map/middle_backward/pallas_call | solution.py:649
  314.7 1.6 copy-done.6
  316.3 5.0 fusion.1
  322.4 25.3 %grads_joint.1 = bf16[8,4,144,1440]{3,2,1,0:T(8,128)(2,1)} custom-call(s32[5]{0:T(128)} %stack.351.where, bf16[1152,1024]{1,0:T(8,128)(2,1)} %get-tuple-element.123.left_ref, bf16[1152,1024]{1,0:T(8,128)(2,1)} %get-tuple-element.124.small_left_ref, bf16[1024,4608]{1,0:T(8,128)(2,1)} %get-tuple-element.125.right_ref, ...), custom_call_target="tpu_custom_call" | custom-call | flops 271790912 | bytes 600000 | tf_op jit(solution)/shard_map/grads_joint/pallas_call | solution.py:649
  347.7 1.4 fusion.14
  349.0 4.6 collective-permute-start.31
  353.6 1.5 collective-permute-start.32
  355.2 62.3 %attention_backward.1 = (bf16[1024,3456]{1,0:T(8,128)(2,1)}, f32[1024,128]{1,0:T(8,128)}, f32[1,128]{1,0:T(1,128)}, f32[9,1152]{1,0:T(8,128)}) custom-call(s32[1]{0:T(128)S(6)} %copy.95.flag_ref, bf16[1024,3456]{1,0:T(8,128)(2,1)} %get-tuple-element.96.proj_ref, f32[1024,128]{1,0:T(8,128)} %get-tuple-element.97.gate_ref, f32[1,128]{1,0:T(1,128)} %pad.13.bias_ref, ...), custom_call_target="tpu_custom_call" | custom-call | flops 760000000 | bytes 800000 | tf_op jit(solution)/shard_map/attention_backward/pallas_call | solution.py:346
  418.7 16.7 %weight_grads.1 = (bf16[2,2,4,144,868]{4,3,2,1,0:T(8,128)(2,1)}, bf16[2,2,4,144,868]{4,3,2,1,0:T(8,128)(2,1)}) custom-call(s32[5]{0:T(128)} %stack.351.where, bf16[1152,1024]{1,0:T(8,128)(2,1)} %get-tuple-element.117.rest_0_.rest_1_.rest_2_.rest_3_.rest_4_.rest_5_.rest_6_.rest_7_, ...), custom_call_target="tpu_custom_call" | custom-call | flops 163074544 | bytes 347996 | tf_op jit(solution)/shard_map/weight_grads/pallas_call | solution.py:649
  436.0 4.7 collective-permute-done.35
  440.7 2.1 collective-permute-done.34
  442.8 3.7 fusion.3
  447.1 22.4 %front_backward.1 = (bf16[1024,1152]{1,0:T(8,128)(2,1)}, f32[4,8,1152]{2,1,0:T(8,128)}) custom-call(s32[5]{0:T(128)} %stack.351.where, bf16[1024,3456]{1,0:T(8,128)(2,1)} %get-tuple-element.146.rest_8_.gradproj_ref, f32[1024,128]{1,0:T(8,128)} %get-tuple-element.137.rest_9_.gradgate_ref, f32[1024,1152]{1,0:T(8,128)} %get-tuple-element.147.gradafter_ref, ...), custom_call_target="tpu_custom_call" | custom-call | flops 163829520 | bytes 500000 | tf_op jit(solution)/shard_map/front_backward/pallas_call | solution.py:649
  469.5 17.9 %collective-permute-done.36 = bf16[2,4,144,868]{3,2,1,0:T(8,128)(2,1)} collective-permute-done((bf16[2,4,144,868]{3,2,1,0:T(8,128)(2,1)S(1)}, bf16[2,4,144,868]{3,2,1,0:T(8,128)(2,1)}, u32[]{:S(2)}, u32[]{:S(2)}) %collective-permute-start.36) | collective-permute-done | bytes 1999904 | tf_op jit(solution)/shard_map/ppermute | solution.py:404
  488.9 2.7 collective-permute-start.37
  491.6 1.5 collective-permute-start.39
  493.1 4.6 fusion.4
  501.4 1.3 collective-permute-done.42
  503.6 2.0 collective-permute-done.40
  507.2 2.3 add_bitcast_fusion
  509.5 6.3 %collective-permute-done.44 = bf16[4,144,868]{2,1,0:T(8,128)(2,1)S(1)} collective-permute-done((bf16[4,144,868]{2,1,0:T(8,128)(2,1)}, bf16[4,144,868]{2,1,0:T(8,128)(2,1)S(1)}, u32[]{:S(2)}, u32[]{:S(2)}) %collective-permute-start.44) | collective-permute-done | bytes 999968 | tf_op jit(solution)/shard_map/ppermute | solution.py:404
  515.8 1.7 add.1046
  517.7 2.2 fusion.17
  519.9 3.5 collective-permute-start.47
  523.3 2.4 fusion.6
  526.2 3.5 collective-permute-done.48
  529.6 13.8 %collective-permute-done.47 = bf16[144,868]{1,0:T(8,128)(2,1)S(1)} collective-permute-done((bf16[144,868]{1,0:T(8,128)(2,1)}, bf16[144,868]{1,0:T(8,128)(2,1)S(1)}, u32[]{:S(2)}, u32[]{:S(2)}) %collective-permute-start.47) | collective-permute-done | bytes 250016 | tf_op jit(solution)/shard_map/ppermute | solution.py:404
  543.4 2.4 collective-permute-start.59
  548.1 1.3 fusion.8
  551.1 2.0 collective-permute-start.50
  555.1 2.9 collective-permute-done.52
  559.3 2.2 collective-permute-start.55
  561.5 3.8 collective-permute-start.54
  (243 shorter events, 49.6 us)
Async XLA Ops:
  7.2 162.2 %all-gather.5.cloned.1.call-start = ((), (), s32[]{:S(2)}) async-start(), calls=%async_computation.2 | async-start | bytes 14598144 | tf_op jit(solution)/shard_map/all_gather | solution.py:1270
  9.1 237.4 %all-gather.7.cloned.1.call-start = ((), (), s32[]{:S(2)}) async-start(), calls=%async_computation.3 | async-start | bytes 10948608 | tf_op jit(solution)/shard_map/all_gather | solution.py:1278
  11.4 11.4 %collective-permute-start.2 = (bf16[1,4968]{1,0:T(2,128)(2,1)S(1)}, bf16[1,4968]{1,0:T(2,128)(2,1)S(1)}, u32[]{:S(2)}, u32[]{:S(2)}) collective-permute-start(bf16[1,4968]{1,0:T(2,128)(2,1)S(1)} %reshape.443), channel_id=1, source_target_pairs={{0,24},{1,25},{2,26},{3,27},{4,28},{5,29},{6,30},{7,31},{8,0},{9,1... | collective-permute-start | bytes 29816 | tf_op jit(solution)/shard_map/ppermute | solution.py:404
  16.5 8.8 %collective-permute-start.1 = (bf16[1,4968]{1,0:T(2,128)(2,1)S(1)}, bf16[1,4968]{1,0:T(2,128)(2,1)S(1)}, u32[]{:S(2)}, u32[]{:S(2)}) collective-permute-start(bf16[1,4968]{1,0:T(2,128)(2,1)S(1)} %reshape.443), channel_id=1, source_target_pairs={{0,16},{1,17},{2,18},{3,19},{4,20},{5,21},{6,22},{7,23},{8,24},{9,... | collective-permute-start | bytes 29816 | tf_op jit(solution)/shard_map/ppermute | solution.py:404
  16.5 8.8 %collective-permute-start = (bf16[1,4968]{1,0:T(2,128)(2,1)S(1)}, bf16[1,4968]{1,0:T(2,128)(2,1)S(1)}, u32[]{:S(2)}, u32[]{:S(2)}) collective-permute-start(bf16[1,4968]{1,0:T(2,128)(2,1)S(1)} %reshape.443), channel_id=1, source_target_pairs={{0,8},{1,9},{2,10},{3,11},{4,12},{5,13},{6,14},{7,15},{8,16},{9,17... | collective-permute-start | bytes 29816 | tf_op jit(solution)/shard_map/ppermute | solution.py:404
  19.4 30.7 %collective-permute-start.18 = (bf16[144,868]{1,0:T(8,128)(2,1)S(1)}, bf16[144,868]{1,0:T(8,128)(2,1)S(1)}, u32[]{:S(2)}, u32[]{:S(2)}) collective-permute-start(bf16[144,868]{1,0:T(8,128)(2,1)S(1)} %pad_maximum_fusion.3), channel_id=1, source_target_pairs={{0,16},{1,17},{2,18},{3,19},{4,20},{5,21},{6,22},{7,23},{8,24},{9,... | collective-permute-start | bytes 749960 | tf_op jit(solution)/shard_map/ppermute | solution.py:404
  21.3 28.7 %collective-permute-start.17 = (bf16[144,868]{1,0:T(8,128)(2,1)S(1)}, bf16[144,868]{1,0:T(8,128)(2,1)S(1)}, u32[]{:S(2)}, u32[]{:S(2)}) collective-permute-start(bf16[144,868]{1,0:T(8,128)(2,1)S(1)} %pad_maximum_fusion.3), channel_id=1, source_target_pairs={{0,8},{1,9},{2,10},{3,11},{4,12},{5,13},{6,14},{7,15},{8,16},{9,17... | collective-permute-start | bytes 749960 | tf_op jit(solution)/shard_map/ppermute | solution.py:404
  22.8 27.2 %collective-permute-start.19 = (bf16[144,868]{1,0:T(8,128)(2,1)S(1)}, bf16[144,868]{1,0:T(8,128)(2,1)S(1)}, u32[]{:S(2)}, u32[]{:S(2)}) collective-permute-start(bf16[144,868]{1,0:T(8,128)(2,1)S(1)} %pad_maximum_fusion.3), channel_id=1, source_target_pairs={{0,24},{1,25},{2,26},{3,27},{4,28},{5,29},{6,30},{7,31},{8,0},{9,1... | collective-permute-start | bytes 749960 | tf_op jit(solution)/shard_map/ppermute | solution.py:404
  25.4 4.4 collective-permute-start.4
  26.9 4.0 collective-permute-start.3
  29.8 5.2 collective-permute-start.6
  30.9 4.0 collective-permute-start.5
  34.9 1.9 collective-permute-start.8
  35.0 1.4 collective-permute-start.7
  36.4 1.2 collective-permute-start.9
  50.2 31.0 %collective-permute-start.21 = (bf16[4,144,868]{2,1,0:T(8,128)(2,1)S(1)}, bf16[4,144,868]{2,1,0:T(8,128)(2,1)S(1)}, u32[]{:S(2)}, u32[]{:S(2)}) collective-permute-start(bf16[4,144,868]{2,1,0:T(8,128)(2,1)S(1)} %pad_maximum_fusion.rest_0_), channel_id=1, source_target_pairs={{0,2},{1,3},{2,0},{3,1},{4,5},{5,4},{6,7},{7,6},{8,10},{9,11},{10,... | collective-permute-start | bytes 2999816 | tf_op jit(solution)/shard_map/ppermute | solution.py:404
  51.9 2.0 collective-permute-start.10
  52.0 57.7 %collective-permute-start.20 = (bf16[4,144,868]{2,1,0:T(8,128)(2,1)S(1)}, bf16[4,144,868]{2,1,0:T(8,128)(2,1)}, u32[]{:S(2)}, u32[]{:S(2)}) collective-permute-start(bf16[4,144,868]{2,1,0:T(8,128)(2,1)S(1)} %pad_maximum_fusion.rest_0_), channel_id=1, source_target_pairs={{0,1},{1,0},{2,3},{3,2},{4,6},{5,7},{6,4},{7,5},{8,9},{9,8},{10,11... | collective-permute-start | bytes 2999816 | tf_op jit(solution)/shard_map/ppermute | solution.py:404
  81.2 28.5 %collective-permute-start.22 = (bf16[4,144,868]{2,1,0:T(8,128)(2,1)S(1)}, bf16[4,144,868]{2,1,0:T(8,128)(2,1)}, u32[]{:S(2)}, u32[]{:S(2)}) collective-permute-start(bf16[4,144,868]{2,1,0:T(8,128)(2,1)S(1)} %collective-permute-done.21.rest_2_), channel_id=1, source_target_pairs={{0,1},{1,0},{2,3},{3,2},{4,6},{5,7},{6,4},{7,5},{8,9},{9,8},{10,11... | collective-permute-start | bytes 2999816 | tf_op jit(solution)/shard_map/ppermute | solution.py:404
  83.4 10.4 %collective-permute-start.11 = (f32[16,1728]{1,0:T(8,128)}, f32[16,1728]{1,0:T(8,128)}, u32[]{:S(2)}, u32[]{:S(2)}) collective-permute-start(f32[16,1728]{1,0:T(8,128)} %get-tuple-element.229), channel_id=1, source_target_pairs={{0,8},{1,9},{2,10},{3,11},{4,12},{5,13},{6,14},{7,15},{8,16},{9,17... | collective-permute-start | bytes 331784 | tf_op jit(solution)/shard_map/ppermute | solution.py:404
  88.3 6.6 %collective-permute-start.13 = (f32[16,1728]{1,0:T(8,128)}, f32[16,1728]{1,0:T(8,128)}, u32[]{:S(2)}, u32[]{:S(2)}) collective-permute-start(f32[16,1728]{1,0:T(8,128)} %get-tuple-element.230), channel_id=1, source_target_pairs={{0,24},{1,25},{2,26},{3,27},{4,28},{5,29},{6,30},{7,31},{8,0},{9,1... | collective-permute-start | bytes 331784 | tf_op jit(solution)/shard_map/ppermute | solution.py:404
  88.3 8.9 %collective-permute-start.12 = (f32[16,1728]{1,0:T(8,128)}, f32[16,1728]{1,0:T(8,128)}, u32[]{:S(2)}, u32[]{:S(2)}) collective-permute-start(f32[16,1728]{1,0:T(8,128)} %get-tuple-element.231), channel_id=1, source_target_pairs={{0,16},{1,17},{2,18},{3,19},{4,20},{5,21},{6,22},{7,23},{8,24},{9,... | collective-permute-start | bytes 331784 | tf_op jit(solution)/shard_map/ppermute | solution.py:404
  99.9 6.4 %collective-permute-start.16 = (f32[4,1728]{1,0:T(4,128)S(1)}, f32[4,1728]{1,0:T(4,128)S(1)}, u32[]{:S(2)}, u32[]{:S(2)}) collective-permute-start(f32[4,1728]{1,0:T(4,128)S(1)} %get-tuple-element.246), channel_id=1, source_target_pairs={{0,3},{1,0},{2,1},{3,2},{4,7},{5,4},{6,5},{7,6},{8,11},{9,8},{10,9... | collective-permute-start | bytes 82952 | tf_op jit(solution)/shard_map/ppermute | solution.py:404
  101.1 6.3 %collective-permute-start.15 = (f32[4,1728]{1,0:T(4,128)S(1)}, f32[4,1728]{1,0:T(4,128)S(1)}, u32[]{:S(2)}, u32[]{:S(2)}) collective-permute-start(f32[4,1728]{1,0:T(4,128)S(1)} %get-tuple-element.247), channel_id=1, source_target_pairs={{0,2},{1,3},{2,0},{3,1},{4,6},{5,7},{6,4},{7,5},{8,10},{9,11},{10,... | collective-permute-start | bytes 82952 | tf_op jit(solution)/shard_map/ppermute | solution.py:404
  102.2 14.3 %collective-permute-start.23 = (bf16[4,144,868]{2,1,0:T(8,128)(2,1)S(1)}, bf16[4,144,868]{2,1,0:T(8,128)(2,1)}, u32[]{:S(2)}, u32[]{:S(2)}) collective-permute-start(bf16[4,144,868]{2,1,0:T(8,128)(2,1)S(1)} %pad_maximum_fusion.rest_0_), channel_id=1, source_target_pairs={{0,4},{1,5},{2,6},{3,7},{4,0},{5,1},{6,2},{7,3},{8,12},{9,13},{10,... | collective-permute-start | bytes 2999816 | tf_op jit(solution)/shard_map/ppermute | solution.py:404
  106.2 8.6 %collective-permute-start.14 = (f32[4,1728]{1,0:T(4,128)S(1)}, f32[4,1728]{1,0:T(4,128)}, u32[]{:S(2)}, u32[]{:S(2)}) collective-permute-start(f32[4,1728]{1,0:T(4,128)S(1)} %get-tuple-element.248), channel_id=1, source_target_pairs={{0,1},{1,2},{2,3},{3,0},{4,5},{5,6},{6,7},{7,4},{8,9},{9,10},{10,1... | collective-permute-start | bytes 82952 | tf_op jit(solution)/shard_map/ppermute | solution.py:404
  107.5 9.1 %collective-permute-start.25 = (bf16[4,144,868]{2,1,0:T(8,128)(2,1)S(1)}, bf16[4,144,868]{2,1,0:T(8,128)(2,1)}, u32[]{:S(2)}, u32[]{:S(2)}) collective-permute-start(bf16[4,144,868]{2,1,0:T(8,128)(2,1)S(1)} %collective-permute-done.21.rest_2_), channel_id=1, source_target_pairs={{0,4},{1,5},{2,6},{3,7},{4,0},{5,1},{6,2},{7,3},{8,12},{9,13},{10,... | collective-permute-start | bytes 2999816 | tf_op jit(solution)/shard_map/ppermute | solution.py:404
  109.7 6.9 %collective-permute-start.24 = (bf16[4,144,868]{2,1,0:T(8,128)(2,1)}, bf16[4,144,868]{2,1,0:T(8,128)(2,1)}, u32[]{:S(2)}, u32[]{:S(2)}) collective-permute-start(bf16[4,144,868]{2,1,0:T(8,128)(2,1)} %collective-permute-done.20.rest_1_), channel_id=1, source_target_pairs={{0,4},{1,5},{2,6},{3,7},{4,0},{5,1},{6,2},{7,3},{8,12},{9,13},{10,... | collective-permute-start | bytes 2999816 | tf_op jit(solution)/shard_map/ppermute | solution.py:404
  109.7 6.8 %collective-permute-start.26 = (bf16[4,144,868]{2,1,0:T(8,128)(2,1)}, bf16[4,144,868]{2,1,0:T(8,128)(2,1)}, u32[]{:S(2)}, u32[]{:S(2)}) collective-permute-start(bf16[4,144,868]{2,1,0:T(8,128)(2,1)} %collective-permute-done.22.rest_3_), channel_id=1, source_target_pairs={{0,4},{1,5},{2,6},{3,7},{4,0},{5,1},{6,2},{7,3},{8,12},{9,13},{10,... | collective-permute-start | bytes 2999816 | tf_op jit(solution)/shard_map/ppermute | solution.py:404
  137.3 431.7 %reduce-scatter.2.cloned.1.call-start = ((), (), s32[]{:S(2)}) async-start(), calls=%async_computation.1 | async-start | bytes 14598144 | tf_op jit(solution)/shard_map/reduce_scatter | solution.py:1304
  227.6 10.0 %collective-permute-start.27 = (bf16[2,2,4,288,576]{4,3,2,1,0:T(8,128)(2,1)}, bf16[2,2,4,288,576]{4,3,2,1,0:T(8,128)(2,1)S(1)}, u32[]{:S(2)}, u32[]{:S(2)}) collective-permute-start(bf16[2,2,4,288,576]{4,3,2,1,0:T(8,128)(2,1)} %get-tuple-element.102), channel_id=1, source_target_pairs={{0,4},{1,5},{2,6},{3,7},{4,0},{5,1},{6,2},{7,3},{8,12},{9,13},{10,... | collective-permute-start | bytes 15925256 | tf_op jit(solution)/shard_map/ppermute | solution.py:404
  243.8 70.9 %collective-permute-start.28 = (bf16[2,4,288,576]{3,2,1,0:T(8,128)(2,1)}, bf16[2,4,288,576]{3,2,1,0:T(8,128)(2,1)S(1)}, u32[]{:S(2)}, u32[]{:S(2)}) collective-permute-start(bf16[2,4,288,576]{3,2,1,0:T(8,128)(2,1)} %fusion), channel_id=1, source_target_pairs={{0,2},{1,3},{2,0},{3,1},{4,5},{5,4},{6,7},{7,6},{8,10},{9,11},{10,... | collective-permute-start | bytes 7962632 | tf_op jit(solution)/shard_map/ppermute | solution.py:404
  321.2 26.4 %collective-permute-start.29 = (bf16[4,288,576]{2,1,0:T(8,128)(2,1)}, bf16[4,288,576]{2,1,0:T(8,128)(2,1)S(1)}, u32[]{:S(2)}, u32[]{:S(2)}) collective-permute-start(bf16[4,288,576]{2,1,0:T(8,128)(2,1)} %get-tuple-element.218), channel_id=1, source_target_pairs={{0,1},{1,0},{2,3},{3,2},{4,6},{5,7},{6,4},{7,5},{8,9},{9,8},{10,11... | collective-permute-start | bytes 3981320 | tf_op jit(solution)/shard_map/ppermute | solution.py:404
  349.0 68.4 %collective-permute-start.30 = (bf16[288,576]{1,0:T(8,128)(2,1)}, bf16[288,576]{1,0:T(8,128)(2,1)S(1)}, u32[]{:S(2)}, u32[]{:S(2)}) collective-permute-start(bf16[288,576]{1,0:T(8,128)(2,1)} %get-tuple-element.133), channel_id=1, source_target_pairs={{0,8},{1,9},{2,10},{3,11},{4,12},{5,13},{6,14},{7,15},{8,16},{9,17... | collective-permute-start | bytes 995336 | tf_op jit(solution)/shard_map/ppermute | solution.py:404
  349.0 68.5 %collective-permute-start.31 = (bf16[288,576]{1,0:T(8,128)(2,1)}, bf16[288,576]{1,0:T(8,128)(2,1)S(1)}, u32[]{:S(2)}, u32[]{:S(2)}) collective-permute-start(bf16[288,576]{1,0:T(8,128)(2,1)} %get-tuple-element.134), channel_id=1, source_target_pairs={{0,16},{1,17},{2,18},{3,19},{4,20},{5,21},{6,22},{7,23},{8,24},{9,... | collective-permute-start | bytes 995336 | tf_op jit(solution)/shard_map/ppermute | solution.py:404
  353.6 63.9 %collective-permute-start.32 = (bf16[288,576]{1,0:T(8,128)(2,1)}, bf16[288,576]{1,0:T(8,128)(2,1)S(1)}, u32[]{:S(2)}, u32[]{:S(2)}) collective-permute-start(bf16[288,576]{1,0:T(8,128)(2,1)} %get-tuple-element.135), channel_id=1, source_target_pairs={{0,24},{1,25},{2,26},{3,27},{4,28},{5,29},{6,30},{7,31},{8,0},{9,1... | collective-permute-start | bytes 995336 | tf_op jit(solution)/shard_map/ppermute | solution.py:404
  418.6 16.8 %collective-permute-start.33 = (f32[14,1152]{1,0:T(8,128)S(1)}, f32[14,1152]{1,0:T(8,128)S(1)}, u32[]{:S(2)}, u32[]{:S(2)}) collective-permute-start(f32[14,1152]{1,0:T(8,128)S(1)} %fusion.21), channel_id=1, source_target_pairs={{0,1},{1,0},{2,3},{3,2},{4,5},{5,4},{6,7},{7,6},{8,9},{9,8},{10,11... | collective-permute-start | bytes 193544 | tf_op jit(solution)/shard_map/ppermute | solution.py:404
  435.4 7.3 %collective-permute-start.34 = (bf16[2,2,4,144,868]{4,3,2,1,0:T(8,128)(2,1)}, bf16[2,2,4,144,868]{4,3,2,1,0:T(8,128)(2,1)S(1)}, u32[]{:S(2)}, u32[]{:S(2)}) collective-permute-start(bf16[2,2,4,144,868]{4,3,2,1,0:T(8,128)(2,1)} %get-tuple-element.144), channel_id=1, source_target_pairs={{0,4},{1,5},{2,6},{3,7},{4,0},{5,1},{6,2},{7,3},{8,12},{9,13},{10,... | collective-permute-start | bytes 11999240 | tf_op jit(solution)/shard_map/ppermute | solution.py:404
  435.5 5.1 collective-permute-start.35
  446.5 40.9 %collective-permute-start.36 = (bf16[2,4,144,868]{3,2,1,0:T(8,128)(2,1)S(1)}, bf16[2,4,144,868]{3,2,1,0:T(8,128)(2,1)}, u32[]{:S(2)}, u32[]{:S(2)}) collective-permute-start(bf16[2,4,144,868]{3,2,1,0:T(8,128)(2,1)S(1)} %fusion.3), channel_id=1, source_target_pairs={{0,2},{1,3},{2,0},{3,1},{4,5},{5,4},{6,7},{7,6},{8,10},{9,11},{10,... | collective-permute-start | bytes 5999624 | tf_op jit(solution)/shard_map/ppermute | solution.py:404
  488.9 8.8 %collective-permute-start.37 = (bf16[4,1728]{1,0:T(4,128)(2,1)S(1)}, bf16[4,1728]{1,0:T(4,128)(2,1)S(1)}, u32[]{:S(2)}, u32[]{:S(2)}) collective-permute-start(bf16[4,1728]{1,0:T(4,128)(2,1)S(1)} %bitcast.307), channel_id=1, source_target_pairs={{0,1},{1,2},{2,3},{3,0},{4,5},{5,6},{6,7},{7,4},{8,9},{9,10},{10,1... | collective-permute-start | bytes 41480 | tf_op jit(solution)/shard_map/ppermute | solution.py:404
  491.6 6.1 %collective-permute-start.38 = (bf16[4,1728]{1,0:T(4,128)(2,1)S(1)}, bf16[4,1728]{1,0:T(4,128)(2,1)S(1)}, u32[]{:S(2)}, u32[]{:S(2)}) collective-permute-start(bf16[4,1728]{1,0:T(4,128)(2,1)S(1)} %bitcast.306), channel_id=1, source_target_pairs={{0,2},{1,3},{2,0},{3,1},{4,6},{5,7},{6,4},{7,5},{8,10},{9,11},{10,... | collective-permute-start | bytes 41480 | tf_op jit(solution)/shard_map/ppermute | solution.py:404
  491.6 6.1 %collective-permute-start.39 = (bf16[4,1728]{1,0:T(4,128)(2,1)S(1)}, bf16[4,1728]{1,0:T(4,128)(2,1)S(1)}, u32[]{:S(2)}, u32[]{:S(2)}) collective-permute-start(bf16[4,1728]{1,0:T(4,128)(2,1)S(1)} %bitcast.305), channel_id=1, source_target_pairs={{0,3},{1,0},{2,1},{3,2},{4,7},{5,4},{6,5},{7,6},{8,11},{9,8},{10,9... | collective-permute-start | bytes 41480 | tf_op jit(solution)/shard_map/ppermute | solution.py:404
  497.7 18.1 %collective-permute-start.44 = (bf16[4,144,868]{2,1,0:T(8,128)(2,1)}, bf16[4,144,868]{2,1,0:T(8,128)(2,1)S(1)}, u32[]{:S(2)}, u32[]{:S(2)}) collective-permute-start(bf16[4,144,868]{2,1,0:T(8,128)(2,1)} %get-tuple-element.159), channel_id=1, source_target_pairs={{0,1},{1,0},{2,3},{3,2},{4,6},{5,7},{6,4},{7,5},{8,9},{9,8},{10,11... | collective-permute-start | bytes 2999816 | tf_op jit(solution)/shard_map/ppermute | solution.py:404
  498.4 4.2 collective-permute-start.42
  498.4 5.1 collective-permute-start.41
  499.5 6.1 %collective-permute-start.40 = (bf16[16,1728]{1,0:T(8,128)(2,1)S(1)}, bf16[16,1728]{1,0:T(8,128)(2,1)S(1)}, u32[]{:S(2)}, u32[]{:S(2)}) collective-permute-start(bf16[16,1728]{1,0:T(8,128)(2,1)S(1)} %reshape.451), channel_id=1, source_target_pairs={{0,8},{1,9},{2,10},{3,11},{4,12},{5,13},{6,14},{7,15},{8,16},{9,17... | collective-permute-start | bytes 165896 | tf_op jit(solution)/shard_map/ppermute | solution.py:404
  501.3 8.1 %collective-permute-start.45 = (f32[14,1152]{1,0:T(8,128)}, f32[14,1152]{1,0:T(8,128)}, u32[]{:S(2)}, u32[]{:S(2)}) collective-permute-start(f32[14,1152]{1,0:T(8,128)} %add.1042), channel_id=1, source_target_pairs={{0,4},{1,5},{2,6},{3,7},{4,0},{5,1},{6,2},{7,3},{8,12},{9,13},{10,... | collective-permute-start | bytes 193544 | tf_op jit(solution)/shard_map/ppermute | solution.py:404
  507.1 2.4 collective-permute-start.43
  517.5 8.7 %collective-permute-start.49 = (f32[14,1152]{1,0:T(8,128)}, f32[14,1152]{1,0:T(8,128)}, u32[]{:S(2)}, u32[]{:S(2)}) collective-permute-start(f32[14,1152]{1,0:T(8,128)} %add.1046), channel_id=1, source_target_pairs={{0,8},{1,9},{2,10},{3,11},{4,12},{5,13},{6,14},{7,15},{8,0},{9,1},... | collective-permute-start | bytes 193544 | tf_op jit(solution)/shard_map/ppermute | solution.py:404
  519.9 9.8 %collective-permute-start.48 = (bf16[144,868]{1,0:T(8,128)(2,1)}, bf16[144,868]{1,0:T(8,128)(2,1)S(1)}, u32[]{:S(2)}, u32[]{:S(2)}) collective-permute-start(bf16[144,868]{1,0:T(8,128)(2,1)} %get-tuple-element.226), channel_id=1, source_target_pairs={{0,24},{1,25},{2,26},{3,27},{4,28},{5,29},{6,30},{7,31},{8,0},{9,1... | collective-permute-start | bytes 749960 | tf_op jit(solution)/shard_map/ppermute | solution.py:404
  519.9 23.5 %collective-permute-start.47 = (bf16[144,868]{1,0:T(8,128)(2,1)}, bf16[144,868]{1,0:T(8,128)(2,1)S(1)}, u32[]{:S(2)}, u32[]{:S(2)}) collective-permute-start(bf16[144,868]{1,0:T(8,128)(2,1)} %get-tuple-element.227), channel_id=1, source_target_pairs={{0,16},{1,17},{2,18},{3,19},{4,20},{5,21},{6,22},{7,23},{8,24},{9,... | collective-permute-start | bytes 749960 | tf_op jit(solution)/shard_map/ppermute | solution.py:404
  523.3 20.1 %collective-permute-start.46 = (bf16[144,868]{1,0:T(8,128)(2,1)}, bf16[144,868]{1,0:T(8,128)(2,1)}, u32[]{:S(2)}, u32[]{:S(2)}) collective-permute-start(bf16[144,868]{1,0:T(8,128)(2,1)} %get-tuple-element.228), channel_id=1, source_target_pairs={{0,8},{1,9},{2,10},{3,11},{4,12},{5,13},{6,14},{7,15},{8,16},{9,17... | collective-permute-start | bytes 749960 | tf_op jit(solution)/shard_map/ppermute | solution.py:404
  543.4 9.7 %collective-permute-start.59 = (f32[1,1728]{1,0:T(1,128)S(1)}, f32[1,1728]{1,0:T(1,128)S(1)}, u32[]{:S(2)}, u32[]{:S(2)}) collective-permute-start(f32[1,1728]{1,0:T(1,128)S(1)} %broadcast_in_dim.40), channel_id=1, source_target_pairs={{0,3},{1,0},{2,1},{3,2},{4,7},{5,4},{6,5},{7,6},{8,11},{9,8},{10,9... | collective-permute-start | bytes 20744 | tf_op jit(solution)/shard_map/ppermute | solution.py:404
  545.8 7.3 %collective-permute-start.58 = (f32[1,1728]{1,0:T(1,128)S(1)}, f32[1,1728]{1,0:T(1,128)S(1)}, u32[]{:S(2)}, u32[]{:S(2)}) collective-permute-start(f32[1,1728]{1,0:T(1,128)S(1)} %broadcast_in_dim.40), channel_id=1, source_target_pairs={{0,2},{1,3},{2,0},{3,1},{4,6},{5,7},{6,4},{7,5},{8,10},{9,11},{10,... | collective-permute-start | bytes 20744 | tf_op jit(solution)/shard_map/ppermute | solution.py:404
  546.3 8.1 %collective-permute-start.57 = (f32[1,1728]{1,0:T(1,128)S(1)}, f32[1,1728]{1,0:T(1,128)S(1)}, u32[]{:S(2)}, u32[]{:S(2)}) collective-permute-start(f32[1,1728]{1,0:T(1,128)S(1)} %broadcast_in_dim.40), channel_id=1, source_target_pairs={{0,1},{1,2},{2,3},{3,0},{4,5},{5,6},{6,7},{7,4},{8,9},{9,10},{10,1... | collective-permute-start | bytes 20744 | tf_op jit(solution)/shard_map/ppermute | solution.py:404
  550.1 17.6 %collective-permute-start.60 = (f32[14,1152]{1,0:T(8,128)S(1)}, f32[14,1152]{1,0:T(8,128)S(1)}, u32[]{:S(2)}, u32[]{:S(2)}) collective-permute-start(f32[14,1152]{1,0:T(8,128)S(1)} %add.1076), channel_id=1, source_target_pairs={{0,16},{1,17},{2,18},{3,19},{4,20},{5,21},{6,22},{7,23},{8,24},{9,... | collective-permute-start | bytes 193544 | tf_op jit(solution)/shard_map/ppermute | solution.py:404
  551.1 4.0 collective-permute-start.50
  553.1 4.8 collective-permute-start.52
  553.2 4.7 collective-permute-start.51
  558.0 1.2 collective-permute-start.53
  559.3 6.7 %collective-permute-start.55 = (f32[2,4,144]{2,1,0:T(4,128)S(1)}, f32[2,4,144]{2,1,0:T(4,128)S(1)}, u32[]{:S(2)}, u32[]{:S(2)}) collective-permute-start(f32[2,4,144]{2,1,0:T(4,128)S(1)} %bitcast.310), channel_id=1, source_target_pairs={{0,16},{1,17},{2,18},{3,19},{4,20},{5,21},{6,22},{7,23},{8,24},{9,... | collective-permute-start | bytes 13832 | tf_op jit(solution)/shard_map/ppermute | solution.py:404
  561.5 5.4 collective-permute-start.56
  561.5 5.4 collective-permute-start.54
  (26 other events, 524.6 us)
Sparse Core Ops, SparseCore 0:
  11.5 137.2 all-gather.4
  151.6 88.7 all-gather.6
  347.8 176.3 reduce-scatter.1
